TPU v7x, 128 devices: a whole 4x4x4 slice. The times are simulated.
128 devices in a mesh: dp: 8 (over y, core), tm: 16 (over z, x).
Axes of the slice: x: 4, y: 4, z: 4, core: 2. Of those that a mesh axis runs over, the one named last changes fastest.
Arguments:
- grad_out: float32 [8, 16384, 512], P('dp', 'tm'), may hold values from -6 to 6
- input_spectrum: float32 [2, 8, 2, 16, 1024, 512], P(None, 'dp', None, 'tm'), may hold values from -6 to 6
- filter_spectrum: float32 [2, 2, 16, 1024, 512], P(None, None, 'tm'), may hold values from -6 to 6
- skip_gain: float32 [512], replicated, may hold values from 0.5 to 2
Outputs:
- grad_in: float32 [8, 16384, 512], P('dp', 'tm')
- grad_filter: float32 [2, 2, 16, 1024, 512], P(None, None, 'tm', 'dp')
All inputs are finite; a program needn't handle non-finite values.
Results may differ from a plain program's by a relative error of at most 0.0001.
Values sent between devices are 32-bit elements; how exact they have to be, the bound alone decides.
No kernel may reach another device: no remote copies, remote signals or barrier semaphores. Data moves between devices by JAX's collectives and lax.ppermute only.
A program may use at most 192 MiB of HBM per device.

v0:
```python
import math

import jax
import jax.numpy as jnp
from jax import lax
from jax.sharding import PartitionSpec as P


def angles(counts, period):
    radians = 2.0 * math.pi / period * counts.astype(jnp.float32)
    return (jnp.cos(radians), jnp.sin(radians))


def complex_dft(real_part, imag_part, cos_table, sin_table, form, inverse):
    highest = lax.Precision.HIGHEST
    real_cos = jnp.einsum(form, real_part, cos_table, precision=highest)
    real_sin = jnp.einsum(form, real_part, sin_table, precision=highest)
    imag_cos = jnp.einsum(form, imag_part, cos_table, precision=highest)
    imag_sin = jnp.einsum(form, imag_part, sin_table, precision=highest)
    if inverse:
        return (real_cos - imag_sin, imag_cos + real_sin)
    return (real_cos + imag_sin, imag_cos - real_sin)


def long_dft(real_part, imag_part, inverse):
    count, pairs, length, channels = real_part.shape
    outer = min(length, 128)
    inner = length // outer
    real_part = real_part.reshape(count, pairs, outer, inner, channels)
    imag_part = imag_part.reshape(count, pairs, outer, inner, channels)
    outer_idx = jnp.arange(outer, dtype=jnp.int32)
    inner_idx = jnp.arange(inner, dtype=jnp.int32)
    cos_outer, sin_outer = angles(outer_idx[:, None] * outer_idx[None, :] % outer, outer)
    real_part, imag_part = complex_dft(
        real_part, imag_part, cos_outer, sin_outer, "nrabc,ak->nrkbc", inverse
    )
    cos_mid, sin_mid = angles(outer_idx[:, None] * inner_idx[None, :] % length, length)
    cos_mid = cos_mid[:, :, None]
    sin_mid = sin_mid[:, :, None]
    if inverse:
        real_next = real_part * cos_mid - imag_part * sin_mid
        imag_next = imag_part * cos_mid + real_part * sin_mid
    else:
        real_next = real_part * cos_mid + imag_part * sin_mid
        imag_next = imag_part * cos_mid - real_part * sin_mid
    cos_inner, sin_inner = angles(inner_idx[:, None] * inner_idx[None, :] % inner, inner)
    real_next, imag_next = complex_dft(
        real_next, imag_next, cos_inner, sin_inner, "nrkbc,bj->nrjkc", inverse
    )
    return (
        real_next.reshape(count, pairs, length, channels),
        imag_next.reshape(count, pairs, length, channels),
    )


def apply_twist(values, position, points):
    cosine, sines = angles(position[..., None], points)
    return (values, values * cosine, -(values * sines))


def fold_parities(real_part, imag_part, position, points):
    cosine, sines = angles(position[..., None], points)
    return real_part[:, 0] + (real_part[:, 1] * cosine - imag_part[:, 1] * sines)


def on_device(grad_out, input_spectrum, filter_spectrum, skip_gain):
    shards = lax.axis_size("tm")
    column = lax.axis_index("tm")
    streams, length, channels = grad_out.shape
    sliver = length // shards
    sequence = length * shards
    points = 2 * sequence
    factor = 1.0 / math.sqrt(points)
    across = jnp.arange(shards, dtype=jnp.int32)
    within = jnp.arange(length, dtype=jnp.int32)
    inside = jnp.arange(sliver, dtype=jnp.int32)
    cos_shards, sin_shards = angles(across[:, None] * across[None, :] % shards, shards)
    blocks = grad_out.reshape(streams, shards, sliver, channels)
    anchor = column * length + within.reshape(shards, sliver)
    parity_even, odd_real, odd_imag = apply_twist(blocks, anchor, points)
    stacked = jnp.stack([parity_even, odd_real, odd_imag], 1)
    arrived = lax.all_to_all(stacked, "tm", split_axis=2, concat_axis=2, tiled=True)
    parity_even, odd_real, odd_imag = (arrived[:, 0], arrived[:, 1], arrived[:, 2])
    real_stack = jnp.stack([parity_even, odd_real], 1)
    imag_stack = jnp.stack([jnp.zeros_like(parity_even), odd_imag], 1)
    real_stack, imag_stack = complex_dft(
        real_stack, imag_stack, cos_shards, sin_shards, "nrpsc,pa->nrasc", False
    )
    global_step = column * sliver + inside
    cos_turn, sin_turn = angles(across[:, None] * global_step[None, :] % sequence, sequence)
    cos_turn = cos_turn[:, :, None]
    sin_turn = sin_turn[:, :, None]
    turned_real = real_stack * cos_turn + imag_stack * sin_turn
    turned_imag = imag_stack * cos_turn - real_stack * sin_turn
    halves = (
        lax.all_to_all(turned_real, "tm", split_axis=2, concat_axis=3, tiled=True),
        lax.all_to_all(turned_imag, "tm", split_axis=2, concat_axis=3, tiled=True),
    )
    real_in = halves[0][:, :, 0]
    imag_in = halves[1][:, :, 0]
    out_real, out_imag = long_dft(real_in, imag_in, False)
    spec_real = out_real * factor
    spec_imag = out_imag * factor
    saved_real = input_spectrum[0][:, :, 0]
    saved_imag = input_spectrum[1][:, :, 0]
    term_real = jnp.sum(saved_real * spec_real + saved_imag * spec_imag, 0)
    term_imag = jnp.sum(saved_real * spec_imag - saved_imag * spec_real, 0)
    partial_terms = jnp.stack([term_real, term_imag])[:, :, None]
    grad_filter = lax.psum_scatter(partial_terms, "dp", scatter_dimension=3, tiled=True)
    filt_real = filter_spectrum[0][:, 0]
    filt_imag = filter_spectrum[1][:, 0]
    back_real = filt_real * spec_real + filt_imag * spec_imag
    back_imag = filt_real * spec_imag - filt_imag * spec_real
    back_real, back_imag = long_dft(back_real, back_imag, True)
    cos_back, sin_back = angles((within * column % sequence)[:, None], sequence)
    untwist_real = back_real * cos_back - back_imag * sin_back
    untwist_imag = back_imag * cos_back + back_real * sin_back
    untwist_real = untwist_real.reshape(streams, 2, shards, sliver, channels)
    untwist_imag = untwist_imag.reshape(streams, 2, shards, sliver, channels)
    halves = (
        lax.all_to_all(untwist_real, "tm", split_axis=2, concat_axis=2, tiled=True),
        lax.all_to_all(untwist_imag, "tm", split_axis=2, concat_axis=2, tiled=True),
    )
    out_real, out_imag = complex_dft(
        halves[0], halves[1], cos_shards, sin_shards, "nrasc,ap->nrpsc", True
    )
    rows_real = out_real * factor
    rows_imag = out_imag * factor
    landed = (
        lax.all_to_all(rows_real, "tm", split_axis=2, concat_axis=3, tiled=True),
        lax.all_to_all(rows_imag, "tm", split_axis=2, concat_axis=3, tiled=True),
    )
    position = column * length + within
    result = fold_parities(landed[0][:, :, 0], landed[1][:, :, 0], position, points)
    grad_in = result + skip_gain * grad_out
    return (grad_in, grad_filter)


def solution(mesh):
    return jax.shard_map(
        on_device,
        mesh=mesh,
        in_specs=(
            P("dp", "tm", None),
            P(None, "dp", None, "tm", None, None),
            P(None, None, "tm", None, None),
            P(),
        ),
        out_specs=(P("dp", "tm", None), P(None, None, "tm", "dp", None)),
        check_vma=False,
    )
```

profile of v0, /device:TPU:0, one launch (start us, length us, event | category | flops | bytes accessed | tf_op | source)
XLA Modules:
  0.0 678.3 jit_solution(16902546212390578453)
XLA Ops:
  13.8 8.5 %all-to-all-start = ((f32[1,3,16,64,512]{4,3,1,0,2:T(8,128)}), f32[1,3,16,64,512]{4,3,1,0,2:T(8,128)}, u32[]{:S(2)}, u32[]{:S(2)}) async-start(f32[1,3,16,64,512]{4,3,1,0,2:T(8,128)} %copy.100), calls=%async_computation | async-start | bytes 12582912 | tf_op jit(solution)/shard_map/all_to_all | solution.py:82
  22.5 92.5 %all-to-all-done = f32[1,3,16,64,512]{4,3,1,0,2:T(8,128)} async-done(((f32[1,3,16,64,512]{4,3,1,0,2:T(8,128)}), f32[1,3,16,64,512]{4,3,1,0,2:T(8,128)}, u32[]{:S(2)}, u32[]{:S(2)}) %all-to-all-start) | async-done | bytes 6291488 | tf_op jit(solution)/shard_map/all_to_all | solution.py:82
  126.4 6.1 fusion.88
  132.5 7.7 %fusion.21 = (f32[1,2,16,64,512]{4,2,3,1,0:T(8,128)}, f32[1,2,16,64,512]{4,2,3,1,0:T(8,128)S(1)}) fusion(f32[16,2,64,512]{3,0,2,1:T(8,128)S(1)} %fusion.88, f32[16,64]{0,1:T(8,128)S(1)} %copy.104, f32[16,64]{0,1:T(8,128)S(1)} %copy.103, f32[16,2,64,512]{3,0,2,1:T(8,128)S(1)} %fusion.24, f32[1,2,16,64,512]{4,3,1,0,2:T(8,128)S(1)} %stack.20), kind=kOutput, calls=%fused_computation.42 | convolution fusion | flops 208670208 | bytes 20979712 | tf_op jit(solution)/shard_map/nrpsc,pa->nrasc/dot_general | solution.py:17
  150.3 6.6 copy.105
  156.9 53.5 %all-to-all-done.2 = f32[1,2,16,64,512]{4,3,1,0,2:T(8,128)} async-done(((f32[1,2,16,64,512]{4,3,1,0,2:T(8,128)}), f32[1,2,16,64,512]{4,3,1,0,2:T(8,128)}, u32[]{:S(2)}, u32[]{:S(2)}) %all-to-all-start.2) | async-done | bytes 4194336 | tf_op jit(solution)/shard_map/all_to_all | solution.py:97
  217.9 7.2 %fusion.62 = f32[128,2,8,512]{3,0,2,1:T(8,128)} fusion(f32[2,128,8,512]{3,2,1,0:T(8,128)S(1)} %bitcast.275), kind=kOutput, calls=%fused_computation.95 | convolution fusion | flops 1610842112 | bytes 8388608 | tf_op jit(solution)/shard_map/nrabc,ak->nrkbc/dot_general | solution.py:19
  225.1 7.5 %fusion.60 = f32[128,2,8,512]{3,0,2,1:T(8,128)} fusion(f32[2,128,8,512]{3,2,1,0:T(8,128)S(1)} %bitcast.276), kind=kOutput, calls=%fused_computation.93 | convolution fusion | flops 1610842112 | bytes 8388608 | tf_op jit(solution)/shard_map/nrabc,ak->nrkbc/dot_general | solution.py:18
  232.6 39.5 %all-to-all-done.1 = f32[1,2,16,64,512]{4,3,1,0,2:T(8,128)} async-done(((f32[1,2,16,64,512]{4,3,1,0,2:T(8,128)}), f32[1,2,16,64,512]{4,3,1,0,2:T(8,128)}, u32[]{:S(2)}, u32[]{:S(2)}) %all-to-all-start.1) | async-done | bytes 4194336 | tf_op jit(solution)/shard_map/all_to_all | solution.py:96
  275.6 6.3 fusion.72
  282.0 7.5 %fusion.17 = (f32[2,128,8,512]{3,1,2,0:T(8,128)S(1)}, f32[2,128,8,512]{3,1,2,0:T(8,128)S(1)}) fusion(f32[128,2,8,512]{3,0,2,1:T(8,128)S(1)} %fusion.72, f32[128,8]{0,1:T(8,128)S(1)} %get-tuple-element.30, f32[128,8]{0,1:T(8,128)S(1)} %get-tuple-element.31, f32[128,2,8,512]{3,0,2,1:T(8,128)S(1)} %copy-done.7, f32[2,128,8,512]{3,2,1,0:T(8,128)S(1)} %bitcast.274), kind=kOutput, calls=%fused_computation.34 | convolution fusion | flops 1618182144 | bytes 20979712 | tf_op jit(solution)/shard_map/nrabc,ak->nrkbc/dot_general | solution.py:17
  295.3 6.5 fusion.52
  301.8 6.1 multiply_bitcast_fusion.3
  310.4 6.7 multiply_bitcast_fusion.2
  322.8 6.2 fusion.46
  329.0 6.6 fusion.44
  335.7 6.3 fusion.78
  341.9 8.4 %fusion.11 = (f32[2,128,8,512]{3,1,2,0:T(8,128)}, f32[2,128,8,512]{3,1,2,0:T(8,128)S(1)}) fusion(f32[128,2,8,512]{3,0,2,1:T(8,128)S(1)} %fusion.78, f32[128,8]{0,1:T(8,128)S(1)} %get-tuple-element.30, f32[128,8]{0,1:T(8,128)S(1)} %get-tuple-element.31, f32[128,2,8,512]{3,0,2,1:T(8,128)S(1)} %fusion.44, f32[2,128,8,512]{3,2,1,0:T(8,128)S(1)} %get-tuple-element.10), kind=kOutput, calls=%fused_computation.22 | convolution fusion | flops 1618182144 | bytes 20979712 | tf_op jit(solution)/shard_map/nrabc,ak->nrkbc/dot_general | solution.py:17
  350.3 6.6 fusion.38
  356.9 6.7 fusion.36
  363.5 9.9 %fusion = (f32[1,2,1024,512]{3,2,1,0:T(8,128)}, f32[1,2,1024,512]{3,2,1,0:T(8,128)}) fusion(f32[1,2,8,128,512]{4,3,2,1,0:T(8,128)} %copy-done.1, f32[1,2,8,128,512]{4,3,2,1,0:T(8,128)S(1)} %copy.115, f32[2,1,2,1,1024,512]{5,4,2,3,1,0:T(8,128)} %bitcast.287), kind=kLoop, calls=%fused_computation.7 | loop fusion | flops 6291456 | bytes 25165824 | tf_op jit(solution)/shard_map/add | solution.py:106
  373.5 7.7 %maximum_bitcast_fusion = f32[2,2,1,1024,512]{4,3,1,0,2:T(8,128)} fusion(f32[1,2,1024,512]{3,2,1,0:T(8,128)} %get-tuple-element.9, f32[1,2,1024,512]{3,2,1,0:T(8,128)} %get-tuple-element.8), kind=kLoop, calls=%fused_computation | loop fusion | flops 2097152 | bytes 16777216 | tf_op jit(solution)/shard_map/broadcast_in_dim | solution.py:108
  381.2 9.2 %subtract_bitcast_fusion = f32[1,2,8,128,512]{4,2,3,1,0:T(8,128)S(1)} fusion(f32[8,2,128,512]{3,0,2,1:T(8,128)} %fusion.38, f32[2,128,8,512]{3,1,2,0:T(8,128)} %get-tuple-element.16), kind=kOutput, calls=%fused_computation.60 | convolution fusion | flops 101712768 | bytes 12582912 | tf_op jit(solution)/shard_map/nrkbc,bj->nrjkc/dot_general | solution.py:16
  393.9 6.0 add_bitcast_fusion
  417.1 50.8 %all-to-all-done.4 = f32[1,2,16,64,512]{4,3,1,0,2:T(8,128)} async-done(((f32[1,2,16,64,512]{4,3,1,0,2:T(8,128)}), f32[1,2,16,64,512]{4,3,1,0,2:T(8,128)}, u32[]{:S(2)}, u32[]{:S(2)}) %all-to-all-start.4) | async-done | bytes 4194336 | tf_op jit(solution)/shard_map/all_to_all | solution.py:122
  472.9 9.7 %fusion.4 = f32[16,2,64,512]{3,0,2,1:T(8,128)} fusion(f32[1,2,16,64,512]{4,3,1,0,2:T(8,128)} %all-to-all-done.4), kind=kOutput, calls=%fused_computation.13 | convolution fusion | flops 201330176 | bytes 8388608 | tf_op jit(solution)/shard_map/nrasc,ap->nrpsc/dot_general | solution.py:19
  482.6 47.2 %all-to-all-done.3 = f32[1,2,16,64,512]{4,3,1,0,2:T(8,128)} async-done(((f32[1,2,16,64,512]{4,3,1,0,2:T(8,128)}), f32[1,2,16,64,512]{4,3,1,0,2:T(8,128)}, u32[]{:S(2)}, u32[]{:S(2)}) %all-to-all-start.3) | async-done | bytes 4194336 | tf_op jit(solution)/shard_map/all_to_all | solution.py:121
  529.8 9.2 %multiply_bitcast_fusion.1 = f32[1,2,16,64,512]{4,2,3,1,0:T(8,128)S(1)} fusion(f32[16,2,64,512]{3,0,2,1:T(8,128)} %fusion.4, f32[1,2,16,64,512]{4,3,1,0,2:T(8,128)} %all-to-all-done.3), kind=kOutput, calls=%fused_computation.56 | convolution fusion | flops 203427328 | bytes 12582912 | tf_op jit(solution)/shard_map/nrasc,ap->nrpsc/dot_general | solution.py:16
  548.1 8.0 %fusion.2 = f32[16,2,64,512]{3,0,2,1:T(8,128)S(1)} fusion(f32[1,2,16,64,512]{4,3,1,0,2:T(8,128)} %all-to-all-done.4), kind=kOutput, calls=%fused_computation.11 | convolution fusion | flops 201330176 | bytes 8388608 | tf_op jit(solution)/shard_map/nrasc,ap->nrpsc/dot_general | solution.py:18
  556.2 8.4 %multiply_bitcast_fusion = f32[1,2,16,64,512]{4,2,3,1,0:T(8,128)S(1)} fusion(f32[16,2,64,512]{3,0,2,1:T(8,128)S(1)} %fusion.2, f32[1,2,16,64,512]{4,3,1,0,2:T(8,128)} %all-to-all-done.3), kind=kOutput, calls=%fused_computation.55 | convolution fusion | flops 203427328 | bytes 12582912 | tf_op jit(solution)/shard_map/nrasc,ap->nrpsc/dot_general | solution.py:17
  569.1 33.8 %all-to-all-done.5 = f32[1,2,16,64,512]{4,3,1,0,2:T(8,128)} async-done(((f32[1,2,16,64,512]{4,3,1,0,2:T(8,128)}), f32[1,2,16,64,512]{4,3,1,0,2:T(8,128)}, u32[]{:S(2)}, u32[]{:S(2)}) %all-to-all-start.5) | async-done | bytes 4194336 | tf_op jit(solution)/shard_map/all_to_all | solution.py:130
  612.4 53.5 %all-to-all-done.6 = f32[1,2,16,64,512]{4,3,1,0,2:T(8,128)} async-done(((f32[1,2,16,64,512]{4,3,1,0,2:T(8,128)}), f32[1,2,16,64,512]{4,3,1,0,2:T(8,128)}, u32[]{:S(2)}, u32[]{:S(2)}) %all-to-all-start.6) | async-done | bytes 4194336 | tf_op jit(solution)/shard_map/all_to_all | solution.py:131
  (65 shorter events, 107.3 us)
Async XLA Ops:
  7.2 2.2 copy-start.2
  13.8 101.2 %all-to-all-start = ((f32[1,3,16,64,512]{4,3,1,0,2:T(8,128)}), f32[1,3,16,64,512]{4,3,1,0,2:T(8,128)}, u32[]{:S(2)}, u32[]{:S(2)}) async-start(f32[1,3,16,64,512]{4,3,1,0,2:T(8,128)} %copy.100), calls=%async_computation | async-start | bytes 12582912 | tf_op jit(solution)/shard_map/all_to_all | solution.py:82
  144.6 65.9 %all-to-all-start.2 = ((f32[1,2,16,64,512]{4,3,1,0,2:T(8,128)}), f32[1,2,16,64,512]{4,3,1,0,2:T(8,128)}, u32[]{:S(2)}, u32[]{:S(2)}) async-start(f32[1,2,16,64,512]{4,3,1,0,2:T(8,128)} %copy.108), calls=%async_computation.2 | async-start | bytes 8388608 | tf_op jit(solution)/shard_map/all_to_all | solution.py:97
  210.4 61.7 %all-to-all-start.1 = ((f32[1,2,16,64,512]{4,3,1,0,2:T(8,128)}), f32[1,2,16,64,512]{4,3,1,0,2:T(8,128)}, u32[]{:S(2)}, u32[]{:S(2)}) async-start(f32[1,2,16,64,512]{4,3,1,0,2:T(8,128)} %copy.105), calls=%async_computation.1 | async-start | bytes 8388608 | tf_op jit(solution)/shard_map/all_to_all | solution.py:96
  215.0 456.3 %reduce-scatter.2.cloned.1.call-start = ((), (), s32[]{:S(2)}) async-start(), calls=%async_computation.8 | async-start | bytes 9437184 | tf_op jit(solution)/shard_map/reduce_scatter | solution.py:109
  272.2 3.4 copy-start.5
  275.6 6.3 copy-start.7
  307.9 11.6 %slice-start = ((s8[8388608]{0:T(1024)(128)(4,1)}), s8[4194304]{0:T(1024)(128)(4,1)S(1)}, s32[]{:S(2)}) async-start(s8[8388608]{0:T(1024)(128)(4,1)} %bitcast.285), calls=%async_computation.9 | async-start | bytes 8388608
  310.4 9.1 %slice-start.1 = ((s8[8388608]{0:T(1024)(128)(4,1)}), s8[4194304]{0:T(1024)(128)(4,1)S(1)}, s32[]{:S(2)}) async-start(s8[8388608]{0:T(1024)(128)(4,1)} %bitcast.285), calls=%async_computation.10 | async-start | bytes 8388608
  319.5 3.3 copy-start.1
  390.4 2.5 copy-start
  390.4 3.5 copy-start.4
  407.5 60.3 %all-to-all-start.4 = ((f32[1,2,16,64,512]{4,3,1,0,2:T(8,128)}), f32[1,2,16,64,512]{4,3,1,0,2:T(8,128)}, u32[]{:S(2)}, u32[]{:S(2)}) async-start(f32[1,2,16,64,512]{4,3,1,0,2:T(8,128)} %copy.131), calls=%async_computation.4 | async-start | bytes 8388608 | tf_op jit(solution)/shard_map/all_to_all | solution.py:122
  467.8 61.9 %all-to-all-start.3 = ((f32[1,2,16,64,512]{4,3,1,0,2:T(8,128)}), f32[1,2,16,64,512]{4,3,1,0,2:T(8,128)}, u32[]{:S(2)}, u32[]{:S(2)}) async-start(f32[1,2,16,64,512]{4,3,1,0,2:T(8,128)} %copy.129), calls=%async_computation.3 | async-start | bytes 8388608 | tf_op jit(solution)/shard_map/all_to_all | solution.py:121
  543.6 59.2 %all-to-all-start.5 = ((f32[1,2,16,64,512]{4,3,1,0,2:T(8,128)}), f32[1,2,16,64,512]{4,3,1,0,2:T(8,128)}, u32[]{:S(2)}, u32[]{:S(2)}) async-start(f32[1,2,16,64,512]{4,3,1,0,2:T(8,128)} %copy.133), calls=%async_computation.5 | async-start | bytes 8388608 | tf_op jit(solution)/shard_map/all_to_all | solution.py:130
  602.8 63.1 %all-to-all-start.6 = ((f32[1,2,16,64,512]{4,3,1,0,2:T(8,128)}), f32[1,2,16,64,512]{4,3,1,0,2:T(8,128)}, u32[]{:S(2)}, u32[]{:S(2)}) async-start(f32[1,2,16,64,512]{4,3,1,0,2:T(8,128)} %copy.135), calls=%async_computation.6 | async-start | bytes 8388608 | tf_op jit(solution)/shard_map/all_to_all | solution.py:131
  612.4 56.4 %copy-start.3 = (f32[1,1024,512]{2,1,0:T(8,128)S(1)}, f32[1,1024,512]{2,1,0:T(8,128)}, u32[]{:S(2)}) copy-start(f32[1,1024,512]{2,1,0:T(8,128)} %param.4) | copy-start | bytes 6291460
  612.4 56.4 %copy-start.8 = (f32[512]{0:T(512)S(1)}, f32[512]{0:T(512)}, u32[]{:S(2)}) copy-start(f32[512]{0:T(512)} %param.7) | copy-start | bytes 6148
  665.9 3.4 copy-start.6
Sparse Core Ops, SparseCore 0:
  381.3 51.1 reduce-scatter.1
where the time goes:
time: 681 us; the launch traced here: 678 us
  waiting for transfers between devices  371 us (54%)
  matrix products  164 us (24%)
  local copies, waits for them, and re-layouts  63.2 us (9%)
  starting transfers between devices  37.5 us (6%)
  other arithmetic  27.9 us (4%)
  between operations  14.7 us (2%)
    all_to_all x1, waiting for transfers between devices, on_device(): lax.all_to_all(stacked, 'tm', split_axis=2, concat_axis=2, tiled=True)  92.5 us
    all_to_all x1, waiting for transfers between devices, on_device(): lax.all_to_all(turned_imag, 'tm', split_axis=2, concat_axis=3, tiled=True)  53.5 us
    all_to_all x1, waiting for transfers between devices, on_device(): lax.all_to_all(rows_imag, 'tm', split_axis=2, concat_axis=3, tiled=True)  53.5 us
    all_to_all x1, waiting for transfers between devices, on_device(): lax.all_to_all(untwist_imag, 'tm', split_axis=2, concat_axis=2, tiled=True)  50.8 us
    all_to_all x1, waiting for transfers between devices, on_device(): lax.all_to_all(untwist_real, 'tm', split_axis=2, concat_axis=2, tiled=True)  47.2 us
    dot_general x6, matrix products, complex_dft(): real_sin = jnp.einsum(form, real_part, sin_table, precision=highest)  44.7 us
    dot_general x6, matrix products, complex_dft(): real_cos = jnp.einsum(form, real_part, cos_table, precision=highest)  43.1 us
    all_to_all x1, waiting for transfers between devices, on_device(): lax.all_to_all(turned_real, 'tm', split_axis=2, concat_axis=3, tiled=True)  39.5 us
  transfers between devices with their start and end apart: 8, of which 7 were waited for; matrix products, arithmetic and copies ran while one was open for 16% of the time, Pallas kernels for 0%

commit v1 on v0

v1 whole, which is shorter than its diff:
```python
import functools
import math

import jax
import jax.numpy as jnp
from jax import lax
from jax.experimental import pallas as pl
from jax.experimental.pallas import tpu as pltpu
from jax.sharding import PartitionSpec as P

LANES = 128
SHARDS = 16
RADIX = 4


def weighted(pairs):
    total = None
    for coefficient, value in pairs:
        if abs(coefficient) < 1e-12:
            continue
        if total is None:
            if abs(coefficient - 1.0) < 1e-12:
                total = value
            else:
                total = value * coefficient
        elif abs(coefficient - 1.0) < 1e-12:
            total = total + value
        elif abs(coefficient + 1.0) < 1e-12:
            total = total - value
        else:
            total = total + value * coefficient
    return total


def cos_at(numerator, denominator):
    return math.cos(2.0 * math.pi * (numerator % denominator) / denominator)


def sin_at(numerator, denominator):
    return math.sin(2.0 * math.pi * (numerator % denominator) / denominator)


def residues_of(x):
    total = {n: x[n] + x[16 - n] for n in range(1, 8)}
    diff = {n: x[n] - x[16 - n] for n in range(1, 8)}
    out = {}
    evens, odds = (2, 4, 6), (1, 3, 5, 7)
    for a in range(0, 5):
        even_re = weighted([(1.0, x[0]), (cos_at(8 * a, 16), x[8])] + [(cos_at(n * a, 16), total[n]) for n in evens])
        odd_re = weighted([(cos_at(n * a, 16), total[n]) for n in odds])
        even_im = weighted([(sin_at(n * a, 16), diff[n]) for n in evens])
        odd_im = weighted([(sin_at(n * a, 16), diff[n]) for n in odds])
        if a == 4:
            out[2 * a] = (even_re, -odd_im)
            continue
        re_low, re_high = even_re + odd_re, even_re - odd_re
        if a == 0:
            out[0], out[16] = (re_low, None), (re_high, None)
        else:
            out[2 * a] = (re_low, -(even_im + odd_im))
            out[16 - 2 * a] = (re_high, even_im - odd_im)
    for rho in (1, 3, 5, 7):
        even_re = weighted([(1.0, x[0])] + [(cos_at(n * rho, 32), diff[n]) for n in evens])
        odd_re = weighted([(cos_at(n * rho, 32), diff[n]) for n in odds])
        even_im = weighted([(sin_at(8 * rho, 32), x[8])] + [(sin_at(n * rho, 32), total[n]) for n in evens])
        odd_im = weighted([(sin_at(n * rho, 32), total[n]) for n in odds])
        out[rho] = (even_re + odd_re, -(even_im + odd_im))
        out[16 - rho] = (even_re - odd_re, even_im - odd_im)
    return out


def expand_kernel(x_ref, out_ref):
    groups = x_ref.shape[1] // RADIX // 8

    def step(index, carry):
        t, group = index // groups, index % groups
        row = pl.ds(pl.multiple_of(group * 8, 8), 8)
        values = [x_ref[n, pl.ds(group * 8 * RADIX + t, 8, stride=RADIX), :] for n in range(SHARDS)]
        found = residues_of(values)
        zero = jnp.zeros_like(values[0])
        for a in range(SHARDS):
            even, odd = 2 * a, 2 * a + 1
            if even <= 16:
                re, im = found[even]
                if a == 0:
                    im = found[16][0]
                elif a == 8:
                    im = zero
            else:
                re, im = found[32 - even]
                im = -im
            out_ref[a, 0, t, row, :] = re
            out_ref[a, 1, t, row, :] = im
            if odd <= 16:
                re, im = found[odd]
            else:
                re, im = found[32 - odd]
                im = -im
            out_ref[a, 2, t, row, :] = re
            out_ref[a, 3, t, row, :] = im
        return carry

    lax.fori_loop(0, RADIX * groups, step, 0)


def times_of(v0, v16, even, odd):
    out = [None] * 16
    ce, se, co, so = {}, {}, {}, {}
    for n in range(0, 5):
        c_even = weighted([(1.0, v0), (1.0 if n % 2 == 0 else -1.0, v16)] + [(cos_at(n * d, 16), even[d][0]) for d in (2, 4, 6)])
        c_odd = weighted([(cos_at(n * d, 16), even[d][0]) for d in (1, 3, 5, 7)])
        s_even = weighted([(sin_at(n * d, 16), even[d][1]) for d in (2, 4, 6)])
        s_odd = weighted([(sin_at(n * d, 16), even[d][1]) for d in (1, 3, 5, 7)])
        if n == 4:
            ce[4], se[4] = c_even, s_odd
        elif n == 0:
            ce[0], ce[8] = c_even + c_odd, c_even - c_odd
        else:
            ce[n], ce[8 - n] = c_even + c_odd, c_even - c_odd
            se[n], se[8 - n] = s_odd + s_even, s_odd - s_even
    re_sum = {q: odd[q][0] + odd[16 - q][0] for q in (1, 3, 5, 7)}
    re_diff = {q: odd[q][0] - odd[16 - q][0] for q in (1, 3, 5, 7)}
    im_sum = {q: odd[q][1] + odd[16 - q][1] for q in (1, 3, 5, 7)}
    im_diff = {q: odd[q][1] - odd[16 - q][1] for q in (1, 3, 5, 7)}
    for n in range(0, 9):
        re_of, im_of = (re_sum, im_diff) if n % 2 == 0 else (re_diff, im_sum)
        co[n] = weighted([(cos_at(n * q, 32), re_of[q]) for q in (1, 3, 5, 7)])
        so[n] = weighted([(sin_at(n * q, 32), im_of[q]) for q in (1, 3, 5, 7)])
    out[0] = ce[0] + co[0]
    out[8] = ce[8] + so[8]
    for n in range(1, 8):
        out[n] = (ce[n] - se[n]) + (co[n] + so[n])
        out[16 - n] = (ce[n] + se[n]) + (so[n] - co[n])
    return out


def combine_kernel(u_ref, x_ref, gain_ref, out_ref):
    groups = x_ref.shape[1] // RADIX // 8

    def step(index, carry):
        t, group = index // groups, index % groups
        row = pl.ds(pl.multiple_of(group * 8, 8), 8)
        even = {d: (u_ref[d, 0, t, row, :], u_ref[d, 1, t, row, :]) for d in range(1, 8)}
        odd = {31 - 2 * d: (u_ref[d, 0, t, row, :], u_ref[d, 1, t, row, :]) for d in range(8, 16)}
        times = times_of(u_ref[0, 0, t, row, :], u_ref[0, 1, t, row, :], even, odd)
        gain = gain_ref[0:1, :]
        rows = pl.ds(group * 8 * RADIX + t, 8, stride=RADIX)
        for n in range(SHARDS):
            out_ref[n, rows, :] = times[n] + gain * x_ref[n, rows, :]
        return carry

    lax.fori_loop(0, RADIX * groups, step, 0)


def halves_of(values):
    high = values.astype(jnp.bfloat16)
    low = (values - high.astype(jnp.float32)).astype(jnp.bfloat16)
    return high, low


def product(table_ref, where, values):
    high, low = halves_of(values)
    table_high = table_ref[where + (0,)]
    table_low = table_ref[where + (1,)]
    dot = functools.partial(jnp.dot, preferred_element_type=jnp.float32)
    return dot(table_high, high) + (dot(table_high, low) + dot(table_low, high))


def spectrum_kernel(pick_ref, z_ref, saved_ref, filt_ref, mirror_ref, fwd_ref, inv_ref, fwd16_ref, inv16_ref, term_ref, u_ref, s_ref, h_ref):
    pick = pick_ref[0]
    first = pick_ref[1]
    keep = (1 - first).astype(jnp.float32)
    inner = fwd_ref.shape[-1]
    lanes = z_ref.shape[-1]

    def turn(parts, sign):
        (r0, i0), (r1, i1), (r2, i2), (r3, i3) = parts
        ar, ai, br, bi = r0 + r2, i0 + i2, r0 - r2, i0 - i2
        cr, ci, dr, di = r1 + r3, i1 + i3, r1 - r3, i1 - i3
        if sign < 0:
            dr, di = -dr, -di
        return (ar + cr, ai + ci), (br + di, bi - dr), (ar - cr, ai - ci), (br - di, bi + dr)

    for r in range(2):
        for t in range(RADIX):
            re = z_ref[:, 2 * r, t].reshape(inner, lanes)
            im = z_ref[:, 2 * r + 1, t].reshape(inner, lanes)
            if r == 0:
                im = im * keep
            both = product(fwd_ref, (r, t), jnp.concatenate([re, im], 1))
            s_ref[r, t, 0] = both[:inner, :lanes] + both[inner:, lanes:]
            s_ref[r, t, 1] = both[:inner, lanes:] - both[inner:, :lanes]

        def rows_step(index, carry):
            row = pl.ds(pl.multiple_of(index * 8, 8), 8)
            parts = [(s_ref[r, t, 0, row], s_ref[r, t, 1, row]) for t in range(RADIX)]
            for q, (re, im) in enumerate(turn(parts, 1)):
                s_ref[r, q, 0, row] = re
                s_ref[r, q, 1, row] = im
                at = pl.ds(pl.multiple_of(q * inner + index * 8, 8), 8)
                a, b = saved_ref[0, r, at], saved_ref[1, r, at]
                term_ref[0, r, at] = a * re + b * im
                term_ref[1, r, at] = a * im - b * re
            return carry

        lax.fori_loop(0, inner // 8, rows_step, 0, unroll=2)

    def back_step(index, carry):
        row = pl.ds(pl.multiple_of(index * 8, 8), 8)
        parts = []
        for q in range(RADIX):
            at = pl.ds(pl.multiple_of(q * inner + index * 8, 8), 8)
            a = filt_ref[0, at] + keep * mirror_ref[0, at]
            b = keep * mirror_ref[1, at] - filt_ref[1, at]
            re, im = s_ref[pick, q, 0, row], s_ref[pick, q, 1, row]
            parts.append((a * re - b * im, a * im + b * re))
        for t, (re, im) in enumerate(turn(parts, -1)):
            h_ref[t, 0, row] = re
            h_ref[t, 1, row] = im
        return carry

    lax.fori_loop(0, inner // 8, back_step, 0, unroll=2)
    slivers = u_ref.shape[0]
    for t in range(RADIX):
        both = product(inv_ref, (t,), jnp.concatenate([h_ref[t, 0], h_ref[t, 1]], 1))
        u_ref[:, 0, t] = (both[:inner, :lanes] - both[inner:, lanes:]).reshape(slivers, inner // slivers, lanes)
        u_ref[:, 1, t] = (both[inner:, :lanes] + both[:inner, lanes:]).reshape(slivers, inner // slivers, lanes)

    @pl.when(first == 1)
    def _():
        for t in range(RADIX):
            both = product(fwd16_ref, (t,), z_ref[:, 1, t].reshape(inner, lanes))
            s_ref[1, t, 0] = both[:inner]
            s_ref[1, t, 1] = -both[inner:]

        def step16(index, carry):
            row = pl.ds(pl.multiple_of(index * 8, 8), 8)
            parts = []
            for q, (re, im) in enumerate(turn([(s_ref[1, t, 0, row], s_ref[1, t, 1, row]) for t in range(RADIX)], 1)):
                at = pl.ds(pl.multiple_of(q * inner + index * 8, 8), 8)
                a, b = mirror_ref[0, at], mirror_ref[1, at]
                parts.append((a * re + b * im, a * im - b * re))
            for t, (re, im) in enumerate(turn(parts, -1)):
                h_ref[t, 0, row] = re
                h_ref[t, 1, row] = im
            return carry

        lax.fori_loop(0, inner // 8, step16, 0)
        for t in range(RADIX):
            both = product(inv16_ref, (t,), jnp.concatenate([h_ref[t, 0], h_ref[t, 1]], 1))
            u_ref[:, 1, t] = (both[:inner, :lanes] - both[inner:, lanes:]).reshape(slivers, inner // slivers, lanes)


def split_table(values):
    high = lax.reduce_precision(values, 8, 7)
    return jnp.stack([high, values - high], -3).astype(jnp.bfloat16)


def make_tables(residues, inner, points, factor, transposed):
    shape = (RADIX, inner, inner)
    t = lax.broadcasted_iota(jnp.int32, shape, 0)
    time = t + RADIX * lax.broadcasted_iota(jnp.int32, shape, 1 if transposed else 2)
    step = 2 * SHARDS * lax.broadcasted_iota(jnp.int32, shape, 2 if transposed else 1)
    tables = []
    for residue in residues:
        phase = (time * (residue + step)) % points
        angle = phase.astype(jnp.float32) * (2.0 * math.pi / points)
        tables.append(split_table(jnp.concatenate([jnp.cos(angle) * factor, jnp.sin(angle) * factor], 1)))
    return jnp.stack(tables)


def on_device(grad_out, input_spectrum, filter_spectrum, skip_gain, interpret=False):
    column = lax.axis_index("tm")
    stream = lax.axis_index("dp")
    groups = lax.axis_size("dp")
    _, length, channels = grad_out.shape
    sliver = length // SHARDS
    inner = length // RADIX
    points = 2 * length * SHARDS
    factor = 1.0 / math.sqrt(points)
    params = functools.partial(pltpu.CompilerParams, vmem_limit_bytes=56 * 1024 * 1024)
    f32 = jnp.float32

    pick = (column >= 8).astype(jnp.int32)
    first = (column == 0).astype(jnp.int32)
    picks = jnp.stack([pick, first])

    mine = filter_spectrum[:, :, 0]
    part = length // groups
    give = lax.dynamic_index_in_dim(mine, (column < 8).astype(jnp.int32), 1, False)
    turned = lax.rev(lax.dynamic_slice_in_dim(give, (groups - 1 - stream) * part, part, 1), (1,))
    plain = lax.dynamic_slice_in_dim(give, stream * part, part, 1)
    sent = jnp.where(column == 8, plain, turned)
    swap = [(a, 15 - a) for a in range(8)] + [(8, 0)] + [(a, 16 - a) for a in range(9, 16)]
    mirror = lax.all_gather(lax.ppermute(sent, "tm", swap), "dp", axis=1, tiled=True)

    raw = lax.all_to_all(grad_out.reshape(SHARDS, sliver, channels), "tm", 0, 0, tiled=True)

    forward = make_tables([2 * column, 2 * column + 1], inner, points, factor, False)
    inverse = make_tables([2 * column + pick], inner, points, factor, True)[0]
    forward16 = make_tables([16], inner, points, factor, False)[0]
    inverse16 = make_tables([16], inner, points, factor, True)[0]

    rows = sliver // RADIX
    expanded = pl.pallas_call(
        expand_kernel,
        grid=(channels // LANES,),
        in_specs=[pl.BlockSpec((SHARDS, sliver, LANES), lambda c: (0, 0, c))],
        out_specs=pl.BlockSpec((SHARDS, 4, RADIX, rows, LANES), lambda c: (0, 0, 0, 0, c)),
        out_shape=jax.ShapeDtypeStruct((SHARDS, 4, RADIX, rows, channels), f32),
        compiler_params=params(),
        cost_estimate=pl.CostEstimate(flops=300 * length * channels // 16, bytes_accessed=5 * length * channels * 4, transcendentals=0),
        interpret=interpret,
        name="expand",
    )(raw)
    arrived = lax.all_to_all(expanded, "tm", 0, 0, tiled=True)

    def fixed(shape):
        return pl.BlockSpec(shape, lambda c, s: (0,) * len(shape), pipeline_mode=pl.Buffered(1))

    terms, inverted = pl.pallas_call(
        spectrum_kernel,
        grid_spec=pltpu.PrefetchScalarGridSpec(
            num_scalar_prefetch=1,
            grid=(channels // LANES,),
            in_specs=[
                pl.BlockSpec((SHARDS, 4, RADIX, rows, LANES), lambda c, s: (0, 0, 0, 0, c)),
                pl.BlockSpec((2, None, 2, None, length, LANES), lambda c, s: (0, 0, 0, 0, 0, c)),
                pl.BlockSpec((2, None, None, length, LANES), lambda c, s: (0, s[0], 0, 0, c)),
                pl.BlockSpec((2, length, LANES), lambda c, s: (0, 0, c)),
                fixed(forward.shape),
                fixed(inverse.shape),
                fixed(forward16.shape),
                fixed(inverse16.shape),
            ],
            out_specs=[
                pl.BlockSpec((2, 2, None, length, LANES), lambda c, s: (0, 0, 0, 0, c)),
                pl.BlockSpec((SHARDS, 2, RADIX, rows, LANES), lambda c, s: (0, 0, 0, 0, c)),
            ],
            scratch_shapes=[
                pltpu.VMEM((2, RADIX, 2, inner, LANES), f32),
                pltpu.VMEM((RADIX, 2, inner, LANES), f32),
            ],
        ),
        out_shape=[
            jax.ShapeDtypeStruct((2, 2, 1, length, channels), f32),
            jax.ShapeDtypeStruct((SHARDS, 2, RADIX, rows, channels), f32),
        ],
        compiler_params=params(),
        cost_estimate=pl.CostEstimate(flops=10**10, bytes_accessed=20 * length * channels * 4, transcendentals=0),
        interpret=interpret,
        name="spectrum",
    )(picks, arrived, input_spectrum, filter_spectrum, mirror, forward, inverse, forward16, inverse16)

    grad_filter = lax.psum_scatter(terms, "dp", scatter_dimension=3, tiled=True)
    landed = lax.all_to_all(inverted, "tm", 0, 0, tiled=True)
    combined = pl.pallas_call(
        combine_kernel,
        grid=(channels // LANES,),
        in_specs=[
            pl.BlockSpec((SHARDS, 2, RADIX, rows, LANES), lambda c: (0, 0, 0, 0, c)),
            pl.BlockSpec((SHARDS, sliver, LANES), lambda c: (0, 0, c)),
            pl.BlockSpec((1, LANES), lambda c: (0, c)),
        ],
        out_specs=pl.BlockSpec((SHARDS, sliver, LANES), lambda c: (0, 0, c)),
        out_shape=jax.ShapeDtypeStruct((SHARDS, sliver, channels), f32),
        compiler_params=params(),
        cost_estimate=pl.CostEstimate(flops=400 * length * channels // 16, bytes_accessed=4 * length * channels * 4, transcendentals=0),
        interpret=interpret,
        name="combine",
    )(landed, raw, skip_gain[None])
    back = lax.all_to_all(combined, "tm", 0, 0, tiled=True)
    return (back.reshape(1, length, channels), grad_filter)


def solution(mesh, interpret=False):
    return jax.shard_map(
        functools.partial(on_device, interpret=interpret),
        mesh=mesh,
        in_specs=(
            P("dp", "tm", None),
            P(None, "dp", None, "tm", None, None),
            P(None, None, "tm", None, None),
            P(),
        ),
        out_specs=(P("dp", "tm", None), P(None, None, "tm", "dp", None)),
        check_vma=False,
    )
```

time: 681 us -> 323 us (0.47)
  waiting for transfers between devices: 371 us -> 115 us
  matrix products: 164 us -> 0 us
  blocking collectives: 0 us -> 85.4 us
  local copies, waits for them, and re-layouts: 63.2 us -> 10 us
  Pallas kernels: 0 us -> 46.5 us
  starting transfers between devices: 37.5 us -> 24 us
    all_to_all x7 -> x2, waiting for transfers between devices: 371 us -> 111 us  [the longest x1 85.6 us: on_device(): arrived = lax.all_to_all(expanded, 'tm', 0, 0, tiled=True)]
    dot_general x24 -> x0, matrix products: 164 us -> none  [the longest x6 44.7 us: complex_dft(): real_sin = jnp.einsum(form, real_part, sin_table, precision=highest)]
    all_to_all x0 -> x2, blocking collectives: none -> 85.4 us  [the longest x1 55.4 us: on_device(): landed = lax.all_to_all(inverted, 'tm', 0, 0, tiled=True)]
    pallas_call x0 -> x3, Pallas kernels: none -> 46.5 us  [the longest x1 35.1 us: on_device(): pl.pallas_call(spectrum_kernel, grid_spec=pltpu.PrefetchScalarGridSpec(nu...]
    concatenate x0 -> x1, other arithmetic: none -> 21.2 us  [make_tables(): jnp.concatenate([jnp.cos(angle) * factor, jnp.sin(angle) * factor], 1)]
    all_to_all x7 -> x2, starting transfers between devices: 37.5 us -> 18.6 us  [the longest x1 10.7 us: on_device(): arrived = lax.all_to_all(expanded, 'tm', 0, 0, tiled=True)]
    add x4, other arithmetic: 14.2 us -> 0.02 us  [make_tables(): phase = time * (residue + step) % points]
    mul x4 -> x0, local copies, waits for them, and re-layouts: 13.9 us -> none  [the longest x1 4.63 us: on_device(): rows_real = out_real * factor]
  transfers between devices with their start and end apart: 8 -> 5, of which waited for: 7 -> 3; matrix products, arithmetic and copies ran while one was open for 16% -> 10% of each run, Pallas kernels for 0% -> 4%
where the time goes in v1:
time: 323 us
  waiting for transfers between devices  115 us (36%)
  blocking collectives  85.4 us (26%)
  Pallas kernels  46.5 us (14%)
  other arithmetic  27.2 us (8%)
  starting transfers between devices  24 us (7%)
  between operations  14.2 us (4%)
  local copies, waits for them, and re-layouts  10 us (3%)
    all_to_all x1, waiting for transfers between devices, on_device(): arrived = lax.all_to_all(expanded, 'tm', 0, 0, tiled=True)  85.6 us
    all_to_all x1, blocking collectives, on_device(): landed = lax.all_to_all(inverted, 'tm', 0, 0, tiled=True)  55.4 us
    pallas_call x1, Pallas kernels, on_device(): pl.pallas_call(spectrum_kernel, grid_spec=pltpu.PrefetchScalarGridSpec(nu...  35.1 us
    all_to_all x1, blocking collectives, on_device(): back = lax.all_to_all(combined, 'tm', 0, 0, tiled=True)  30 us
    all_to_all x1, waiting for transfers between devices, on_device(): lax.all_to_all(grad_out.reshape(SHARDS, sliver, channels), 'tm', 0, 0, ti...  24.9 us
    concatenate x1, other arithmetic, make_tables(): jnp.concatenate([jnp.cos(angle) * factor, jnp.sin(angle) * factor], 1)  21.2 us
    all_to_all x1, starting transfers between devices, on_device(): arrived = lax.all_to_all(expanded, 'tm', 0, 0, tiled=True)  10.7 us
    all_to_all x1, starting transfers between devices, on_device(): lax.all_to_all(grad_out.reshape(SHARDS, sliver, channels), 'tm', 0, 0, ti...  7.97 us
  transfers between devices with their start and end apart: 5, of which 3 were waited for; matrix products, arithmetic and copies ran while one was open for 10% of the time, Pallas kernels for 4%

profile of v1, /device:TPU:0, one launch (start us, length us, event | category | flops | bytes accessed | tf_op | source)
XLA Modules:
  0.0 322.7 jit_solution(12667150848709083450)
XLA Ops:
  7.2 8.0 %all-to-all-start = ((f32[16,64,512]{2,1,0:T(8,128)}), f32[16,64,512]{2,1,0:T(8,128)S(1)}, u32[]{:S(2)}, u32[]{:S(2)}) async-start(f32[16,64,512]{2,1,0:T(8,128)} %bitcast.40), calls=%async_computation | async-start | bytes 4194304 | tf_op jit(solution)/shard_map/all_to_all | solution.py:297
  15.2 1.1 dynamic-slice_bitcast_fusion
  16.3 0.3 rev.3
  16.6 1.2 bitcast_select_fusion
  17.7 5.3 %collective-permute-start = (f32[2,128,512]{2,1,0:T(8,128)S(1)}, f32[2,128,512]{2,1,0:T(8,128)S(1)}, u32[]{:S(2)}, u32[]{:S(2)}) collective-permute-start(f32[2,128,512]{2,1,0:T(8,128)S(1)} %bitcast_select_fusion), channel_id=1, source_target_pairs={{0,15},{1,14},{2,13},{3,12},{4,11},{5,10},{6,9},{7,8},{8,0},{9,7},... | collective-permute-start | bytes 1572872 | tf_op jit(solution)/shard_map/ppermute | solution.py:295
  23.0 24.9 %all-to-all-done.x_ref = f32[16,64,512]{2,1,0:T(8,128)S(1)} async-done(((f32[16,64,512]{2,1,0:T(8,128)}), f32[16,64,512]{2,1,0:T(8,128)S(1)}, u32[]{:S(2)}, u32[]{:S(2)}) %all-to-all-start) | async-done | bytes 2097184 | tf_op jit(solution)/shard_map/all_to_all | solution.py:297
  47.9 1.3 copy-done
  49.3 5.9 %expand.1 = f32[16,4,4,16,512]{4,3,2,1,0:T(8,128)} custom-call(f32[16,64,512]{2,1,0:T(8,128)} %copy-done), custom_call_target="tpu_custom_call" | custom-call | flops 9830400 | bytes 10485760 | tf_op jit(solution)/shard_map/expand/pallas_call | solution.py:305
  55.2 10.7 %all-to-all-start.1 = ((f32[16,4,4,16,512]{4,3,2,1,0:T(8,128)}), f32[16,4,4,16,512]{4,3,2,1,0:T(8,128)}, u32[]{:S(2)}, u32[]{:S(2)}) async-start(f32[16,4,4,16,512]{4,3,2,1,0:T(8,128)} %expand.1), calls=%async_computation.1 | async-start | bytes 16777216 | tf_op jit(solution)/shard_map/all_to_all | solution.py:316
  65.8 0.0 all-gather.2.cloned.1.call-start
  65.9 0.8 copy-done.1
  66.7 0.0 all-gather.2.cloned.1.call-update
  66.7 0.0 reduce-scatter.2.cloned.1.call-start
  66.8 21.2 %multiply_bitcast_fusion.1 = (f32[4,1,256,256]{3,2,1,0:T(8,128)S(1)}, f32[4,1,256,256]{3,2,0,1:T(8,128)S(1)}, f32[4,1,256,256]{3,2,1,0:T(8,128)S(1)}, f32[4,1,25...) fusion(s32[256]{0:T(256)S(1)} %fusion.24, ...), kind=kLoop, calls=%fused_computation.59 | loop fusion | flops 21495808 | bytes 10490880 | tf_op jit(solution)/shard_map/concatenate | solution.py:268
  88.0 0.8 reduce-precision_convert_fusion.1
  88.8 0.2 pad_maximum_fusion.5
  89.0 1.4 copy.9.fwd16_ref
  90.5 0.2 pad_maximum_fusion.3
  90.7 1.5 copy.8.inv_ref
  92.2 0.8 fusion.22
  93.0 0.4 maximum_maximum_fusion
  93.4 2.3 copy.7.fwd_ref
  95.7 0.6 pad_add_fusion.pick_ref
  96.3 0.3 reduce-precision_convert_fusion
  96.6 1.5 pad_maximum_fusion.7.inv16_ref
  98.1 4.7 %all-gather.2.cloned.1.call-done.mirror_ref = f32[2,1024,512]{2,1,0:T(8,128)} async-done(((f32[2,128,512]{2,1,0:T(8,128)}), f32[2,1024,512]{2,1,0:T(8,128)}) %all-gather.2.cloned.1.call-update) | async-done | bytes 4194320 | tf_op jit(solution)/shard_map/all_gather | solution.py:295
  102.8 85.6 %all-to-all-done.1.z_ref = f32[16,4,4,16,512]{4,3,2,1,0:T(8,128)} async-done(((f32[16,4,4,16,512]{4,3,2,1,0:T(8,128)}), f32[16,4,4,16,512]{4,3,2,1,0:T(8,128)}, u32[]{:S(2)}, u32[]{:S(2)}) %all-to-all-start.1) | async-done | bytes 8388640 | tf_op jit(solution)/shard_map/all_to_all | solution.py:316
  188.4 35.1 %spectrum.1 = (f32[2,2,1,1024,512]{4,3,2,1,0:T(8,128)}, f32[16,2,4,16,512]{4,3,2,1,0:T(8,128)}) custom-call(s32[2]{0:T(128)} %pad_add_fusion.pick_ref, f32[16,4,4,16,512]{4,3,2,1,0:T(8,128)} %all-to-all-done.1.z_ref, f32[2,1,2,1,1024,512]{5,4,3,2,1,0:T(8,128)} %saved_ref.1, f32[2,2,1,1024,512]{4,3,2,1,0:T(8,128)} %filt_ref.1, ...), custom_call_target="tpu_custom_call" | custom-call | flops 10000000000 | bytes 41943040 | tf_op jit(solution)/shard_map/spectrum/pallas_call | solution.py:321
  223.5 55.4 %all_to_all.20.u_ref = f32[16,2,4,16,512]{4,3,2,1,0:T(8,128)} all-to-all(f32[16,2,4,16,512]{4,3,2,1,0:T(8,128)} %get-tuple-element.4), channel_id=1, replica_groups=mesh['dp'=8,'tm'=16] {'tm'}, dimensions={0} | all-to-all | bytes 8388608 | tf_op jit(solution)/shard_map/all_to_all | solution.py:356
  278.9 5.6 %combine.1 = f32[16,64,512]{2,1,0:T(8,128)} custom-call(f32[16,2,4,16,512]{4,3,2,1,0:T(8,128)} %all_to_all.20.u_ref, f32[16,64,512]{2,1,0:T(8,128)} %copy-done, f32[1,512]{1,0:T(1,128)} %bitcast.41), custom_call_target="tpu_custom_call" | custom-call | flops 13107200 | bytes 8388608 | tf_op jit(solution)/shard_map/combine/pallas_call | solution.py:357
  284.5 30.0 %all_to_all.21 = f32[16,64,512]{2,1,0:T(8,128)S(1)} all-to-all(f32[16,64,512]{2,1,0:T(8,128)} %combine.1), channel_id=1, replica_groups=mesh['dp'=8,'tm'=16] {'tm'}, dimensions={0} | all-to-all | bytes 4194304 | tf_op jit(solution)/shard_map/all_to_all | solution.py:372
  314.5 1.3 copy.11
  (10 shorter events, 0.1 us)
Async XLA Ops:
  7.2 40.8 %all-to-all-start = ((f32[16,64,512]{2,1,0:T(8,128)}), f32[16,64,512]{2,1,0:T(8,128)S(1)}, u32[]{:S(2)}, u32[]{:S(2)}) async-start(f32[16,64,512]{2,1,0:T(8,128)} %bitcast.40), calls=%async_computation | async-start | bytes 4194304 | tf_op jit(solution)/shard_map/all_to_all | solution.py:297
  17.7 48.1 %collective-permute-start = (f32[2,128,512]{2,1,0:T(8,128)S(1)}, f32[2,128,512]{2,1,0:T(8,128)S(1)}, u32[]{:S(2)}, u32[]{:S(2)}) collective-permute-start(f32[2,128,512]{2,1,0:T(8,128)S(1)} %bitcast_select_fusion), channel_id=1, source_target_pairs={{0,15},{1,14},{2,13},{3,12},{4,11},{5,10},{6,9},{7,8},{8,0},{9,7},... | collective-permute-start | bytes 1572872 | tf_op jit(solution)/shard_map/ppermute | solution.py:295
  47.9 1.3 copy-start
  55.2 133.3 %all-to-all-start.1 = ((f32[16,4,4,16,512]{4,3,2,1,0:T(8,128)}), f32[16,4,4,16,512]{4,3,2,1,0:T(8,128)}, u32[]{:S(2)}, u32[]{:S(2)}) async-start(f32[16,4,4,16,512]{4,3,2,1,0:T(8,128)} %expand.1), calls=%async_computation.1 | async-start | bytes 16777216 | tf_op jit(solution)/shard_map/all_to_all | solution.py:316
  65.8 36.9 %all-gather.2.cloned.1.call-start = ((), (), s32[]{:S(2)}) async-start(), calls=%async_computation.5 | async-start | bytes 4718592 | tf_op jit(solution)/shard_map/all_gather | solution.py:295
  65.9 0.8 copy-start.1
  66.7 247.8 %reduce-scatter.2.cloned.1.call-start = ((), (), s32[]{:S(2)}) async-start(), calls=%async_computation.6 | async-start | bytes 9437184 | tf_op jit(solution)/shard_map/reduce_scatter | solution.py:355
Sparse Core Ops, SparseCore 0:
  68.9 33.7 all-gather.1
  223.6 48.8 reduce-scatter.1

commit v2 on v1

v2 whole, which is shorter than its diff:
```python
import functools
import math

import jax
import jax.numpy as jnp
import numpy as np
from jax import lax
from jax.experimental import pallas as pl
from jax.experimental.pallas import tpu as pltpu
from jax.sharding import PartitionSpec as P

LANES = 128
SHARDS = 16
RADIX = 4


def weighted(pairs):
    total = None
    for coefficient, value in pairs:
        if abs(coefficient) < 1e-12:
            continue
        if total is None:
            if abs(coefficient - 1.0) < 1e-12:
                total = value
            else:
                total = value * coefficient
        elif abs(coefficient - 1.0) < 1e-12:
            total = total + value
        elif abs(coefficient + 1.0) < 1e-12:
            total = total - value
        else:
            total = total + value * coefficient
    return total


def cos_at(numerator, denominator):
    return math.cos(2.0 * math.pi * (numerator % denominator) / denominator)


def sin_at(numerator, denominator):
    return math.sin(2.0 * math.pi * (numerator % denominator) / denominator)


def residues_of(x):
    total = {n: x[n] + x[16 - n] for n in range(1, 8)}
    diff = {n: x[n] - x[16 - n] for n in range(1, 8)}
    out = {}
    evens, odds = (2, 4, 6), (1, 3, 5, 7)
    for a in range(0, 5):
        even_re = weighted([(1.0, x[0]), (cos_at(8 * a, 16), x[8])] + [(cos_at(n * a, 16), total[n]) for n in evens])
        odd_re = weighted([(cos_at(n * a, 16), total[n]) for n in odds])
        even_im = weighted([(sin_at(n * a, 16), diff[n]) for n in evens])
        odd_im = weighted([(sin_at(n * a, 16), diff[n]) for n in odds])
        if a == 4:
            out[2 * a] = (even_re, -odd_im)
            continue
        re_low, re_high = even_re + odd_re, even_re - odd_re
        if a == 0:
            out[0], out[16] = (re_low, None), (re_high, None)
        else:
            out[2 * a] = (re_low, -(even_im + odd_im))
            out[16 - 2 * a] = (re_high, even_im - odd_im)
    for rho in (1, 3, 5, 7):
        even_re = weighted([(1.0, x[0])] + [(cos_at(n * rho, 32), diff[n]) for n in evens])
        odd_re = weighted([(cos_at(n * rho, 32), diff[n]) for n in odds])
        even_im = weighted([(sin_at(8 * rho, 32), x[8])] + [(sin_at(n * rho, 32), total[n]) for n in evens])
        odd_im = weighted([(sin_at(n * rho, 32), total[n]) for n in odds])
        out[rho] = (even_re + odd_re, -(even_im + odd_im))
        out[16 - rho] = (even_re - odd_re, even_im - odd_im)
    return out


def expand_kernel(x_ref, picked_ref, other_ref):
    groups = x_ref.shape[1] // RADIX // 8

    def step(index, carry):
        t, group = index // groups, index % groups
        row = pl.ds(pl.multiple_of(group * 8, 8), 8)
        values = [x_ref[n, pl.ds(group * 8 * RADIX + t, 8, stride=RADIX), :] for n in range(SHARDS)]
        found = residues_of(values)
        zero = jnp.zeros_like(values[0])
        for a in range(SHARDS):
            for rho in (2 * a, 2 * a + 1):
                if rho <= 16:
                    re, im = found[rho]
                    if rho == 0:
                        im = found[16][0]
                    elif rho == 16:
                        im = zero
                else:
                    re, im = found[32 - rho]
                    im = -im
                out_ref = picked_ref if (rho % 2 == 1) == (a >= 8) else other_ref
                out_ref[a, 0, t, row, :] = re
                out_ref[a, 1, t, row, :] = im
        return carry

    lax.fori_loop(0, RADIX * groups, step, 0)


def times_of(v0, v16, even, odd):
    out = [None] * 16
    ce, se, co, so = {}, {}, {}, {}
    for n in range(0, 5):
        c_even = weighted([(1.0, v0), (1.0 if n % 2 == 0 else -1.0, v16)] + [(cos_at(n * d, 16), even[d][0]) for d in (2, 4, 6)])
        c_odd = weighted([(cos_at(n * d, 16), even[d][0]) for d in (1, 3, 5, 7)])
        s_even = weighted([(sin_at(n * d, 16), even[d][1]) for d in (2, 4, 6)])
        s_odd = weighted([(sin_at(n * d, 16), even[d][1]) for d in (1, 3, 5, 7)])
        if n == 4:
            ce[4], se[4] = c_even, s_odd
        elif n == 0:
            ce[0], ce[8] = c_even + c_odd, c_even - c_odd
        else:
            ce[n], ce[8 - n] = c_even + c_odd, c_even - c_odd
            se[n], se[8 - n] = s_odd + s_even, s_odd - s_even
    re_sum = {q: odd[q][0] + odd[16 - q][0] for q in (1, 3, 5, 7)}
    re_diff = {q: odd[q][0] - odd[16 - q][0] for q in (1, 3, 5, 7)}
    im_sum = {q: odd[q][1] + odd[16 - q][1] for q in (1, 3, 5, 7)}
    im_diff = {q: odd[q][1] - odd[16 - q][1] for q in (1, 3, 5, 7)}
    for n in range(0, 9):
        re_of, im_of = (re_sum, im_diff) if n % 2 == 0 else (re_diff, im_sum)
        co[n] = weighted([(cos_at(n * q, 32), re_of[q]) for q in (1, 3, 5, 7)])
        so[n] = weighted([(sin_at(n * q, 32), im_of[q]) for q in (1, 3, 5, 7)])
    out[0] = ce[0] + co[0]
    out[8] = ce[8] + so[8]
    for n in range(1, 8):
        out[n] = (ce[n] - se[n]) + (co[n] + so[n])
        out[16 - n] = (ce[n] + se[n]) + (so[n] - co[n])
    return out


def combine_kernel(u_ref, out_ref):
    groups = out_ref.shape[1] // RADIX // 8

    def step(index, carry):
        t, group = index // groups, index % groups
        row = pl.ds(pl.multiple_of(group * 8, 8), 8)
        even = {d: (u_ref[d, 0, t, row, :], u_ref[d, 1, t, row, :]) for d in range(1, 8)}
        odd = {31 - 2 * d: (u_ref[d, 0, t, row, :], u_ref[d, 1, t, row, :]) for d in range(8, 16)}
        times = times_of(u_ref[0, 0, t, row, :], u_ref[0, 1, t, row, :], even, odd)
        rows = pl.ds(group * 8 * RADIX + t, 8, stride=RADIX)
        for n in range(SHARDS):
            out_ref[n, rows, :] = times[n]
        return carry

    lax.fori_loop(0, RADIX * groups, step, 0)


dot = functools.partial(jnp.dot, preferred_element_type=jnp.float32)


def halves_of(values):
    high = values.astype(jnp.bfloat16)
    low = (values - high.astype(jnp.float32)).astype(jnp.bfloat16)
    return high, low


def product(tables, t, values):
    high, low = halves_of(values)
    return [
        dot(tables[k][t], high) + (dot(tables[k][t], low) + dot(tables[k + 1][t], high)) for k in (0, 2)
    ]


def turn(parts, sign):
    (r0, i0), (r1, i1), (r2, i2), (r3, i3) = parts
    ar, ai, br, bi = r0 + r2, i0 + i2, r0 - r2, i0 - i2
    cr, ci, dr, di = r1 + r3, i1 + i3, r1 - r3, i1 - i3
    if sign < 0:
        dr, di = -dr, -di
    return (ar + cr, ai + ci), (br + di, bi - dr), (ar - cr, ai - ci), (br - di, bi + dr)


def forward_parts(z_ref, tables, s_ref, keep):
    inner, lanes = s_ref.shape[2:]
    for t in range(RADIX):
        re = z_ref[:, 0, t].reshape(inner, lanes)
        im = z_ref[:, 1, t].reshape(inner, lanes) * keep
        cosine, sine = product(tables, t, jnp.concatenate([re, im], 1))
        s_ref[t, 0] = cosine[:, :lanes] + sine[:, lanes:]
        s_ref[t, 1] = cosine[:, lanes:] - sine[:, :lanes]


def rows_at(index):
    return pl.ds(pl.multiple_of(index, 8), 8)


def write_terms(s_ref, row, at, saved_ref, term_ref, re, im):
    a, b = saved_ref[0, at], saved_ref[1, at]
    term_ref[0, at] = a * re + b * im
    term_ref[1, at] = a * im - b * re


def other_kernel(pick_ref, z_ref, *refs):
    tables = refs[:4]
    saved_ref, term_ref, s_ref = refs[4:]
    inner = s_ref.shape[2]
    forward_parts(z_ref, tables, s_ref, 1.0)

    def step(index, carry):
        row = rows_at(index * 8)
        parts = [(s_ref[t, 0, row], s_ref[t, 1, row]) for t in range(RADIX)]
        for q, (re, im) in enumerate(turn(parts, 1)):
            write_terms(s_ref, row, rows_at(q * inner + index * 8), saved_ref, term_ref, re, im)
        return carry

    lax.fori_loop(0, inner // 8, step, 0, unroll=2)


def spectrum_kernel(pick_ref, z_ref, *refs):
    tables, tables16, back, back16 = refs[0:4], refs[4:8], refs[8:12], refs[12:16]
    saved_ref, filt_ref, mirror_ref, term_ref, u_ref, s_ref = refs[16:]
    first = pick_ref[1]
    keep = (1 - first).astype(jnp.float32)
    inner, lanes = s_ref.shape[2:]
    slivers = u_ref.shape[0]

    def inverse_of(tables, slots):
        for t in range(RADIX):
            cosine, sine = product(tables, t, jnp.concatenate([s_ref[t, 0], s_ref[t, 1]], 1))
            values = (cosine[:, :lanes] - sine[:, lanes:], sine[:, :lanes] + cosine[:, lanes:])
            for slot, of in slots:
                u_ref[:, slot, t] = values[of].reshape(slivers, inner // slivers, lanes)

    forward_parts(z_ref, tables, s_ref, keep)

    def step(index, carry):
        row = rows_at(index * 8)
        parts = [(s_ref[t, 0, row], s_ref[t, 1, row]) for t in range(RADIX)]
        back_parts = []
        for q, (re, im) in enumerate(turn(parts, 1)):
            at = rows_at(q * inner + index * 8)
            write_terms(s_ref, row, at, saved_ref, term_ref, re, im)
            a = filt_ref[0, at] + keep * mirror_ref[0, at]
            b = keep * mirror_ref[1, at] - filt_ref[1, at]
            back_parts.append((a * re - b * im, a * im + b * re))
        for t, (re, im) in enumerate(turn(back_parts, -1)):
            s_ref[t, 0, row] = re
            s_ref[t, 1, row] = im
        return carry

    lax.fori_loop(0, inner // 8, step, 0, unroll=2)
    inverse_of(back, ((0, 0), (1, 1)))

    @pl.when(first == 1)
    def _():
        for t in range(RADIX):
            cosine, sine = product(tables16, t, z_ref[:, 1, t].reshape(inner, lanes))
            s_ref[t, 0] = cosine
            s_ref[t, 1] = -sine

        def step16(index, carry):
            row = rows_at(index * 8)
            parts = []
            for q, (re, im) in enumerate(turn([(s_ref[t, 0, row], s_ref[t, 1, row]) for t in range(RADIX)], 1)):
                at = rows_at(q * inner + index * 8)
                a, b = mirror_ref[0, at], mirror_ref[1, at]
                parts.append((a * re + b * im, a * im - b * re))
            for t, (re, im) in enumerate(turn(parts, -1)):
                s_ref[t, 0, row] = re
                s_ref[t, 1, row] = im
            return carry

        lax.fori_loop(0, inner // 8, step16, 0, unroll=2)
        inverse_of(back16, ((1, 0),))


def split_table(values):
    high = lax.reduce_precision(values, 8, 7)
    return [high.astype(jnp.bfloat16), (values - high).astype(jnp.bfloat16)]


def base_table(inner, points, transposed):
    time = np.arange(RADIX)[:, None, None] + RADIX * np.arange(inner)[None, None, :]
    angle = 2.0 * np.pi * ((time * 2 * SHARDS * np.arange(inner)[None, :, None]) % points) / points
    if transposed:
        angle = angle.transpose(0, 2, 1)
    return np.cos(angle).astype(np.float32), np.sin(angle).astype(np.float32)


def make_table(residue, inner, points, factor, transposed):
    base_cos, base_sin = base_table(inner, points, transposed)
    time = jnp.arange(RADIX)[:, None] + RADIX * jnp.arange(inner)[None, :]
    angle = ((time * residue) % points).astype(jnp.float32) * (2.0 * math.pi / points)
    twist_cos, twist_sin = lax.optimization_barrier((jnp.cos(angle) * factor, jnp.sin(angle) * factor))
    at = (slice(None), slice(None), None) if transposed else (slice(None), None, slice(None))
    twist_cos, twist_sin = twist_cos[at], twist_sin[at]
    cosine = base_cos * twist_cos - base_sin * twist_sin
    sine = base_sin * twist_cos + base_cos * twist_sin
    return split_table(cosine) + split_table(sine)


def fixed_table(residue, inner, points, factor, transposed):
    time = np.arange(RADIX)[:, None, None] + RADIX * np.arange(inner)[None, None, :]
    phase = (time * (residue + 2 * SHARDS * np.arange(inner))[None, :, None]) % points
    if transposed:
        phase = phase.transpose(0, 2, 1)
    found = []
    for values in (np.cos(2.0 * np.pi * phase / points) * factor, np.sin(2.0 * np.pi * phase / points) * factor):
        high = values.astype(np.float32).astype(jnp.bfloat16)
        found += [high, (values - high.astype(np.float64)).astype(jnp.bfloat16)]
    return found


def on_device(grad_out, input_spectrum, filter_spectrum, skip_gain, interpret=False):
    column = lax.axis_index("tm")
    stream = lax.axis_index("dp")
    groups = lax.axis_size("dp")
    _, length, channels = grad_out.shape
    sliver = length // SHARDS
    inner = length // RADIX
    points = 2 * length * SHARDS
    factor = 1.0 / math.sqrt(points)
    params = functools.partial(pltpu.CompilerParams, vmem_limit_bytes=56 * 1024 * 1024)
    f32 = jnp.float32

    pick = (column >= 8).astype(jnp.int32)
    first = (column == 0).astype(jnp.int32)
    picks = jnp.stack([pick, first])

    rows = sliver // RADIX
    raw = lax.all_to_all(grad_out.reshape(SHARDS, sliver, channels), "tm", 0, 0, tiled=True)

    part = length // groups
    filt = filter_spectrum[:, :, 0]
    give = lax.dynamic_index_in_dim(filt, (column < 8).astype(jnp.int32), 1, False)
    turned = lax.rev(lax.dynamic_slice_in_dim(give, (groups - 1 - stream) * part, part, 1), (1,))
    plain = lax.dynamic_slice_in_dim(give, stream * part, part, 1)
    sent = jnp.where(column == 8, plain, turned)
    swap = [(a, 15 - a) for a in range(8)] + [(8, 0)] + [(a, 16 - a) for a in range(9, 16)]
    swapped, raw = lax.optimization_barrier((lax.ppermute(sent, "tm", swap), raw))
    mirror = lax.all_gather(swapped, "dp", axis=1, tiled=True)

    z_shape = (SHARDS, 2, RADIX, rows)
    z_block = pl.BlockSpec(z_shape + (LANES,), lambda c: (0, 0, 0, 0, c))
    picked, other = pl.pallas_call(
        expand_kernel,
        grid=(channels // LANES,),
        in_specs=[pl.BlockSpec((SHARDS, sliver, LANES), lambda c: (0, 0, c))],
        out_specs=[z_block, z_block],
        out_shape=[jax.ShapeDtypeStruct(z_shape + (channels,), f32)] * 2,
        compiler_params=params(),
        cost_estimate=pl.CostEstimate(flops=300 * length * channels // 16, bytes_accessed=5 * length * channels * 4, transcendentals=0),
        interpret=interpret,
        name="expand",
    )(raw)
    z_picked = lax.all_to_all(picked, "tm", 0, 0, tiled=True)
    z_picked, other = lax.optimization_barrier((z_picked, other))
    z_other = lax.all_to_all(other, "tm", 0, 0, tiled=True)

    table = functools.partial(make_table, inner=inner, points=points, factor=factor)
    known = functools.partial(fixed_table, residue=16, inner=inner, points=points, factor=factor)
    residue = 2 * column + pick
    picked_tables = table(residue, transposed=False) + known(transposed=False)
    picked_tables += table(residue, transposed=True) + known(transposed=True)
    other_tables = table(2 * column + 1 - pick, transposed=False)

    def fixed(values):
        return pl.BlockSpec(values.shape, lambda c, s: (0,) * values.ndim, pipeline_mode=pl.Buffered(1))

    z_spec = pl.BlockSpec(z_shape + (LANES,), lambda c, s: (0, 0, 0, 0, c))
    saved_shape = (2, None, None, None, length, LANES)
    term_shape = jax.ShapeDtypeStruct((2, length, channels), f32)
    term_spec = pl.BlockSpec((2, length, LANES), lambda c, s: (0, 0, c))
    scratch = [pltpu.VMEM((RADIX, 2, inner, LANES), f32)]

    terms, inverted = pl.pallas_call(
        spectrum_kernel,
        grid_spec=pltpu.PrefetchScalarGridSpec(
            num_scalar_prefetch=1,
            grid=(channels // LANES,),
            in_specs=[z_spec]
            + [fixed(table) for table in picked_tables]
            + [
                pl.BlockSpec(saved_shape, lambda c, s: (0, 0, s[0], 0, 0, c)),
                pl.BlockSpec((2, None, None, length, LANES), lambda c, s: (0, s[0], 0, 0, c)),
                pl.BlockSpec((2, length, LANES), lambda c, s: (0, 0, c)),
            ],
            out_specs=[
                term_spec,
                z_spec,
            ],
            scratch_shapes=scratch,
        ),
        out_shape=[term_shape, jax.ShapeDtypeStruct((SHARDS, 2, RADIX, rows, channels), f32)],
        compiler_params=params(),
        cost_estimate=pl.CostEstimate(flops=10**10, bytes_accessed=12 * length * channels * 4, transcendentals=0),
        interpret=interpret,
        name="spectrum",
    )(picks, z_picked, *picked_tables, input_spectrum, filter_spectrum, mirror)
    terms, inverted, z_other = lax.optimization_barrier((terms, inverted, z_other))
    other_terms = pl.pallas_call(
        other_kernel,
        grid_spec=pltpu.PrefetchScalarGridSpec(
            num_scalar_prefetch=1,
            grid=(channels // LANES,),
            in_specs=[z_spec]
            + [fixed(table) for table in other_tables]
            + [
                pl.BlockSpec(saved_shape, lambda c, s: (0, 0, 1 - s[0], 0, 0, c)),
            ],
            out_specs=term_spec,
            scratch_shapes=scratch,
        ),
        out_shape=term_shape,
        compiler_params=params(),
        cost_estimate=pl.CostEstimate(flops=7 * 10**9, bytes_accessed=8 * length * channels * 4, transcendentals=0),
        interpret=interpret,
        name="other",
    )(picks, z_other, *other_tables, input_spectrum)

    landed = lax.all_to_all(inverted, "tm", 0, 0, tiled=True)
    ours = lax.psum_scatter(terms, "dp", scatter_dimension=1, tiled=True)
    other_terms, _ = lax.optimization_barrier((other_terms, landed))
    others = lax.psum_scatter(other_terms, "dp", scatter_dimension=1, tiled=True)
    combined = pl.pallas_call(
        combine_kernel,
        grid=(channels // LANES,),
        in_specs=[
            pl.BlockSpec((SHARDS, 2, RADIX, rows, LANES), lambda c: (0, 0, 0, 0, c)),
        ],
        out_specs=pl.BlockSpec((SHARDS, sliver, LANES), lambda c: (0, 0, c)),
        out_shape=jax.ShapeDtypeStruct((SHARDS, sliver, channels), f32),
        compiler_params=params(),
        cost_estimate=pl.CostEstimate(flops=400 * length * channels // 16, bytes_accessed=4 * length * channels * 4, transcendentals=0),
        interpret=interpret,
        name="combine",
    )(landed)
    back = lax.all_to_all(combined, "tm", 0, 0, tiled=True)
    grad_filter = jnp.where(pick == 0, jnp.stack([ours, others], 1), jnp.stack([others, ours], 1))[:, :, None]
    return (back.reshape(1, length, channels) + skip_gain * grad_out, grad_filter)


def solution(mesh, interpret=False):
    return jax.shard_map(
        functools.partial(on_device, interpret=interpret),
        mesh=mesh,
        in_specs=(
            P("dp", "tm", None),
            P(None, "dp", None, "tm", None, None),
            P(None, None, "tm", None, None),
            P(),
        ),
        out_specs=(P("dp", "tm", None), P(None, None, "tm", "dp", None)),
        check_vma=False,
    )
```

time: 323 us -> 297 us (0.920)
  blocking collectives: 85.4 us -> 59.1 us
  waiting for transfers between devices: 115 us -> 133 us
  other arithmetic: 27.2 us -> 11.2 us
  local copies, waits for them, and re-layouts: 10 us -> 3.92 us
  starting transfers between devices: 24 us -> 27.3 us
    ppermute x1, waiting for transfers between devices: 0.01 us -> 29.7 us  [on_device(): lax.ppermute(sent, 'tm', swap)]
    all_to_all x2 -> x1, blocking collectives: 85.4 us -> 59.1 us  [on_device(): z_picked = lax.all_to_all(picked, 'tm', 0, 0, tiled=True)]
    all_to_all x1, waiting for transfers between devices: 24.9 us -> 0.01 us  [on_device(): lax.all_to_all(grad_out.reshape(SHARDS, sliver, channels), 'tm', 0, 0, ti...]
    concatenate x1 -> x0, other arithmetic: 21.2 us -> none  [make_tables(): jnp.concatenate([jnp.cos(angle) * factor, jnp.sin(angle) * factor], 1)]
    all_to_all x1 -> x3, waiting for transfers between devices: 85.6 us -> 103 us  [the longest x1 47.4 us: on_device(): landed = lax.all_to_all(inverted, 'tm', 0, 0, tiled=True)]
    pallas_call x0 -> x1, Pallas kernels: none -> 10.1 us  [on_device(): pl.pallas_call(other_kernel, grid_spec=pltpu.PrefetchScalarGridSpec(num_s...]
    pallas_call x1, Pallas kernels: 35.1 us -> 27.1 us  [on_device(): pl.pallas_call(spectrum_kernel, grid_spec=pltpu.PrefetchScalarGridSpec(nu...]
    another operation x3 -> x0, local copies, waits for them, and re-layouts: 5.19 us -> none  [the longest x2 2.93 us: split_table(): return jnp.stack([high, values - high], -3).astype(jnp.bfloat16)]
  transfers between devices with their start and end apart: 5 -> 8, of which waited for: 3 -> 4; matrix products, arithmetic and copies ran while one was open for 10% -> 4% of each run, Pallas kernels for 4% -> 16%
where the time goes in v2:
time: 297 us
  waiting for transfers between devices  133 us (45%)
  blocking collectives  59.1 us (20%)
  Pallas kernels  48.3 us (16%)
  starting transfers between devices  27.3 us (9%)
  between operations  13.9 us (5%)
  other arithmetic  11.2 us (4%)
  local copies, waits for them, and re-layouts  3.92 us (1%)
    all_to_all x1, blocking collectives, on_device(): z_picked = lax.all_to_all(picked, 'tm', 0, 0, tiled=True)  59.1 us
    all_to_all x1, waiting for transfers between devices, on_device(): landed = lax.all_to_all(inverted, 'tm', 0, 0, tiled=True)  47.4 us
    ppermute x1, waiting for transfers between devices, on_device(): lax.ppermute(sent, 'tm', swap)  29.7 us
    all_to_all x1, waiting for transfers between devices, on_device(): z_other = lax.all_to_all(other, 'tm', 0, 0, tiled=True)  28.3 us
    all_to_all x1, waiting for transfers between devices, on_device(): back = lax.all_to_all(combined, 'tm', 0, 0, tiled=True)  27.6 us
    pallas_call x1, Pallas kernels, on_device(): pl.pallas_call(spectrum_kernel, grid_spec=pltpu.PrefetchScalarGridSpec(nu...  27.1 us
    pallas_call x1, Pallas kernels, on_device(): pl.pallas_call(other_kernel, grid_spec=pltpu.PrefetchScalarGridSpec(num_s...  10.1 us
    all_to_all x1, starting transfers between devices, on_device(): lax.all_to_all(grad_out.reshape(SHARDS, sliver, channels), 'tm', 0, 0, ti...  7.97 us
  transfers between devices with their start and end apart: 8, of which 4 were waited for; matrix products, arithmetic and copies ran while one was open for 4% of the time, Pallas kernels for 16%

profile of v2, /device:TPU:0, one launch (start us, length us, event | category | flops | bytes accessed | tf_op | source)
XLA Modules:
  0.0 296.7 jit_solution(13338379304807428293)
XLA Ops:
  7.2 8.0 %all-to-all-start = ((f32[16,64,512]{2,1,0:T(8,128)}), f32[16,64,512]{2,1,0:T(8,128)S(1)}, u32[]{:S(2)}, u32[]{:S(2)}) async-start(f32[16,64,512]{2,1,0:T(8,128)} %bitcast.12), calls=%async_computation | async-start | bytes 4194304 | tf_op jit(solution)/shard_map/all_to_all | solution.py:322
  15.1 0.0 all-gather.2.cloned.1.call-start
  15.2 1.1 dynamic-slice_bitcast_fusion
  16.3 0.3 rev.3
  16.6 1.2 bitcast_select_fusion
  17.8 5.3 %collective-permute-start = (f32[2,128,512]{2,1,0:T(8,128)S(1)}, f32[2,128,512]{2,1,0:T(8,128)S(1)}, u32[]{:S(2)}, u32[]{:S(2)}) collective-permute-start(f32[2,128,512]{2,1,0:T(8,128)S(1)} %bitcast_select_fusion), channel_id=1, source_target_pairs={{0,15},{1,14},{2,13},{3,12},{4,11},{5,10},{6,9},{7,8},{8,0},{9,7},... | collective-permute-start | bytes 1572872 | tf_op jit(solution)/shard_map/ppermute | solution.py:331
  23.1 29.7 %collective-permute-done = f32[2,128,512]{2,1,0:T(8,128)S(1)} collective-permute-done((f32[2,128,512]{2,1,0:T(8,128)S(1)}, f32[2,128,512]{2,1,0:T(8,128)S(1)}, u32[]{:S(2)}, u32[]{:S(2)}) %collective-permute-start) | collective-permute-done | bytes 524320 | tf_op jit(solution)/shard_map/ppermute | solution.py:331
  52.8 0.8 copy-done.5
  53.7 0.0 all-gather.2.cloned.1.call-update
  53.7 0.6 copy-done.1
  54.3 6.0 %expand.1 = (f32[16,2,4,16,512]{4,3,2,1,0:T(8,128)}, f32[16,2,4,16,512]{4,3,2,1,0:T(8,128)}) custom-call(f32[16,64,512]{2,1,0:T(8,128)} %copy-done.1), custom_call_target="tpu_custom_call" | custom-call | flops 9830400 | bytes 10485760 | tf_op jit(solution)/shard_map/expand/pallas_call | solution.py:336
  60.3 59.1 %all_to_all.25.z_ref = f32[16,2,4,16,512]{4,3,2,1,0:T(8,128)} all-to-all(f32[16,2,4,16,512]{4,3,2,1,0:T(8,128)} %get-tuple-element.19), channel_id=1, replica_groups=mesh['dp'=8,'tm'=16] {'tm'}, dimensions={0} | all-to-all | bytes 8388608 | tf_op jit(solution)/shard_map/all_to_all | solution.py:347
  119.4 4.8 %all-to-all-start.2 = ((f32[16,2,4,16,512]{4,3,2,1,0:T(8,128)}), f32[16,2,4,16,512]{4,3,2,1,0:T(8,128)}, u32[]{:S(2)}, u32[]{:S(2)}) async-start(f32[16,2,4,16,512]{4,3,2,1,0:T(8,128)} %get-tuple-element.27), calls=%async_computation.2 | async-start | bytes 8388608 | tf_op jit(solution)/shard_map/all_to_all | solution.py:349
  124.2 0.0 reduce-scatter.3.cloned.1.call-start
  124.3 0.1 sine_multiply_fusion
  124.4 0.6 pad_add_fusion.pick_ref
  125.0 4.1 %fusion.5 = (bf16[4,256,256]{2,1,0:T(8,128)(2,1)}, bf16[4,256,256]{2,1,0:T(8,128)(2,1)}, bf16[4,256,256]{2,1,0:T(8,128)(2,1)}, bf16[4,256,256]{2,1,0:T(8,128)(2,...) fusion(f32[4,256,256]{2,1,0:T(8,128)} %constant.129.clone, ...), kind=kLoop, calls=%fused_computation.18 | loop fusion | flops 11010048 | bytes 10502144 | tf_op jit(solution)/shard_map/convert_element_type | solution.py:270
  129.2 0.0 all-gather.2.cloned.1.call-done.refs_18_
  129.2 27.1 %spectrum.1 = (f32[2,1024,512]{2,1,0:T(8,128)}, f32[16,2,4,16,512]{4,3,2,1,0:T(8,128)}) custom-call(s32[2]{0:T(128)} %pad_add_fusion.pick_ref, f32[16,2,4,16,512]{4,3,2,1,0:T(8,128)} %all_to_all.25.z_ref, bf16[4,256,256]{2,1,0:T(8,128)(2,1)} %get-tuple-element.48.refs_0_, bf16[4,256,256]{2,1,0:T(8,128)(2,1)} %get-tuple-element.50.refs_1_, ...), custom_call_target="tpu_custom_call" | custom-call | flops 10000000000 | bytes 25165824 | tf_op jit(solution)/shard_map/spectrum/pallas_call | solution.py:367
  156.3 28.3 %all-to-all-done.2.z_ref = f32[16,2,4,16,512]{4,3,2,1,0:T(8,128)} async-done(((f32[16,2,4,16,512]{4,3,2,1,0:T(8,128)}), f32[16,2,4,16,512]{4,3,2,1,0:T(8,128)}, u32[]{:S(2)}, u32[]{:S(2)}) %all-to-all-start.2) | async-done | bytes 4194336 | tf_op jit(solution)/shard_map/all_to_all | solution.py:349
  184.5 0.0 reduce-scatter.3.cloned.1.call-update
  184.6 4.6 %all-to-all-start.3 = ((f32[16,2,4,16,512]{4,3,2,1,0:T(8,128)}), f32[16,2,4,16,512]{4,3,2,1,0:T(8,128)}, u32[]{:S(2)}, u32[]{:S(2)}) async-start(f32[16,2,4,16,512]{4,3,2,1,0:T(8,128)} %get-tuple-element.28), calls=%async_computation.3 | async-start | bytes 8388608 | tf_op jit(solution)/shard_map/all_to_all | solution.py:412
  189.1 0.0 reduce-scatter.5.cloned.1.call-start
  189.2 10.1 %other.1 = f32[2,1024,512]{2,1,0:T(8,128)} custom-call(s32[2]{0:T(128)} %pad_add_fusion.pick_ref, f32[16,2,4,16,512]{4,3,2,1,0:T(8,128)} %all-to-all-done.2.z_ref, bf16[4,256,256]{2,1,0:T(8,128)(2,1)} %get-tuple-element.39.refs_0_, bf16[4,256,256]{2,1,0:T(8,128)(2,1)} %get-tuple-element.37.refs_1_, bf16[4,256,256]{2,1,0:T(8,128)(2,1)} %get-tuple-element.38.refs_2_, ...), custom_call_target="tpu_custom_call" | custom-call | flops 7000000000 | bytes 16777216 | tf_op jit(solution)/shard_map/other/pallas_call | solution.py:392
  199.3 47.4 %all-to-all-done.3.u_ref = f32[16,2,4,16,512]{4,3,2,1,0:T(8,128)} async-done(((f32[16,2,4,16,512]{4,3,2,1,0:T(8,128)}), f32[16,2,4,16,512]{4,3,2,1,0:T(8,128)}, u32[]{:S(2)}, u32[]{:S(2)}) %all-to-all-start.3) | async-done | bytes 4194336 | tf_op jit(solution)/shard_map/all_to_all | solution.py:412
  246.7 0.0 reduce-scatter.5.cloned.1.call-update
  246.7 5.1 %combine.1 = f32[16,64,512]{2,1,0:T(8,128)} custom-call(f32[16,2,4,16,512]{4,3,2,1,0:T(8,128)} %all-to-all-done.3.u_ref), custom_call_target="tpu_custom_call" | custom-call | flops 13107200 | bytes 8388608 | tf_op jit(solution)/shard_map/combine/pallas_call | solution.py:416
  251.8 4.5 %all-to-all-start.4 = ((f32[16,64,512]{2,1,0:T(8,128)}), f32[16,64,512]{2,1,0:T(8,128)}, u32[]{:S(2)}, u32[]{:S(2)}) async-start(f32[16,64,512]{2,1,0:T(8,128)} %combine.1), calls=%async_computation.4 | async-start | bytes 4194304 | tf_op jit(solution)/shard_map/all_to_all | solution.py:429
  256.3 27.6 %all-to-all-done.4 = f32[16,64,512]{2,1,0:T(8,128)} async-done(((f32[16,64,512]{2,1,0:T(8,128)}), f32[16,64,512]{2,1,0:T(8,128)}, u32[]{:S(2)}, u32[]{:S(2)}) %all-to-all-start.4) | async-done | bytes 2097184 | tf_op jit(solution)/shard_map/all_to_all | solution.py:429
  283.9 3.4 %bitcast_add_fusion = f32[1,1024,512]{2,1,0:T(8,128)} fusion(f32[1,1024,512]{2,1,0:T(8,128)S(1)} %copy-done, f32[512]{0:T(512)S(1)} %copy-done.6, f32[1,1024,512]{2,1,0:T(8,128)} %bitcast.11), kind=kLoop, calls=%fused_computation | loop fusion | flops 1048576 | bytes 6293504 | tf_op jit(solution)/shard_map/add | solution.py:431
  287.4 1.8 maximum_select_fusion
  289.1 1.0 copy.20
  (16 shorter events, 0.0 us)
Async XLA Ops:
  7.2 45.7 %all-to-all-start = ((f32[16,64,512]{2,1,0:T(8,128)}), f32[16,64,512]{2,1,0:T(8,128)S(1)}, u32[]{:S(2)}, u32[]{:S(2)}) async-start(f32[16,64,512]{2,1,0:T(8,128)} %bitcast.12), calls=%async_computation | async-start | bytes 4194304 | tf_op jit(solution)/shard_map/all_to_all | solution.py:322
  15.1 114.0 %all-gather.2.cloned.1.call-start = ((), (), s32[]{:S(2)}) async-start(), calls=%async_computation.7 | async-start | bytes 4718592 | tf_op jit(solution)/shard_map/all_gather | solution.py:332
  17.8 35.0 %collective-permute-start = (f32[2,128,512]{2,1,0:T(8,128)S(1)}, f32[2,128,512]{2,1,0:T(8,128)S(1)}, u32[]{:S(2)}, u32[]{:S(2)}) collective-permute-start(f32[2,128,512]{2,1,0:T(8,128)S(1)} %bitcast_select_fusion), channel_id=1, source_target_pairs={{0,15},{1,14},{2,13},{3,12},{4,11},{5,10},{6,9},{7,8},{8,0},{9,7},... | collective-permute-start | bytes 1572872 | tf_op jit(solution)/shard_map/ppermute | solution.py:331
  52.8 0.9 copy-start.5
  52.8 1.5 copy-start.1
  119.4 5.6 %copy-start.2 = (f32[4,256,256]{2,1,0:T(8,128)S(1)}, f32[4,256,256]{2,1,0:T(8,128)}, u32[]{:S(2)}) copy-start(f32[4,256,256]{2,1,0:T(8,128)} %constant.132.clone) | copy-start | bytes 3145732
  119.4 5.6 %copy-start.3 = (f32[4,256,256]{2,1,0:T(8,128)S(1)}, f32[4,256,256]{2,1,0:T(8,128)}, u32[]{:S(2)}) copy-start(f32[4,256,256]{2,1,0:T(8,128)} %constant.131.clone) | copy-start | bytes 3145732
  119.4 5.6 %copy-start.4 = (f32[4,256,256]{2,1,0:T(8,128)S(1)}, f32[4,256,256]{2,1,0:T(8,128)}, u32[]{:S(2)}) copy-start(f32[4,256,256]{2,1,0:T(8,128)} %constant.130.clone) | copy-start | bytes 3145732
  119.4 65.1 %all-to-all-start.2 = ((f32[16,2,4,16,512]{4,3,2,1,0:T(8,128)}), f32[16,2,4,16,512]{4,3,2,1,0:T(8,128)}, u32[]{:S(2)}, u32[]{:S(2)}) async-start(f32[16,2,4,16,512]{4,3,2,1,0:T(8,128)} %get-tuple-element.27), calls=%async_computation.2 | async-start | bytes 8388608 | tf_op jit(solution)/shard_map/all_to_all | solution.py:349
  124.2 163.1 %reduce-scatter.3.cloned.1.call-start = ((), (), s32[]{:S(2)}) async-start(), calls=%async_computation.8 | async-start | bytes 4718592 | tf_op jit(solution)/shard_map/reduce_scatter | solution.py:413
  184.6 62.1 %all-to-all-start.3 = ((f32[16,2,4,16,512]{4,3,2,1,0:T(8,128)}), f32[16,2,4,16,512]{4,3,2,1,0:T(8,128)}, u32[]{:S(2)}, u32[]{:S(2)}) async-start(f32[16,2,4,16,512]{4,3,2,1,0:T(8,128)} %get-tuple-element.28), calls=%async_computation.3 | async-start | bytes 8388608 | tf_op jit(solution)/shard_map/all_to_all | solution.py:412
  189.1 98.2 %reduce-scatter.5.cloned.1.call-start = ((), (), s32[]{:S(2)}) async-start(), calls=%async_computation.9 | async-start | bytes 4718592 | tf_op jit(solution)/shard_map/reduce_scatter | solution.py:415
  246.7 37.2 %copy-start = (f32[1,1024,512]{2,1,0:T(8,128)S(1)}, f32[1,1024,512]{2,1,0:T(8,128)}, u32[]{:S(2)}) copy-start(f32[1,1024,512]{2,1,0:T(8,128)} %param.18) | copy-start | bytes 6291460
  246.7 37.2 %copy-start.6 = (f32[512]{0:T(512)S(1)}, f32[512]{0:T(512)}, u32[]{:S(2)}) copy-start(f32[512]{0:T(512)} %param.21) | copy-start | bytes 6148
  251.8 32.1 %all-to-all-start.4 = ((f32[16,64,512]{2,1,0:T(8,128)}), f32[16,64,512]{2,1,0:T(8,128)}, u32[]{:S(2)}, u32[]{:S(2)}) async-start(f32[16,64,512]{2,1,0:T(8,128)} %combine.1), calls=%async_computation.4 | async-start | bytes 4194304 | tf_op jit(solution)/shard_map/all_to_all | solution.py:429
Sparse Core Ops, SparseCore 0:
  53.8 34.9 all-gather.1
  184.7 37.3 reduce-scatter.2
  246.8 37.6 reduce-scatter.4

commit v3 on v2

--- a/solution.py
+++ b/solution.py
@@ -70,7 +70,7 @@
     return out
 
 
-def expand_kernel(x_ref, picked_ref, other_ref):
+def expand_block(x_ref, out_ref, other):
     groups = x_ref.shape[1] // RADIX // 8
 
     def step(index, carry):
@@ -80,22 +80,31 @@
         found = residues_of(values)
         zero = jnp.zeros_like(values[0])
         for a in range(SHARDS):
-            for rho in (2 * a, 2 * a + 1):
-                if rho <= 16:
-                    re, im = found[rho]
-                    if rho == 0:
-                        im = found[16][0]
-                    elif rho == 16:
-                        im = zero
-                else:
-                    re, im = found[32 - rho]
-                    im = -im
-                out_ref = picked_ref if (rho % 2 == 1) == (a >= 8) else other_ref
-                out_ref[a, 0, t, row, :] = re
-                out_ref[a, 1, t, row, :] = im
+            rho = 2 * a + ((a >= 8) != other)
+            if rho <= 16:
+                re, im = found[rho]
+                if rho == 0:
+                    im = found[16][0]
+                elif rho == 16:
+                    im = zero
+            else:
+                re, im = found[32 - rho]
+                im = -im
+            out_ref[a, 0, t, row, :] = re
+            out_ref[a, 1, t, row, :] = im
         return carry
 
     lax.fori_loop(0, RADIX * groups, step, 0)
+
+
+def expand_kernel(blocks, x_ref, out_ref):
+    @pl.when(pl.program_id(0) < blocks)
+    def _():
+        expand_block(x_ref, out_ref, False)
+
+    @pl.when(pl.program_id(0) >= blocks)
+    def _():
+        expand_block(x_ref, out_ref, True)
 
 
 def times_of(v0, v16, even, odd):
@@ -129,7 +138,7 @@
     return out
 
 
-def combine_kernel(u_ref, out_ref):
+def combine_kernel(u_ref, x_ref, gain_ref, out_ref):
     groups = out_ref.shape[1] // RADIX // 8
 
     def step(index, carry):
@@ -139,8 +148,9 @@
         odd = {31 - 2 * d: (u_ref[d, 0, t, row, :], u_ref[d, 1, t, row, :]) for d in range(8, 16)}
         times = times_of(u_ref[0, 0, t, row, :], u_ref[0, 1, t, row, :], even, odd)
         rows = pl.ds(group * 8 * RADIX + t, 8, stride=RADIX)
+        gain = gain_ref[0:1, :]
         for n in range(SHARDS):
-            out_ref[n, rows, :] = times[n]
+            out_ref[n, rows, :] = times[n] + gain * x_ref[n, rows, :]
         return carry
 
     lax.fori_loop(0, RADIX * groups, step, 0)
@@ -193,7 +203,7 @@
 
 def other_kernel(pick_ref, z_ref, *refs):
     tables = refs[:4]
-    saved_ref, term_ref, s_ref = refs[4:]
+    saved_ref, _, term_ref, s_ref = refs[4:]
     inner = s_ref.shape[2]
     forward_parts(z_ref, tables, s_ref, 1.0)
 
@@ -319,6 +329,8 @@
     picks = jnp.stack([pick, first])
 
     rows = sliver // RADIX
+    blocks = channels // LANES
+    early = blocks // 2
     raw = lax.all_to_all(grad_out.reshape(SHARDS, sliver, channels), "tm", 0, 0, tiled=True)
 
     part = length // groups
@@ -327,41 +339,52 @@
     turned = lax.rev(lax.dynamic_slice_in_dim(give, (groups - 1 - stream) * part, part, 1), (1,))
     plain = lax.dynamic_slice_in_dim(give, stream * part, part, 1)
     sent = jnp.where(column == 8, plain, turned)
-    swap = [(a, 15 - a) for a in range(8)] + [(8, 0)] + [(a, 16 - a) for a in range(9, 16)]
-    swapped, raw = lax.optimization_barrier((lax.ppermute(sent, "tm", swap), raw))
-    mirror = lax.all_gather(swapped, "dp", axis=1, tiled=True)
-
-    z_shape = (SHARDS, 2, RADIX, rows)
-    z_block = pl.BlockSpec(z_shape + (LANES,), lambda c: (0, 0, 0, 0, c))
-    picked, other = pl.pallas_call(
-        expand_kernel,
-        grid=(channels // LANES,),
-        in_specs=[pl.BlockSpec((SHARDS, sliver, LANES), lambda c: (0, 0, c))],
-        out_specs=[z_block, z_block],
-        out_shape=[jax.ShapeDtypeStruct(z_shape + (channels,), f32)] * 2,
-        compiler_params=params(),
-        cost_estimate=pl.CostEstimate(flops=300 * length * channels // 16, bytes_accessed=5 * length * channels * 4, transcendentals=0),
-        interpret=interpret,
-        name="expand",
-    )(raw)
-    z_picked = lax.all_to_all(picked, "tm", 0, 0, tiled=True)
-    z_picked, other = lax.optimization_barrier((z_picked, other))
-    z_other = lax.all_to_all(other, "tm", 0, 0, tiled=True)
-
     table = functools.partial(make_table, inner=inner, points=points, factor=factor)
     known = functools.partial(fixed_table, residue=16, inner=inner, points=points, factor=factor)
     residue = 2 * column + pick
-    picked_tables = table(residue, transposed=False) + known(transposed=False)
-    picked_tables += table(residue, transposed=True) + known(transposed=True)
-    other_tables = table(2 * column + 1 - pick, transposed=False)
+    made = [table(residue, transposed=False), table(residue, transposed=True), table(2 * column + 1 - pick, transposed=False)]
+    raw, sent, made = lax.optimization_barrier((raw, sent, made))
+    picked_tables = made[0] + known(transposed=False) + made[1] + known(transposed=True)
+    other_tables = made[2]
+    swap = [(a, 15 - a) for a in range(8)] + [(8, 0)] + [(a, 16 - a) for a in range(9, 16)]
+    swapped = lax.ppermute(sent, "tm", swap)
+
+    z_shape = (SHARDS, 2, RADIX, rows)
+
+    def expand(picked, first_other, others, name):
+        return pl.pallas_call(
+            functools.partial(expand_kernel, picked),
+            grid=(picked + others,),
+            in_specs=[
+                pl.BlockSpec((SHARDS, sliver, LANES), lambda c: (0, 0, jnp.where(c < picked, c, c - picked + first_other)))
+            ],
+            out_specs=pl.BlockSpec(z_shape + (LANES,), lambda c: (0, 0, 0, 0, c)),
+            out_shape=jax.ShapeDtypeStruct(z_shape + ((picked + others) * LANES,), f32),
+            compiler_params=params(),
+            cost_estimate=pl.CostEstimate(
+                flops=300 * sliver * LANES * (picked + others), bytes_accessed=(picked + others) * 2**21, transcendentals=0
+            ),
+            interpret=interpret,
+            name=name,
+        )(raw)
+
+    first_part = expand(blocks, 0, early, "expand")
+    rest = expand(0, early, blocks - early, "expand_rest")
+    swapped, first_part, rest = lax.optimization_barrier((swapped, first_part, rest))
+    mirror = lax.all_gather(swapped, "dp", axis=1, tiled=True)
+    z_first = lax.all_to_all(first_part, "tm", 0, 0, tiled=True)
+    z_first, rest = lax.optimization_barrier((z_first, rest))
+    z_rest = lax.all_to_all(rest, "tm", 0, 0, tiled=True)
 
     def fixed(values):
         return pl.BlockSpec(values.shape, lambda c, s: (0,) * values.ndim, pipeline_mode=pl.Buffered(1))
 
-    z_spec = pl.BlockSpec(z_shape + (LANES,), lambda c, s: (0, 0, 0, 0, c))
+    def z_spec(shift):
+        return pl.BlockSpec(z_shape + (LANES,), lambda c, s: (0, 0, 0, 0, c + shift))
+
     saved_shape = (2, None, None, None, length, LANES)
-    term_shape = jax.ShapeDtypeStruct((2, length, channels), f32)
-    term_spec = pl.BlockSpec((2, length, LANES), lambda c, s: (0, 0, c))
+    term_shape = jax.ShapeDtypeStruct((2, 2, 1, length, channels), f32)
+    term_block = (2, None, None, length, LANES)
     scratch = [pltpu.VMEM((RADIX, 2, inner, LANES), f32)]
 
     terms, inverted = pl.pallas_call(
@@ -369,7 +392,7 @@
         grid_spec=pltpu.PrefetchScalarGridSpec(
             num_scalar_prefetch=1,
             grid=(channels // LANES,),
-            in_specs=[z_spec]
+            in_specs=[z_spec(0)]
             + [fixed(table) for table in picked_tables]
             + [
                 pl.BlockSpec(saved_shape, lambda c, s: (0, 0, s[0], 0, 0, c)),
@@ -377,8 +400,8 @@
                 pl.BlockSpec((2, length, LANES), lambda c, s: (0, 0, c)),
             ],
             out_specs=[
-                term_spec,
-                z_spec,
+                pl.BlockSpec(term_block, lambda c, s: (0, s[0], 0, 0, c)),
+                pl.BlockSpec(z_shape + (LANES,), lambda c, s: (0, 0, 0, 0, c)),
             ],
             scratch_shapes=scratch,
         ),
@@ -387,37 +410,46 @@
         cost_estimate=pl.CostEstimate(flops=10**10, bytes_accessed=12 * length * channels * 4, transcendentals=0),
         interpret=interpret,
         name="spectrum",
-    )(picks, z_picked, *picked_tables, input_spectrum, filter_spectrum, mirror)
-    terms, inverted, z_other = lax.optimization_barrier((terms, inverted, z_other))
-    other_terms = pl.pallas_call(
-        other_kernel,
-        grid_spec=pltpu.PrefetchScalarGridSpec(
-            num_scalar_prefetch=1,
-            grid=(channels // LANES,),
-            in_specs=[z_spec]
-            + [fixed(table) for table in other_tables]
-            + [
-                pl.BlockSpec(saved_shape, lambda c, s: (0, 0, 1 - s[0], 0, 0, c)),
-            ],
-            out_specs=term_spec,
-            scratch_shapes=scratch,
-        ),
-        out_shape=term_shape,
-        compiler_params=params(),
-        cost_estimate=pl.CostEstimate(flops=7 * 10**9, bytes_accessed=8 * length * channels * 4, transcendentals=0),
-        interpret=interpret,
-        name="other",
-    )(picks, z_other, *other_tables, input_spectrum)
-
+    )(picks, z_first, *picked_tables, input_spectrum, filter_spectrum, mirror)
+
+    def second(z, at, first_block, count, terms, name):
+        return pl.pallas_call(
+            other_kernel,
+            grid_spec=pltpu.PrefetchScalarGridSpec(
+                num_scalar_prefetch=1,
+                grid=(count,),
+                in_specs=[z_spec(at)]
+                + [fixed(table) for table in other_tables]
+                + [
+                    pl.BlockSpec(saved_shape, lambda c, s: (0, 0, 1 - s[0], 0, 0, c + first_block)),
+                    pl.BlockSpec(memory_space=pl.ANY),
+                ],
+                out_specs=pl.BlockSpec(term_block, lambda c, s: (0, 1 - s[0], 0, 0, c + first_block)),
+                scratch_shapes=scratch,
+            ),
+            out_shape=term_shape,
+            input_output_aliases={2 + len(other_tables) + 1: 0},
+            compiler_params=params(),
+            cost_estimate=pl.CostEstimate(
+                flops=2 * 10**9 * count, bytes_accessed=count * 2 * length * LANES * 4 * 3, transcendentals=0
+            ),
+            interpret=interpret,
+            name=name,
+        )(picks, z, *other_tables, input_spectrum, terms)
+
+    terms = second(z_first, blocks, 0, early, terms, "other")
+    terms, inverted, z_rest = lax.optimization_barrier((terms, inverted, z_rest))
+    terms = second(z_rest, 0, early, blocks - early, terms, "other_rest")
+    terms, inverted = lax.optimization_barrier((terms, inverted))
+    grad_filter = lax.psum_scatter(terms, "dp", scatter_dimension=3, tiled=True)
     landed = lax.all_to_all(inverted, "tm", 0, 0, tiled=True)
-    ours = lax.psum_scatter(terms, "dp", scatter_dimension=1, tiled=True)
-    other_terms, _ = lax.optimization_barrier((other_terms, landed))
-    others = lax.psum_scatter(other_terms, "dp", scatter_dimension=1, tiled=True)
     combined = pl.pallas_call(
         combine_kernel,
         grid=(channels // LANES,),
         in_specs=[
             pl.BlockSpec((SHARDS, 2, RADIX, rows, LANES), lambda c: (0, 0, 0, 0, c)),
+            pl.BlockSpec((SHARDS, sliver, LANES), lambda c: (0, 0, c)),
+            pl.BlockSpec((1, LANES), lambda c: (0, c)),
         ],
         out_specs=pl.BlockSpec((SHARDS, sliver, LANES), lambda c: (0, 0, c)),
         out_shape=jax.ShapeDtypeStruct((SHARDS, sliver, channels), f32),
@@ -425,10 +457,9 @@
         cost_estimate=pl.CostEstimate(flops=400 * length * channels // 16, bytes_accessed=4 * length * channels * 4, transcendentals=0),
         interpret=interpret,
         name="combine",
-    )(landed)
+    )(landed, raw, skip_gain[None])
     back = lax.all_to_all(combined, "tm", 0, 0, tiled=True)
-    grad_filter = jnp.where(pick == 0, jnp.stack([ours, others], 1), jnp.stack([others, ours], 1))[:, :, None]
-    return (back.reshape(1, length, channels) + skip_gain * grad_out, grad_filter)
+    return (back.reshape(1, length, channels), grad_filter)
 
 
 def solution(mesh, interpret=False):

time: 297 us -> 285 us (0.960)
  waiting for transfers between devices: 133 us -> 27.1 us
  blocking collectives: 59.1 us -> 164 us
  starting transfers between devices: 27.3 us -> 12.6 us
  Pallas kernels: 48.3 us -> 55.1 us
  other arithmetic: 11.2 us -> 6.45 us
    all_to_all x1 -> x3, blocking collectives: 59.1 us -> 164 us  [the longest x1 78.2 us: on_device(): z_first = lax.all_to_all(first_part, 'tm', 0, 0, tiled=True)]
    all_to_all x3 -> x1, waiting for transfers between devices: 103 us -> 0.01 us  [on_device(): z_rest = lax.all_to_all(rest, 'tm', 0, 0, tiled=True)]
    ppermute x1, waiting for transfers between devices: 29.7 us -> 2.79 us  [on_device(): swapped = lax.ppermute(sent, 'tm', swap)]
    all_to_all x1, waiting for transfers between devices: 0.01 us -> 24.3 us  [on_device(): lax.all_to_all(grad_out.reshape(SHARDS, sliver, channels), 'tm', 0, 0, ti...]
    all_to_all x3 -> x1, starting transfers between devices: 13.9 us -> 3.72 us  [on_device(): z_rest = lax.all_to_all(rest, 'tm', 0, 0, tiled=True)]
    pallas_call x2 -> x4, Pallas kernels: 16.1 us -> 22.7 us  [the longest x2 13.1 us: second(): pl.pallas_call(other_kernel, grid_spec=pltpu.PrefetchScalarGridSpec(num_s...]
    ppermute x1, starting transfers between devices: 5.32 us -> 0.85 us  [on_device(): swapped = lax.ppermute(sent, 'tm', swap)]
    add x1 -> x0, other arithmetic: 3.44 us -> none  [on_device(): back.reshape(1, length, channels) + skip_gain * grad_out]
  transfers between devices with their start and end apart: 8 -> 5, of which waited for: 4 -> 2; matrix products, arithmetic and copies ran while one was open for 4% -> 3% of each run, Pallas kernels for 16% -> 17%
where the time goes in v3:
time: 285 us; the launch traced here: 284 us
  blocking collectives  164 us (58%)
  Pallas kernels  55.1 us (19%)
  waiting for transfers between devices  27.1 us (10%)
  between operations  14.1 us (5%)
  starting transfers between devices  12.6 us (4%)
  other arithmetic  6.45 us (2%)
  local copies, waits for them, and re-layouts  5.35 us (2%)
    all_to_all x1, blocking collectives, on_device(): z_first = lax.all_to_all(first_part, 'tm', 0, 0, tiled=True)  78.2 us
    all_to_all x1, blocking collectives, on_device(): landed = lax.all_to_all(inverted, 'tm', 0, 0, tiled=True)  55.4 us
    all_to_all x1, blocking collectives, on_device(): back = lax.all_to_all(combined, 'tm', 0, 0, tiled=True)  30 us
    pallas_call x1, Pallas kernels, on_device(): pl.pallas_call(spectrum_kernel, grid_spec=pltpu.PrefetchScalarGridSpec(nu...  26.8 us
    all_to_all x1, waiting for transfers between devices, on_device(): lax.all_to_all(grad_out.reshape(SHARDS, sliver, channels), 'tm', 0, 0, ti...  24.3 us
    pallas_call x2, Pallas kernels, second(): pl.pallas_call(other_kernel, grid_spec=pltpu.PrefetchScalarGridSpec(num_s...  13.1 us
    pallas_call x2, Pallas kernels, expand(): pl.pallas_call(functools.partial(expand_kernel, picked), grid=(picked + o...  9.62 us
    all_to_all x1, starting transfers between devices, on_device(): lax.all_to_all(grad_out.reshape(SHARDS, sliver, channels), 'tm', 0, 0, ti...  7.97 us
  transfers between devices with their start and end apart: 5, of which 2 were waited for; matrix products, arithmetic and copies ran while one was open for 3% of the time, Pallas kernels for 17%

profile of v3, /device:TPU:0, one launch (start us, length us, event | category | flops | bytes accessed | tf_op | source)
XLA Modules:
  0.0 284.4 jit_solution(7237488037763812210)
XLA Ops:
  7.2 8.0 %all-to-all-start = ((f32[16,64,512]{2,1,0:T(8,128)}), f32[16,64,512]{2,1,0:T(8,128)S(1)}, u32[]{:S(2)}, u32[]{:S(2)}) async-start(f32[16,64,512]{2,1,0:T(8,128)} %bitcast.10), calls=%async_computation | async-start | bytes 4194304 | tf_op jit(solution)/shard_map/all_to_all | solution.py:334
  15.1 0.0 all-gather.2.cloned.1.call-start
  15.2 0.1 sine_multiply_fusion
  15.3 1.1 dynamic-slice_bitcast_fusion
  16.4 0.3 rev.3
  16.7 1.2 bitcast_select_fusion
  17.9 4.6 %fusion.5 = (bf16[4,256,256]{2,1,0:T(8,128)(2,1)}, bf16[4,256,256]{2,1,0:T(8,128)(2,1)}, bf16[4,256,256]{2,1,0:T(8,128)(2,1)}, bf16[4,256,256]{2,1,0:T(8,128)(2,...) fusion(f32[4,256,256]{2,1,0:T(8,128)} %constant.129.clone, ...), kind=kLoop, calls=%fused_computation.17 | loop fusion | flops 11010048 | bytes 10502144 | tf_op jit(solution)/shard_map/convert_element_type | solution.py:280
  22.5 24.3 %all-to-all-done.x_ref = f32[16,64,512]{2,1,0:T(8,128)S(1)} async-done(((f32[16,64,512]{2,1,0:T(8,128)}), f32[16,64,512]{2,1,0:T(8,128)S(1)}, u32[]{:S(2)}, u32[]{:S(2)}) %all-to-all-start) | async-done | bytes 2097184 | tf_op jit(solution)/shard_map/all_to_all | solution.py:334
  46.8 0.0 copy-start
  46.8 0.8 collective-permute-start
  47.6 0.5 copy-done
  48.1 2.8 expand_rest.1
  50.9 6.8 %expand.1 = f32[16,2,4,16,768]{4,3,2,1,0:T(8,128)} custom-call(f32[16,64,512]{2,1,0:T(8,128)} %copy-done), custom_call_target="tpu_custom_call" | custom-call | flops 14745600 | bytes 12582912 | tf_op jit(solution)/shard_map/expand/pallas_call | solution.py:355
  57.7 2.8 collective-permute-done
  60.5 0.0 copy-start.2
  60.5 0.8 copy-done.2
  61.3 0.0 all-gather.2.cloned.1.call-update
  61.3 78.2 %all_to_all.25.z_ref = f32[16,2,4,16,768]{4,3,2,1,0:T(8,128)} all-to-all(f32[16,2,4,16,768]{4,3,2,1,0:T(8,128)} %expand.1), channel_id=1, replica_groups=mesh['dp'=8,'tm'=16] {'tm'}, dimensions={0} | all-to-all | bytes 12582912 | tf_op jit(solution)/shard_map/all_to_all | solution.py:375
  139.6 3.7 %all-to-all-start.2 = ((f32[16,2,4,16,256]{4,3,2,1,0:T(8,128)}), f32[16,2,4,16,256]{4,3,2,1,0:T(8,128)S(1)}, u32[]{:S(2)}, u32[]{:S(2)}) async-start(f32[16,2,4,16,256]{4,3,2,1,0:T(8,128)} %expand_rest.1), calls=%async_computation.2 | async-start | bytes 4194304 | tf_op jit(solution)/shard_map/all_to_all | solution.py:377
  143.3 0.0 reduce-scatter.2.cloned.1.call-start
  143.4 0.6 pad_add_fusion.pick_ref
  143.9 0.0 all-gather.2.cloned.1.call-done.refs_18_
  143.9 26.8 %spectrum.1 = (f32[2,2,1,1024,512]{4,3,2,1,0:T(8,128)}, f32[16,2,4,16,512]{4,3,2,1,0:T(8,128)}) custom-call(s32[2]{0:T(128)} %pad_add_fusion.pick_ref, f32[16,2,4,16,768]{4,3,2,1,0:T(8,128)} %all_to_all.25.z_ref, bf16[4,256,256]{2,1,0:T(8,128)(2,1)} %get-tuple-element.45.refs_0_, bf16[4,256,256]{2,1,0:T(8,128)(2,1)} %get-tuple-element.46.refs_1_, ...), custom_call_target="tpu_custom_call" | custom-call | flops 10000000000 | bytes 25165824 | tf_op jit(solution)/shard_map/spectrum/pallas_call | solution.py:390
  170.7 6.6 %other.1.refs_5_ = f32[2,2,1,1024,512]{4,3,2,1,0:T(8,128)} custom-call(s32[2]{0:T(128)} %pad_add_fusion.pick_ref, f32[16,2,4,16,768]{4,3,2,1,0:T(8,128)} %all_to_all.25.z_ref, bf16[4,256,256]{2,1,0:T(8,128)(2,1)} %get-tuple-element.41.refs_0_, bf16[4,256,256]{2,1,0:T(8,128)(2,1)} %get-tuple-element.42.refs_1_, ...), custom_call_target="tpu_custom_call", output_to_operand_aliasing={{}: (7, {})} | custom-call | flops 4000000000 | bytes 6291456 | tf_op jit(solution)/shard_map/other/pallas_call | solution.py:416
  177.3 0.0 all-to-all-done.2.z_ref
  177.3 1.4 copy-done.1
  178.7 6.6 %other_rest.1 = f32[2,2,1,1024,512]{4,3,2,1,0:T(8,128)} custom-call(s32[2]{0:T(128)} %pad_add_fusion.pick_ref, f32[16,2,4,16,256]{4,3,2,1,0:T(8,128)} %copy-done.1, bf16[4,256,256]{2,1,0:T(8,128)(2,1)} %get-tuple-element.41.refs_0_, bf16[4,256,256]{2,1,0:T(8,128)(2,1)} %get-tuple-element.42.refs_1_, ...), custom_call_target="tpu_custom_call", output_to_operand_aliasing={{}: (7, {})} | custom-call | flops 4000000000 | bytes 6291456 | tf_op jit(solution)/shard_map/other_rest/pallas_call | solution.py:416
  185.2 0.0 reduce-scatter.2.cloned.1.call-update
  185.3 55.4 %all_to_all.26.u_ref = f32[16,2,4,16,512]{4,3,2,1,0:T(8,128)} all-to-all(f32[16,2,4,16,512]{4,3,2,1,0:T(8,128)} %get-tuple-element.60), channel_id=1, replica_groups=mesh['dp'=8,'tm'=16] {'tm'}, dimensions={0} | all-to-all | bytes 8388608 | tf_op jit(solution)/shard_map/all_to_all | solution.py:445
  240.7 5.5 %combine.1 = f32[16,64,512]{2,1,0:T(8,128)} custom-call(f32[16,2,4,16,512]{4,3,2,1,0:T(8,128)} %all_to_all.26.u_ref, f32[16,64,512]{2,1,0:T(8,128)} %copy-done, f32[1,512]{1,0:T(1,128)} %bitcast.11), custom_call_target="tpu_custom_call" | custom-call | flops 13107200 | bytes 8388608 | tf_op jit(solution)/shard_map/combine/pallas_call | solution.py:446
  246.2 30.0 %all_to_all.27 = f32[16,64,512]{2,1,0:T(8,128)S(1)} all-to-all(f32[16,64,512]{2,1,0:T(8,128)} %combine.1), channel_id=1, replica_groups=mesh['dp'=8,'tm'=16] {'tm'}, dimensions={0} | all-to-all | bytes 4194304 | tf_op jit(solution)/shard_map/all_to_all | solution.py:461
  276.2 1.3 copy.25
  (3 shorter events, 0.0 us)
Async XLA Ops:
  7.2 39.6 %all-to-all-start = ((f32[16,64,512]{2,1,0:T(8,128)}), f32[16,64,512]{2,1,0:T(8,128)S(1)}, u32[]{:S(2)}, u32[]{:S(2)}) async-start(f32[16,64,512]{2,1,0:T(8,128)} %bitcast.10), calls=%async_computation | async-start | bytes 4194304 | tf_op jit(solution)/shard_map/all_to_all | solution.py:334
  15.1 128.8 %all-gather.2.cloned.1.call-start = ((), (), s32[]{:S(2)}) async-start(), calls=%async_computation.6 | async-start | bytes 4718592 | tf_op jit(solution)/shard_map/all_gather | solution.py:374
  46.8 1.3 copy-start
  46.8 13.7 %collective-permute-start = (f32[2,128,512]{2,1,0:T(8,128)S(1)}, f32[2,128,512]{2,1,0:T(8,128)S(1)}, u32[]{:S(2)}, u32[]{:S(2)}) collective-permute-start(f32[2,128,512]{2,1,0:T(8,128)S(1)} %bitcast_select_fusion), channel_id=1, source_target_pairs={{0,15},{1,14},{2,13},{3,12},{4,11},{5,10},{6,9},{7,8},{8,0},{9,7},... | collective-permute-start | bytes 1572872 | tf_op jit(solution)/shard_map/ppermute | solution.py:350
  60.5 0.8 copy-start.2
  139.6 37.7 %all-to-all-start.2 = ((f32[16,2,4,16,256]{4,3,2,1,0:T(8,128)}), f32[16,2,4,16,256]{4,3,2,1,0:T(8,128)S(1)}, u32[]{:S(2)}, u32[]{:S(2)}) async-start(f32[16,2,4,16,256]{4,3,2,1,0:T(8,128)} %expand_rest.1), calls=%async_computation.2 | async-start | bytes 4194304 | tf_op jit(solution)/shard_map/all_to_all | solution.py:377
  143.3 132.9 %reduce-scatter.2.cloned.1.call-start = ((), (), s32[]{:S(2)}) async-start(), calls=%async_computation.7 | async-start | bytes 9437184 | tf_op jit(solution)/shard_map/reduce_scatter | solution.py:444
  177.3 1.4 copy-start.1
Sparse Core Ops, SparseCore 0:
  61.5 31.5 all-gather.1
  185.4 48.8 reduce-scatter.1

commit v4 on v3

--- a/solution.py
+++ b/solution.py
@@ -94,7 +94,7 @@
             out_ref[a, 1, t, row, :] = im
         return carry
 
-    lax.fori_loop(0, RADIX * groups, step, 0)
+    lax.fori_loop(0, RADIX * groups, step, 0, unroll=True)
 
 
 def expand_kernel(blocks, x_ref, out_ref):
@@ -153,7 +153,7 @@
             out_ref[n, rows, :] = times[n] + gain * x_ref[n, rows, :]
         return carry
 
-    lax.fori_loop(0, RADIX * groups, step, 0)
+    lax.fori_loop(0, RADIX * groups, step, 0, unroll=True)
 
 
 dot = functools.partial(jnp.dot, preferred_element_type=jnp.float32)
@@ -181,12 +181,12 @@
     return (ar + cr, ai + ci), (br + di, bi - dr), (ar - cr, ai - ci), (br - di, bi + dr)
 
 
-def forward_parts(z_ref, tables, s_ref, keep):
+def forward_parts(z_ref, blocks, tables, s_ref, keep):
     inner, lanes = s_ref.shape[2:]
     for t in range(RADIX):
-        re = z_ref[:, 0, t].reshape(inner, lanes)
-        im = z_ref[:, 1, t].reshape(inner, lanes) * keep
-        cosine, sine = product(tables, t, jnp.concatenate([re, im], 1))
+        re = [z_ref[:, c, 0, t].reshape(inner, LANES) for c in blocks]
+        im = [z_ref[:, c, 1, t].reshape(inner, LANES) * keep for c in blocks]
+        cosine, sine = product(tables, t, jnp.concatenate(re + im, 1))
         s_ref[t, 0] = cosine[:, :lanes] + sine[:, lanes:]
         s_ref[t, 1] = cosine[:, lanes:] - sine[:, :lanes]
 
@@ -205,7 +205,7 @@
     tables = refs[:4]
     saved_ref, _, term_ref, s_ref = refs[4:]
     inner = s_ref.shape[2]
-    forward_parts(z_ref, tables, s_ref, 1.0)
+    forward_parts(z_ref, [0], tables, s_ref, 1.0)
 
     def step(index, carry):
         row = rows_at(index * 8)
@@ -223,16 +223,17 @@
     first = pick_ref[1]
     keep = (1 - first).astype(jnp.float32)
     inner, lanes = s_ref.shape[2:]
-    slivers = u_ref.shape[0]
+    slivers, blocks = u_ref.shape[:2]
 
     def inverse_of(tables, slots):
         for t in range(RADIX):
             cosine, sine = product(tables, t, jnp.concatenate([s_ref[t, 0], s_ref[t, 1]], 1))
             values = (cosine[:, :lanes] - sine[:, lanes:], sine[:, :lanes] + cosine[:, lanes:])
             for slot, of in slots:
-                u_ref[:, slot, t] = values[of].reshape(slivers, inner // slivers, lanes)
-
-    forward_parts(z_ref, tables, s_ref, keep)
+                for c in range(blocks):
+                    u_ref[:, c, slot, t] = values[of][:, c * LANES : (c + 1) * LANES].reshape(slivers, inner // slivers, LANES)
+
+    forward_parts(z_ref, range(blocks), tables, s_ref, keep)
 
     def step(index, carry):
         row = rows_at(index * 8)
@@ -255,7 +256,8 @@
     @pl.when(first == 1)
     def _():
         for t in range(RADIX):
-            cosine, sine = product(tables16, t, z_ref[:, 1, t].reshape(inner, lanes))
+            values = jnp.concatenate([z_ref[:, c, 1, t].reshape(inner, LANES) for c in range(blocks)], 1)
+            cosine, sine = product(tables16, t, values)
             s_ref[t, 0] = cosine
             s_ref[t, 1] = -sine
 
@@ -290,7 +292,7 @@
 
 def make_table(residue, inner, points, factor, transposed):
     base_cos, base_sin = base_table(inner, points, transposed)
-    time = jnp.arange(RADIX)[:, None] + RADIX * jnp.arange(inner)[None, :]
+    time = np.arange(RADIX, dtype=np.int32)[:, None] + RADIX * np.arange(inner, dtype=np.int32)[None, :]
     angle = ((time * residue) % points).astype(jnp.float32) * (2.0 * math.pi / points)
     twist_cos, twist_sin = lax.optimization_barrier((jnp.cos(angle) * factor, jnp.sin(angle) * factor))
     at = (slice(None), slice(None), None) if transposed else (slice(None), None, slice(None))
@@ -331,7 +333,6 @@
     rows = sliver // RADIX
     blocks = channels // LANES
     early = blocks // 2
-    raw = lax.all_to_all(grad_out.reshape(SHARDS, sliver, channels), "tm", 0, 0, tiled=True)
 
     part = length // groups
     filt = filter_spectrum[:, :, 0]
@@ -339,37 +340,41 @@
     turned = lax.rev(lax.dynamic_slice_in_dim(give, (groups - 1 - stream) * part, part, 1), (1,))
     plain = lax.dynamic_slice_in_dim(give, stream * part, part, 1)
     sent = jnp.where(column == 8, plain, turned)
+    grad_out, sent, picks, pick = lax.optimization_barrier((grad_out, sent, picks, pick))
+    raw = lax.all_to_all(grad_out.reshape(SHARDS, sliver, channels), "tm", 0, 0, tiled=True)
+    raw, sent = lax.optimization_barrier((raw, sent))
+    swap = [(a, 15 - a) for a in range(8)] + [(8, 0)] + [(a, 16 - a) for a in range(9, 16)]
+    swapped = lax.ppermute(sent, "tm", swap)
+
+    late, _ = lax.optimization_barrier((column, raw))
     table = functools.partial(make_table, inner=inner, points=points, factor=factor)
     known = functools.partial(fixed_table, residue=16, inner=inner, points=points, factor=factor)
-    residue = 2 * column + pick
-    made = [table(residue, transposed=False), table(residue, transposed=True), table(2 * column + 1 - pick, transposed=False)]
-    raw, sent, made = lax.optimization_barrier((raw, sent, made))
+    residue = 2 * late + pick
+    made = [table(residue, transposed=False), table(residue, transposed=True), table(2 * late + 1 - pick, transposed=False)]
+    raw, made = lax.optimization_barrier((raw, made))
     picked_tables = made[0] + known(transposed=False) + made[1] + known(transposed=True)
     other_tables = made[2]
-    swap = [(a, 15 - a) for a in range(8)] + [(8, 0)] + [(a, 16 - a) for a in range(9, 16)]
-    swapped = lax.ppermute(sent, "tm", swap)
-
-    z_shape = (SHARDS, 2, RADIX, rows)
-
-    def expand(picked, first_other, others, name):
+
+    z_tail = (2, RADIX, rows, LANES)
+
+    def expand(raw, picked, first_other, others, name):
         return pl.pallas_call(
             functools.partial(expand_kernel, picked),
             grid=(picked + others,),
             in_specs=[
                 pl.BlockSpec((SHARDS, sliver, LANES), lambda c: (0, 0, jnp.where(c < picked, c, c - picked + first_other)))
             ],
-            out_specs=pl.BlockSpec(z_shape + (LANES,), lambda c: (0, 0, 0, 0, c)),
-            out_shape=jax.ShapeDtypeStruct(z_shape + ((picked + others) * LANES,), f32),
+            out_specs=pl.BlockSpec((SHARDS, None) + z_tail, lambda c: (0, c, 0, 0, 0, 0)),
+            out_shape=jax.ShapeDtypeStruct((SHARDS, picked + others) + z_tail, f32),
             compiler_params=params(),
-            cost_estimate=pl.CostEstimate(
-                flops=300 * sliver * LANES * (picked + others), bytes_accessed=(picked + others) * 2**21, transcendentals=0
-            ),
+            cost_estimate=pl.CostEstimate(flops=2**20, bytes_accessed=2**20, transcendentals=0),
             interpret=interpret,
             name=name,
         )(raw)
 
-    first_part = expand(blocks, 0, early, "expand")
-    rest = expand(0, early, blocks - early, "expand_rest")
+    first_part = expand(raw, blocks, 0, early, "expand")
+    swapped, first_part, raw = lax.optimization_barrier((swapped, first_part, raw))
+    rest = expand(raw, 0, early, blocks - early, "expand_rest")
     swapped, first_part, rest = lax.optimization_barrier((swapped, first_part, rest))
     mirror = lax.all_gather(swapped, "dp", axis=1, tiled=True)
     z_first = lax.all_to_all(first_part, "tm", 0, 0, tiled=True)
@@ -380,32 +385,33 @@
         return pl.BlockSpec(values.shape, lambda c, s: (0,) * values.ndim, pipeline_mode=pl.Buffered(1))
 
     def z_spec(shift):
-        return pl.BlockSpec(z_shape + (LANES,), lambda c, s: (0, 0, 0, 0, c + shift))
+        return pl.BlockSpec((SHARDS, 1) + z_tail, lambda c, s: (0, c + shift, 0, 0, 0, 0))
 
     saved_shape = (2, None, None, None, length, LANES)
     term_shape = jax.ShapeDtypeStruct((2, 2, 1, length, channels), f32)
     term_block = (2, None, None, length, LANES)
     scratch = [pltpu.VMEM((RADIX, 2, inner, LANES), f32)]
 
+    wide = min(2 * LANES, channels)
     terms, inverted = pl.pallas_call(
         spectrum_kernel,
         grid_spec=pltpu.PrefetchScalarGridSpec(
             num_scalar_prefetch=1,
-            grid=(channels // LANES,),
-            in_specs=[z_spec(0)]
+            grid=(channels // wide,),
+            in_specs=[pl.BlockSpec((SHARDS, wide // LANES) + z_tail, lambda c, s: (0, c, 0, 0, 0, 0))]
             + [fixed(table) for table in picked_tables]
             + [
-                pl.BlockSpec(saved_shape, lambda c, s: (0, 0, s[0], 0, 0, c)),
-                pl.BlockSpec((2, None, None, length, LANES), lambda c, s: (0, s[0], 0, 0, c)),
-                pl.BlockSpec((2, length, LANES), lambda c, s: (0, 0, c)),
+                pl.BlockSpec(saved_shape[:-1] + (wide,), lambda c, s: (0, 0, s[0], 0, 0, c)),
+                pl.BlockSpec((2, None, None, length, wide), lambda c, s: (0, s[0], 0, 0, c)),
+                pl.BlockSpec((2, length, wide), lambda c, s: (0, 0, c)),
             ],
             out_specs=[
-                pl.BlockSpec(term_block, lambda c, s: (0, s[0], 0, 0, c)),
-                pl.BlockSpec(z_shape + (LANES,), lambda c, s: (0, 0, 0, 0, c)),
+                pl.BlockSpec(term_block[:-1] + (wide,), lambda c, s: (0, s[0], 0, 0, c)),
+                pl.BlockSpec((SHARDS, wide // LANES) + z_tail, lambda c, s: (0, c, 0, 0, 0, 0)),
             ],
-            scratch_shapes=scratch,
+            scratch_shapes=[pltpu.VMEM((RADIX, 2, inner, wide), f32)],
         ),
-        out_shape=[term_shape, jax.ShapeDtypeStruct((SHARDS, 2, RADIX, rows, channels), f32)],
+        out_shape=[term_shape, jax.ShapeDtypeStruct((SHARDS, blocks) + z_tail, f32)],
         compiler_params=params(),
         cost_estimate=pl.CostEstimate(flops=10**10, bytes_accessed=12 * length * channels * 4, transcendentals=0),
         interpret=interpret,
@@ -447,7 +453,7 @@
         combine_kernel,
         grid=(channels // LANES,),
         in_specs=[
-            pl.BlockSpec((SHARDS, 2, RADIX, rows, LANES), lambda c: (0, 0, 0, 0, c)),
+            pl.BlockSpec((SHARDS, None) + z_tail, lambda c: (0, c, 0, 0, 0, 0)),
             pl.BlockSpec((SHARDS, sliver, LANES), lambda c: (0, 0, c)),
             pl.BlockSpec((1, LANES), lambda c: (0, c)),
         ],

time: 285 us -> 278 us (0.975)
  blocking collectives: 164 us -> 194 us
  waiting for transfers between devices: 27.1 us -> 1.93 us
  starting transfers between devices: 12.6 us -> 4.97 us
  Pallas kernels: 55.1 us -> 51.3 us
    all_to_all x0 -> x1, blocking collectives: none -> 36.4 us  [on_device(): lax.all_to_all(grad_out.reshape(SHARDS, sliver, channels), 'tm', 0, 0, ti...]
    all_to_all x1 -> x0, waiting for transfers between devices: 24.3 us -> none  [on_device(): lax.all_to_all(grad_out.reshape(SHARDS, sliver, channels), 'tm', 0, 0, ti...]
    all_to_all x1 -> x0, starting transfers between devices: 7.97 us -> none  [on_device(): lax.all_to_all(grad_out.reshape(SHARDS, sliver, channels), 'tm', 0, 0, ti...]
    pallas_call x1, Pallas kernels: 26.8 us -> 23.7 us  [on_device(): pl.pallas_call(spectrum_kernel, grid_spec=pltpu.PrefetchScalarGridSpec(nu...]
  transfers between devices with their start and end apart: 5 -> 4, of which waited for: 2 -> 1; matrix products, arithmetic and copies ran while one was open for 3% -> 2% of each run, Pallas kernels for 17% -> 15%
where the time goes in v4:
time: 278 us
  blocking collectives  194 us (70%)
  Pallas kernels  51.3 us (18%)
  between operations  14.1 us (5%)
  other arithmetic  7.05 us (3%)
  starting transfers between devices  4.97 us (2%)
  local copies, waits for them, and re-layouts  4.18 us (2%)
    all_to_all x1, blocking collectives, on_device(): z_first = lax.all_to_all(first_part, 'tm', 0, 0, tiled=True)  76.6 us
    all_to_all x1, blocking collectives, on_device(): landed = lax.all_to_all(inverted, 'tm', 0, 0, tiled=True)  52.6 us
    all_to_all x1, blocking collectives, on_device(): lax.all_to_all(grad_out.reshape(SHARDS, sliver, channels), 'tm', 0, 0, ti...  36.4 us
    all_to_all x1, blocking collectives, on_device(): back = lax.all_to_all(combined, 'tm', 0, 0, tiled=True)  28.5 us
    pallas_call x1, Pallas kernels, on_device(): pl.pallas_call(spectrum_kernel, grid_spec=pltpu.PrefetchScalarGridSpec(nu...  23.7 us
    pallas_call x2, Pallas kernels, second(): pl.pallas_call(other_kernel, grid_spec=pltpu.PrefetchScalarGridSpec(num_s...  13.1 us
    pallas_call x2, Pallas kernels, expand(): pl.pallas_call(functools.partial(expand_kernel, picked), grid=(picked + o...  9.27 us
  transfers between devices with their start and end apart: 4, of which 1 were waited for; matrix products, arithmetic and copies ran while one was open for 2% of the time, Pallas kernels for 15%

profile of v4, /device:TPU:0, one launch (start us, length us, event | category | flops | bytes accessed | tf_op | source)
XLA Modules:
  0.0 277.7 jit_solution(14834013331247051638)
XLA Ops:
  7.2 0.0 copy-start.4
  7.2 0.0 copy-start.1
  7.2 0.0 all-gather.2.cloned.1.call-start
  7.3 1.2 dynamic-slice_bitcast_fusion
  8.5 0.3 rev.3
  8.8 0.6 pad_add_fusion.pick_ref
  9.4 1.9 bitcast_select_fusion
  11.3 0.0 copy-done.1
  11.3 36.4 %all_to_all.25.x_ref = f32[16,64,512]{2,1,0:T(8,128)} all-to-all(f32[16,64,512]{2,1,0:T(8,128)S(1)} %bitcast.10), channel_id=1, replica_groups=mesh['dp'=8,'tm'=16] {'tm'}, dimensions={0} | all-to-all | bytes 4194304 | tf_op jit(solution)/shard_map/all_to_all | solution.py:344
  47.7 1.2 collective-permute-start
  48.9 0.0 copy-done.4
  48.9 0.1 sine_multiply_fusion
  49.0 0.0 copy-done.2
  49.0 4.5 %fusion.5 = (bf16[4,256,256]{2,1,0:T(8,128)(2,1)}, bf16[4,256,256]{2,1,0:T(8,128)(2,1)}, bf16[4,256,256]{2,1,0:T(8,128)(2,1)}, bf16[4,256,256]{2,1,0:T(8,128)(2,...) fusion(f32[4,256,256]{2,1,0:T(8,128)} %constant.132.clone, ...), kind=kLoop, calls=%fused_computation.17 | loop fusion | flops 11010048 | bytes 10502144 | tf_op jit(solution)/shard_map/convert_element_type | solution.py:282
  53.4 6.5 %expand.1 = f32[16,6,2,4,16,128]{5,4,3,2,1,0:T(8,128)} custom-call(f32[16,64,512]{2,1,0:T(8,128)} %all_to_all.25.x_ref), custom_call_target="tpu_custom_call" | custom-call | flops 1048576 | bytes 1048576 | tf_op jit(solution)/shard_map/expand/pallas_call | solution.py:361
  59.9 1.9 collective-permute-done
  61.8 2.8 %expand_rest.1 = f32[16,2,2,4,16,128]{5,4,3,2,1,0:T(8,128)} custom-call(f32[16,64,512]{2,1,0:T(8,128)} %all_to_all.25.x_ref), custom_call_target="tpu_custom_call" | custom-call | flops 1048576 | bytes 1048576 | tf_op jit(solution)/shard_map/expand_rest/pallas_call | solution.py:361
  64.6 0.0 all-gather.2.cloned.1.call-update
  64.6 76.6 %all_to_all.26.z_ref = f32[16,6,2,4,16,128]{5,4,3,2,1,0:T(8,128)} all-to-all(f32[16,6,2,4,16,128]{5,4,3,2,1,0:T(8,128)} %expand.1), channel_id=1, replica_groups=mesh['dp'=8,'tm'=16] {'tm'}, dimensions={0} | all-to-all | bytes 12582912 | tf_op jit(solution)/shard_map/all_to_all | solution.py:380
  141.2 3.7 %all-to-all-start.2 = ((f32[16,2,2,4,16,128]{5,4,3,2,1,0:T(8,128)}), f32[16,2,2,4,16,128]{5,4,3,2,1,0:T(8,128)S(1)}, u32[]{:S(2)}, u32[]{:S(2)}) async-start(f32[16,2,2,4,16,128]{5,4,3,2,1,0:T(8,128)} %expand_rest.1), calls=%async_computation.2 | async-start | bytes 4194304 | tf_op jit(solution)/shard_map/all_to_all | solution.py:382
  144.9 0.0 reduce-scatter.2.cloned.1.call-start
  144.9 0.0 all-gather.2.cloned.1.call-done.refs_18_
  145.0 23.7 %spectrum.1 = (f32[2,2,1,1024,512]{4,3,2,1,0:T(8,128)}, f32[16,4,2,4,16,128]{5,4,3,2,1,0:T(8,128)}) custom-call(s32[2]{0:T(128)} %pad_add_fusion.pick_ref, f32[16,6,2,4,16,128]{5,4,3,2,1,0:T(8,128)} %all_to_all.26.z_ref, bf16[4,256,256]{2,1,0:T(8,128)(2,1)} %get-tuple-element.67.refs_0_, bf16[4,256,256]{2,1,0:T(8,128)(2,1)} %get-tuple-element.68.refs_1_, ...), custom_call_target="tpu_custom_call" | custom-call | flops 10000000000 | bytes 25165824 | tf_op jit(solution)/shard_map/spectrum/pallas_call | solution.py:396
  168.7 6.6 %other.1.refs_5_ = f32[2,2,1,1024,512]{4,3,2,1,0:T(8,128)} custom-call(s32[2]{0:T(128)} %pad_add_fusion.pick_ref, f32[16,6,2,4,16,128]{5,4,3,2,1,0:T(8,128)} %all_to_all.26.z_ref, bf16[4,256,256]{2,1,0:T(8,128)(2,1)} %get-tuple-element.63.refs_0_, bf16[4,256,256]{2,1,0:T(8,128)(2,1)} %get-tuple-element.64.refs_1_, ...), custom_call_target="tpu_custom_call", output_to_operand_aliasing={{}: (7, {})} | custom-call | flops 4000000000 | bytes 6291456 | tf_op jit(solution)/shard_map/other/pallas_call | solution.py:422
  175.2 0.0 all-to-all-done.2.z_ref
  175.2 1.3 copy-done
  176.5 6.6 %other_rest.1 = f32[2,2,1,1024,512]{4,3,2,1,0:T(8,128)} custom-call(s32[2]{0:T(128)} %pad_add_fusion.pick_ref, f32[16,2,2,4,16,128]{5,4,3,2,1,0:T(8,128)} %copy-done, bf16[4,256,256]{2,1,0:T(8,128)(2,1)} %get-tuple-element.63.refs_0_, bf16[4,256,256]{2,1,0:T(8,128)(2,1)} %get-tuple-element.64.refs_1_, ...), custom_call_target="tpu_custom_call", output_to_operand_aliasing={{}: (7, {})} | custom-call | flops 4000000000 | bytes 6291456 | tf_op jit(solution)/shard_map/other_rest/pallas_call | solution.py:422
  183.1 0.0 reduce-scatter.2.cloned.1.call-update
  183.1 52.6 %all_to_all.27.u_ref = f32[16,4,2,4,16,128]{5,4,3,2,1,0:T(8,128)} all-to-all(f32[16,4,2,4,16,128]{5,4,3,2,1,0:T(8,128)} %get-tuple-element.82), channel_id=1, replica_groups=mesh['dp'=8,'tm'=16] {'tm'}, dimensions={0} | all-to-all | bytes 8388608 | tf_op jit(solution)/shard_map/all_to_all | solution.py:451
  235.8 5.2 %combine.1 = f32[16,64,512]{2,1,0:T(8,128)} custom-call(f32[16,4,2,4,16,128]{5,4,3,2,1,0:T(8,128)} %all_to_all.27.u_ref, f32[16,64,512]{2,1,0:T(8,128)} %all_to_all.25.x_ref, f32[1,512]{1,0:T(1,128)} %bitcast.11), custom_call_target="tpu_custom_call" | custom-call | flops 13107200 | bytes 8388608 | tf_op jit(solution)/shard_map/combine/pallas_call | solution.py:452
  240.9 28.5 %all_to_all.28 = f32[16,64,512]{2,1,0:T(8,128)S(1)} all-to-all(f32[16,64,512]{2,1,0:T(8,128)} %combine.1), channel_id=1, replica_groups=mesh['dp'=8,'tm'=16] {'tm'}, dimensions={0} | all-to-all | bytes 4194304 | tf_op jit(solution)/shard_map/all_to_all | solution.py:467
  269.5 1.3 copy.28
  (5 shorter events, 0.0 us)
Async XLA Ops:
  7.2 41.7 %copy-start.4 = (s32[4,256]{1,0:T(4,128)S(1)}, s32[4,256]{1,0:T(4,128)}, u32[]{:S(2)}) copy-start(s32[4,256]{1,0:T(4,128)} %constant.131.clone) | copy-start | bytes 12292
  7.2 4.1 %copy-start.1 = (f32[1,1024,512]{2,1,0:T(8,128)S(1)}, f32[1,1024,512]{2,1,0:T(8,128)}, u32[]{:S(2)}) copy-start(f32[1,1024,512]{2,1,0:T(8,128)} %param.21) | copy-start | bytes 6291460
  7.2 137.8 %all-gather.2.cloned.1.call-start = ((), (), s32[]{:S(2)}) async-start(), calls=%async_computation.6 | async-start | bytes 4718592 | tf_op jit(solution)/shard_map/all_gather | solution.py:379
  11.3 37.7 %copy-start.2 = (f32[4,256,256]{2,1,0:T(8,128)S(1)}, f32[4,256,256]{2,1,0:T(8,128)}, u32[]{:S(2)}) copy-start(f32[4,256,256]{2,1,0:T(8,128)} %constant.135.clone) | copy-start | bytes 3145732
  47.7 14.1 %collective-permute-start = (f32[2,128,512]{2,1,0:T(8,128)}, f32[2,128,512]{2,1,0:T(8,128)S(1)}, u32[]{:S(2)}, u32[]{:S(2)}) collective-permute-start(f32[2,128,512]{2,1,0:T(8,128)} %bitcast_select_fusion), channel_id=1, source_target_pairs={{0,15},{1,14},{2,13},{3,12},{4,11},{5,10},{6,9},{7,8},{8,0},{9,7},... | collective-permute-start | bytes 1572872 | tf_op jit(solution)/shard_map/ppermute | solution.py:347
  61.8 2.8 %copy-start.3 = (f32[2,128,512]{2,1,0:T(8,128)}, f32[2,128,512]{2,1,0:T(8,128)S(1)}, u32[]{:S(2)}) copy-start(f32[2,128,512]{2,1,0:T(8,128)S(1)} %collective-permute-done) | copy-start | bytes 1572868
  141.2 34.1 %all-to-all-start.2 = ((f32[16,2,2,4,16,128]{5,4,3,2,1,0:T(8,128)}), f32[16,2,2,4,16,128]{5,4,3,2,1,0:T(8,128)S(1)}, u32[]{:S(2)}, u32[]{:S(2)}) async-start(f32[16,2,2,4,16,128]{5,4,3,2,1,0:T(8,128)} %expand_rest.1), calls=%async_computation.2 | async-start | bytes 4194304 | tf_op jit(solution)/shard_map/all_to_all | solution.py:382
  144.9 124.6 %reduce-scatter.2.cloned.1.call-start = ((), (), s32[]{:S(2)}) async-start(), calls=%async_computation.7 | async-start | bytes 9437184 | tf_op jit(solution)/shard_map/reduce_scatter | solution.py:450
  175.2 1.3 copy-start
Sparse Core Ops, SparseCore 0:
  64.7 31.1 all-gather.1
  183.2 48.9 reduce-scatter.1

commit v5 on v4

--- a/solution.py
+++ b/solution.py
@@ -181,14 +181,23 @@
     return (ar + cr, ai + ci), (br + di, bi - dr), (ar - cr, ai - ci), (br - di, bi + dr)
 
 
-def forward_parts(z_ref, blocks, tables, s_ref, keep):
+def forward_parts(z_ref, blocks, tables, s_ref):
     inner, lanes = s_ref.shape[2:]
     for t in range(RADIX):
         re = [z_ref[:, c, 0, t].reshape(inner, LANES) for c in blocks]
-        im = [z_ref[:, c, 1, t].reshape(inner, LANES) * keep for c in blocks]
+        im = [z_ref[:, c, 1, t].reshape(inner, LANES) for c in blocks]
         cosine, sine = product(tables, t, jnp.concatenate(re + im, 1))
         s_ref[t, 0] = cosine[:, :lanes] + sine[:, lanes:]
         s_ref[t, 1] = cosine[:, lanes:] - sine[:, :lanes]
+
+
+def forward_real(z_ref, slot, blocks, tables, s_ref):
+    inner = s_ref.shape[2]
+    for t in range(RADIX):
+        values = jnp.concatenate([z_ref[:, c, slot, t].reshape(inner, LANES) for c in blocks], 1)
+        cosine, sine = product(tables, t, values)
+        s_ref[t, 0] = cosine
+        s_ref[t, 1] = -sine
 
 
 def rows_at(index):
@@ -205,7 +214,7 @@
     tables = refs[:4]
     saved_ref, _, term_ref, s_ref = refs[4:]
     inner = s_ref.shape[2]
-    forward_parts(z_ref, [0], tables, s_ref, 1.0)
+    forward_parts(z_ref, [0], tables, s_ref)
 
     def step(index, carry):
         row = rows_at(index * 8)
@@ -221,60 +230,57 @@
     tables, tables16, back, back16 = refs[0:4], refs[4:8], refs[8:12], refs[12:16]
     saved_ref, filt_ref, mirror_ref, term_ref, u_ref, s_ref = refs[16:]
     first = pick_ref[1]
-    keep = (1 - first).astype(jnp.float32)
     inner, lanes = s_ref.shape[2:]
     slivers, blocks = u_ref.shape[:2]
 
-    def inverse_of(tables, slots):
+    def put(values, slot, t):
+        for c in range(blocks):
+            u_ref[:, c, slot, t] = values[:, c * LANES : (c + 1) * LANES].reshape(slivers, inner // slivers, LANES)
+
+    def inverse_real(tables, slot):
         for t in range(RADIX):
-            cosine, sine = product(tables, t, jnp.concatenate([s_ref[t, 0], s_ref[t, 1]], 1))
-            values = (cosine[:, :lanes] - sine[:, lanes:], sine[:, :lanes] + cosine[:, lanes:])
-            for slot, of in slots:
-                for c in range(blocks):
-                    u_ref[:, c, slot, t] = values[of][:, c * LANES : (c + 1) * LANES].reshape(slivers, inner // slivers, LANES)
-
-    forward_parts(z_ref, range(blocks), tables, s_ref, keep)
-
-    def step(index, carry):
-        row = rows_at(index * 8)
-        parts = [(s_ref[t, 0, row], s_ref[t, 1, row]) for t in range(RADIX)]
-        back_parts = []
-        for q, (re, im) in enumerate(turn(parts, 1)):
-            at = rows_at(q * inner + index * 8)
-            write_terms(s_ref, row, at, saved_ref, term_ref, re, im)
-            a = filt_ref[0, at] + keep * mirror_ref[0, at]
-            b = keep * mirror_ref[1, at] - filt_ref[1, at]
-            back_parts.append((a * re - b * im, a * im + b * re))
-        for t, (re, im) in enumerate(turn(back_parts, -1)):
-            s_ref[t, 0, row] = re
-            s_ref[t, 1, row] = im
-        return carry
-
-    lax.fori_loop(0, inner // 8, step, 0, unroll=2)
-    inverse_of(back, ((0, 0), (1, 1)))
-
-    @pl.when(first == 1)
-    def _():
-        for t in range(RADIX):
-            values = jnp.concatenate([z_ref[:, c, 1, t].reshape(inner, LANES) for c in range(blocks)], 1)
-            cosine, sine = product(tables16, t, values)
-            s_ref[t, 0] = cosine
-            s_ref[t, 1] = -sine
-
-        def step16(index, carry):
+            total = None
+            for k, part in ((0, s_ref[t, 0]), (2, -s_ref[t, 1])):
+                high, low = halves_of(part)
+                found = dot(tables[k][t], high) + (dot(tables[k][t], low) + dot(tables[k + 1][t], high))
+                total = found if total is None else total + found
+            put(total, slot, t)
+
+    def middle(weigh, with_terms):
+        def step(index, carry):
             row = rows_at(index * 8)
-            parts = []
-            for q, (re, im) in enumerate(turn([(s_ref[t, 0, row], s_ref[t, 1, row]) for t in range(RADIX)], 1)):
+            parts = [(s_ref[t, 0, row], s_ref[t, 1, row]) for t in range(RADIX)]
+            back_parts = []
+            for q, (re, im) in enumerate(turn(parts, 1)):
                 at = rows_at(q * inner + index * 8)
-                a, b = mirror_ref[0, at], mirror_ref[1, at]
-                parts.append((a * re + b * im, a * im - b * re))
-            for t, (re, im) in enumerate(turn(parts, -1)):
+                if with_terms:
+                    write_terms(s_ref, row, at, saved_ref, term_ref, re, im)
+                a, b = weigh(at)
+                back_parts.append((a * re - b * im, a * im + b * re))
+            for t, (re, im) in enumerate(turn(back_parts, -1)):
                 s_ref[t, 0, row] = re
                 s_ref[t, 1, row] = im
             return carry
 
-        lax.fori_loop(0, inner // 8, step16, 0, unroll=2)
-        inverse_of(back16, ((1, 0),))
+        lax.fori_loop(0, inner // 8, step, 0, unroll=2)
+
+    @pl.when(first == 0)
+    def _():
+        forward_parts(z_ref, range(blocks), tables, s_ref)
+        middle(lambda at: (filt_ref[0, at] + mirror_ref[0, at], mirror_ref[1, at] - filt_ref[1, at]), True)
+        for t in range(RADIX):
+            cosine, sine = product(back, t, jnp.concatenate([s_ref[t, 0], s_ref[t, 1]], 1))
+            put(cosine[:, :lanes] - sine[:, lanes:], 0, t)
+            put(sine[:, :lanes] + cosine[:, lanes:], 1, t)
+
+    @pl.when(first == 1)
+    def _():
+        forward_real(z_ref, 0, range(blocks), tables, s_ref)
+        middle(lambda at: (filt_ref[0, at], -filt_ref[1, at]), True)
+        inverse_real(back, 0)
+        forward_real(z_ref, 1, range(blocks), tables16, s_ref)
+        middle(lambda at: (mirror_ref[0, at], mirror_ref[1, at]), False)
+        inverse_real(back16, 1)
 
 
 def split_table(values):
@@ -337,9 +343,7 @@
     part = length // groups
     filt = filter_spectrum[:, :, 0]
     give = lax.dynamic_index_in_dim(filt, (column < 8).astype(jnp.int32), 1, False)
-    turned = lax.rev(lax.dynamic_slice_in_dim(give, (groups - 1 - stream) * part, part, 1), (1,))
-    plain = lax.dynamic_slice_in_dim(give, stream * part, part, 1)
-    sent = jnp.where(column == 8, plain, turned)
+    sent = lax.rev(lax.dynamic_slice_in_dim(give, (groups - 1 - stream) * part, part, 1), (1,))
     grad_out, sent, picks, pick = lax.optimization_barrier((grad_out, sent, picks, pick))
     raw = lax.all_to_all(grad_out.reshape(SHARDS, sliver, channels), "tm", 0, 0, tiled=True)
     raw, sent = lax.optimization_barrier((raw, sent))
@@ -373,7 +377,6 @@
         )(raw)
 
     first_part = expand(raw, blocks, 0, early, "expand")
-    swapped, first_part, raw = lax.optimization_barrier((swapped, first_part, raw))
     rest = expand(raw, 0, early, blocks - early, "expand_rest")
     swapped, first_part, rest = lax.optimization_barrier((swapped, first_part, rest))
     mirror = lax.all_gather(swapped, "dp", axis=1, tiled=True)

time: 278 us -> 276 us (level)
  Pallas kernels: 51.3 us -> 47.3 us
  blocking collectives: 194 us -> 197 us
    pallas_call x1, Pallas kernels: 23.7 us -> 19.9 us  [on_device(): pl.pallas_call(spectrum_kernel, grid_spec=pltpu.PrefetchScalarGridSpec(nu...]
where the time goes in v5:
time: 276 us
  blocking collectives  197 us (71%)
  Pallas kernels  47.3 us (17%)
  between operations  14.1 us (5%)
  local copies, waits for them, and re-layouts  6.55 us (2%)
  starting transfers between devices  5.09 us (2%)
  other arithmetic  4.79 us (2%)
    all_to_all x1, blocking collectives, on_device(): z_first = lax.all_to_all(first_part, 'tm', 0, 0, tiled=True)  78 us
    all_to_all x1, blocking collectives, on_device(): landed = lax.all_to_all(inverted, 'tm', 0, 0, tiled=True)  53.5 us
    all_to_all x1, blocking collectives, on_device(): lax.all_to_all(grad_out.reshape(SHARDS, sliver, channels), 'tm', 0, 0, ti...  36.5 us
    all_to_all x1, blocking collectives, on_device(): back = lax.all_to_all(combined, 'tm', 0, 0, tiled=True)  28.8 us
    pallas_call x1, Pallas kernels, on_device(): pl.pallas_call(spectrum_kernel, grid_spec=pltpu.PrefetchScalarGridSpec(nu...  19.9 us
    pallas_call x2, Pallas kernels, second(): pl.pallas_call(other_kernel, grid_spec=pltpu.PrefetchScalarGridSpec(num_s...  13.1 us
    pallas_call x2, Pallas kernels, expand(): pl.pallas_call(functools.partial(expand_kernel, picked), grid=(picked + o...  9.08 us
  transfers between devices with their start and end apart: 4, of which 1 were waited for; matrix products, arithmetic and copies ran while one was open for 2% of the time, Pallas kernels for 15%

profile of v5, /device:TPU:0, one launch (start us, length us, event | category | flops | bytes accessed | tf_op | source)
XLA Modules:
  0.0 275.7 jit_solution(3107307808255467508)
XLA Ops:
  7.2 0.0 copy-start.4
  7.2 0.0 copy-start.1
  7.2 0.0 copy-start.2
  7.2 0.0 all-gather.2.cloned.1.call-start
  7.3 1.2 dynamic-slice_bitcast_fusion
  8.5 2.6 rev.3
  11.2 0.6 pad_add_fusion.pick_ref
  11.7 36.5 %all_to_all.25.x_ref = f32[16,64,512]{2,1,0:T(8,128)} all-to-all(f32[16,64,512]{2,1,0:T(8,128)} %bitcast.8), channel_id=1, replica_groups=mesh['dp'=8,'tm'=16] {'tm'}, dimensions={0} | all-to-all | bytes 4194304 | tf_op jit(solution)/shard_map/all_to_all | solution.py:348
  48.2 1.2 collective-permute-start
  49.4 0.0 copy-done.4
  49.4 0.1 sine_multiply_fusion
  49.4 0.0 copy-done.1
  49.5 0.0 copy-done.2
  49.5 4.1 %fusion.5 = (bf16[4,256,256]{2,1,0:T(8,128)(2,1)}, bf16[4,256,256]{2,1,0:T(8,128)(2,1)}, bf16[4,256,256]{2,1,0:T(8,128)(2,1)}, bf16[4,256,256]{2,1,0:T(8,128)(2,...) fusion(f32[4,256,256]{2,1,0:T(8,128)} %constant.108.clone, ...), kind=kLoop, calls=%fused_computation.17 | loop fusion | flops 11010048 | bytes 10502144 | tf_op jit(solution)/shard_map/convert_element_type | solution.py:288
  53.6 2.6 expand_rest.1
  56.3 6.4 %expand.1 = f32[16,6,2,4,16,128]{5,4,3,2,1,0:T(8,128)} custom-call(f32[16,64,512]{2,1,0:T(8,128)} %all_to_all.25.x_ref), custom_call_target="tpu_custom_call" | custom-call | flops 1048576 | bytes 1048576 | tf_op jit(solution)/shard_map/expand/pallas_call | solution.py:365
  62.7 0.0 collective-permute-done
  62.7 0.0 all-gather.2.cloned.1.call-update
  62.7 78.0 %all_to_all.26.z_ref = f32[16,6,2,4,16,128]{5,4,3,2,1,0:T(8,128)} all-to-all(f32[16,6,2,4,16,128]{5,4,3,2,1,0:T(8,128)} %expand.1), channel_id=1, replica_groups=mesh['dp'=8,'tm'=16] {'tm'}, dimensions={0} | all-to-all | bytes 12582912 | tf_op jit(solution)/shard_map/all_to_all | solution.py:383
  140.7 3.8 %all-to-all-start.2 = ((f32[16,2,2,4,16,128]{5,4,3,2,1,0:T(8,128)}), f32[16,2,2,4,16,128]{5,4,3,2,1,0:T(8,128)S(1)}, u32[]{:S(2)}, u32[]{:S(2)}) async-start(f32[16,2,2,4,16,128]{5,4,3,2,1,0:T(8,128)} %expand_rest.1), calls=%async_computation.2 | async-start | bytes 4194304 | tf_op jit(solution)/shard_map/all_to_all | solution.py:385
  144.6 0.0 reduce-scatter.2.cloned.1.call-start
  144.6 0.0 all-gather.2.cloned.1.call-done.refs_18_
  144.6 19.9 %spectrum.1 = (f32[2,2,1,1024,512]{4,3,2,1,0:T(8,128)}, f32[16,4,2,4,16,128]{5,4,3,2,1,0:T(8,128)}) custom-call(s32[2]{0:T(128)} %pad_add_fusion.pick_ref, f32[16,6,2,4,16,128]{5,4,3,2,1,0:T(8,128)} %all_to_all.26.z_ref, bf16[4,256,256]{2,1,0:T(8,128)(2,1)} %get-tuple-element.61.refs_0_, bf16[4,256,256]{2,1,0:T(8,128)(2,1)} %get-tuple-element.62.refs_1_, ...), custom_call_target="tpu_custom_call" | custom-call | flops 10000000000 | bytes 25165824 | tf_op jit(solution)/shard_map/spectrum/pallas_call | solution.py:399
  164.6 6.6 %other.1.refs_5_ = f32[2,2,1,1024,512]{4,3,2,1,0:T(8,128)} custom-call(s32[2]{0:T(128)} %pad_add_fusion.pick_ref, f32[16,6,2,4,16,128]{5,4,3,2,1,0:T(8,128)} %all_to_all.26.z_ref, bf16[4,256,256]{2,1,0:T(8,128)(2,1)} %get-tuple-element.57.refs_0_, bf16[4,256,256]{2,1,0:T(8,128)(2,1)} %get-tuple-element.58.refs_1_, ...), custom_call_target="tpu_custom_call", output_to_operand_aliasing={{}: (7, {})} | custom-call | flops 4000000000 | bytes 6291456 | tf_op jit(solution)/shard_map/other/pallas_call | solution.py:425
  171.1 1.0 all-to-all-done.2.z_ref
  172.2 1.3 copy-done
  173.5 6.6 %other_rest.1 = f32[2,2,1,1024,512]{4,3,2,1,0:T(8,128)} custom-call(s32[2]{0:T(128)} %pad_add_fusion.pick_ref, f32[16,2,2,4,16,128]{5,4,3,2,1,0:T(8,128)} %copy-done, bf16[4,256,256]{2,1,0:T(8,128)(2,1)} %get-tuple-element.57.refs_0_, bf16[4,256,256]{2,1,0:T(8,128)(2,1)} %get-tuple-element.58.refs_1_, ...), custom_call_target="tpu_custom_call", output_to_operand_aliasing={{}: (7, {})} | custom-call | flops 4000000000 | bytes 6291456 | tf_op jit(solution)/shard_map/other_rest/pallas_call | solution.py:425
  180.0 0.0 reduce-scatter.2.cloned.1.call-update
  180.1 53.5 %all_to_all.27.u_ref = f32[16,4,2,4,16,128]{5,4,3,2,1,0:T(8,128)} all-to-all(f32[16,4,2,4,16,128]{5,4,3,2,1,0:T(8,128)} %get-tuple-element.76), channel_id=1, replica_groups=mesh['dp'=8,'tm'=16] {'tm'}, dimensions={0} | all-to-all | bytes 8388608 | tf_op jit(solution)/shard_map/all_to_all | solution.py:454
  233.6 5.2 %combine.1 = f32[16,64,512]{2,1,0:T(8,128)} custom-call(f32[16,4,2,4,16,128]{5,4,3,2,1,0:T(8,128)} %all_to_all.27.u_ref, f32[16,64,512]{2,1,0:T(8,128)} %all_to_all.25.x_ref, f32[1,512]{1,0:T(1,128)} %bitcast.9), custom_call_target="tpu_custom_call" | custom-call | flops 13107200 | bytes 8388608 | tf_op jit(solution)/shard_map/combine/pallas_call | solution.py:455
  238.8 28.8 %all_to_all.28 = f32[16,64,512]{2,1,0:T(8,128)S(1)} all-to-all(f32[16,64,512]{2,1,0:T(8,128)} %combine.1), channel_id=1, replica_groups=mesh['dp'=8,'tm'=16] {'tm'}, dimensions={0} | all-to-all | bytes 4194304 | tf_op jit(solution)/shard_map/all_to_all | solution.py:470
  267.5 1.3 copy.28
  (4 shorter events, 0.0 us)
Async XLA Ops:
  7.2 42.2 %copy-start.4 = (s32[4,256]{1,0:T(4,128)S(1)}, s32[4,256]{1,0:T(4,128)}, u32[]{:S(2)}) copy-start(s32[4,256]{1,0:T(4,128)} %constant.107.clone) | copy-start | bytes 12292
  7.2 42.3 %copy-start.1 = (f32[4,256,256]{2,1,0:T(8,128)S(1)}, f32[4,256,256]{2,1,0:T(8,128)}, u32[]{:S(2)}) copy-start(f32[4,256,256]{2,1,0:T(8,128)} %constant.111.clone) | copy-start | bytes 3145732
  7.2 42.3 %copy-start.2 = (f32[4,256,256]{2,1,0:T(8,128)S(1)}, f32[4,256,256]{2,1,0:T(8,128)}, u32[]{:S(2)}) copy-start(f32[4,256,256]{2,1,0:T(8,128)} %constant.110.clone) | copy-start | bytes 3145732
  7.2 137.4 %all-gather.2.cloned.1.call-start = ((), (), s32[]{:S(2)}) async-start(), calls=%async_computation.6 | async-start | bytes 4718592 | tf_op jit(solution)/shard_map/all_gather | solution.py:382
  11.2 38.3 %copy-start.3 = (f32[4,256,256]{2,1,0:T(8,128)S(1)}, f32[4,256,256]{2,1,0:T(8,128)}, u32[]{:S(2)}) copy-start(f32[4,256,256]{2,1,0:T(8,128)} %constant.109.clone) | copy-start | bytes 3145732
  48.2 14.5 %collective-permute-start = (f32[2,128,512]{2,1,0:T(8,128)}, f32[2,128,512]{2,1,0:T(8,128)}, u32[]{:S(2)}, u32[]{:S(2)}) collective-permute-start(f32[2,128,512]{2,1,0:T(8,128)} %rev.3), channel_id=1, source_target_pairs={{0,15},{1,14},{2,13},{3,12},{4,11},{5,10},{6,9},{7,8},{8,0},{9,7},... | collective-permute-start | bytes 1572872 | tf_op jit(solution)/shard_map/ppermute | solution.py:351
  140.7 31.5 %all-to-all-start.2 = ((f32[16,2,2,4,16,128]{5,4,3,2,1,0:T(8,128)}), f32[16,2,2,4,16,128]{5,4,3,2,1,0:T(8,128)S(1)}, u32[]{:S(2)}, u32[]{:S(2)}) async-start(f32[16,2,2,4,16,128]{5,4,3,2,1,0:T(8,128)} %expand_rest.1), calls=%async_computation.2 | async-start | bytes 4194304 | tf_op jit(solution)/shard_map/all_to_all | solution.py:385
  144.6 123.0 %reduce-scatter.2.cloned.1.call-start = ((), (), s32[]{:S(2)}) async-start(), calls=%async_computation.7 | async-start | bytes 9437184 | tf_op jit(solution)/shard_map/reduce_scatter | solution.py:453
  172.2 1.3 copy-start
Sparse Core Ops, SparseCore 0:
  62.9 32.1 all-gather.1
  180.2 51.0 reduce-scatter.1

commit v6 on v5

--- a/solution.py
+++ b/solution.py
@@ -107,35 +107,44 @@
         expand_block(x_ref, out_ref, True)
 
 
+def turned(value, numerator, denominator):
+    re, im = value
+    c, s = cos_at(numerator, denominator), sin_at(numerator, denominator)
+    if abs(c - s) < 1e-12:
+        return (re - im) * c, (re + im) * c
+    return re * c - im * s, re * s + im * c
+
+
+def inverse_four(y):
+    (r0, i0), (r1, i1), (r2, i2), (r3, i3) = y
+    ar, ai, br, bi = r0 + r2, i0 + i2, r0 - r2, i0 - i2
+    cr, ci, dr, di = r1 + r3, i1 + i3, r1 - r3, i1 - i3
+    return [(ar + cr, ai + ci), (br - di, bi + dr), (ar - cr, ai - ci), (br + di, bi - dr)]
+
+
+def conjugate(value):
+    return value[0], -value[1]
+
+
 def times_of(v0, v16, even, odd):
-    out = [None] * 16
-    ce, se, co, so = {}, {}, {}, {}
-    for n in range(0, 5):
-        c_even = weighted([(1.0, v0), (1.0 if n % 2 == 0 else -1.0, v16)] + [(cos_at(n * d, 16), even[d][0]) for d in (2, 4, 6)])
-        c_odd = weighted([(cos_at(n * d, 16), even[d][0]) for d in (1, 3, 5, 7)])
-        s_even = weighted([(sin_at(n * d, 16), even[d][1]) for d in (2, 4, 6)])
-        s_odd = weighted([(sin_at(n * d, 16), even[d][1]) for d in (1, 3, 5, 7)])
-        if n == 4:
-            ce[4], se[4] = c_even, s_odd
-        elif n == 0:
-            ce[0], ce[8] = c_even + c_odd, c_even - c_odd
-        else:
-            ce[n], ce[8 - n] = c_even + c_odd, c_even - c_odd
-            se[n], se[8 - n] = s_odd + s_even, s_odd - s_even
-    re_sum = {q: odd[q][0] + odd[16 - q][0] for q in (1, 3, 5, 7)}
-    re_diff = {q: odd[q][0] - odd[16 - q][0] for q in (1, 3, 5, 7)}
-    im_sum = {q: odd[q][1] + odd[16 - q][1] for q in (1, 3, 5, 7)}
-    im_diff = {q: odd[q][1] - odd[16 - q][1] for q in (1, 3, 5, 7)}
-    for n in range(0, 9):
-        re_of, im_of = (re_sum, im_diff) if n % 2 == 0 else (re_diff, im_sum)
-        co[n] = weighted([(cos_at(n * q, 32), re_of[q]) for q in (1, 3, 5, 7)])
-        so[n] = weighted([(sin_at(n * q, 32), im_of[q]) for q in (1, 3, 5, 7)])
-    out[0] = ce[0] + co[0]
-    out[8] = ce[8] + so[8]
-    for n in range(1, 8):
-        out[n] = (ce[n] - se[n]) + (co[n] + so[n])
-        out[16 - n] = (ce[n] + se[n]) + (so[n] - co[n])
-    return out
+    a, b = v0 + v16, v0 - v16
+    f0 = [a + even[4][0], b - even[4][1], a - even[4][0], b + even[4][1]]
+    plus = even[2][0] + even[6][0], even[2][1] - even[6][1]
+    minus = even[2][0] - even[6][0], even[2][1] + even[6][1]
+    corner = turned(minus, 1, 8)
+    f1 = [plus[0], corner[0], -plus[1], -corner[1]]
+    e0 = [f0[n] + f1[n] for n in range(4)] + [f0[n] - f1[n] for n in range(4)]
+    y = inverse_four([even[1], even[5], conjugate(even[7]), conjugate(even[3])])
+    c = [y[0]] + [turned(y[m], m, 16) for m in (1, 2, 3)]
+    e1 = [c[m][0] for m in range(4)] + [-c[m][1] for m in range(4)]
+    y = [conjugate(odd[q]) for q in (1, 5, 9, 13)] + [odd[q] for q in (15, 11, 7, 3)]
+    low = inverse_four([y[k] for k in (0, 2, 4, 6)])
+    high = inverse_four([y[k] for k in (1, 3, 5, 7)])
+    high = [high[0], turned(high[1], 1, 8), (-high[2][1], high[2][0]), turned(high[3], 3, 8)]
+    y = [(p[0] + q[0], p[1] + q[1]) for p, q in zip(low, high)] + [(p[0] - q[0], p[1] - q[1]) for p, q in zip(low, high)]
+    c = [y[0]] + [turned(y[m], m, 32) for m in range(1, 8)]
+    out = [e0[n] + e1[n] + c[n][0] for n in range(8)]
+    return out + [e0[n] - e1[n] - c[n][1] for n in range(8)]
 
 
 def combine_kernel(u_ref, x_ref, gain_ref, out_ref):
@@ -344,18 +353,14 @@
     filt = filter_spectrum[:, :, 0]
     give = lax.dynamic_index_in_dim(filt, (column < 8).astype(jnp.int32), 1, False)
     sent = lax.rev(lax.dynamic_slice_in_dim(give, (groups - 1 - stream) * part, part, 1), (1,))
-    grad_out, sent, picks, pick = lax.optimization_barrier((grad_out, sent, picks, pick))
     raw = lax.all_to_all(grad_out.reshape(SHARDS, sliver, channels), "tm", 0, 0, tiled=True)
-    raw, sent = lax.optimization_barrier((raw, sent))
+    table = functools.partial(make_table, inner=inner, points=points, factor=factor)
+    known = functools.partial(fixed_table, residue=16, inner=inner, points=points, factor=factor)
+    residue = 2 * column + pick
+    made = [table(residue, transposed=False), table(residue, transposed=True), table(2 * column + 1 - pick, transposed=False)]
+    raw, sent, made = lax.optimization_barrier((raw, sent, made))
     swap = [(a, 15 - a) for a in range(8)] + [(8, 0)] + [(a, 16 - a) for a in range(9, 16)]
     swapped = lax.ppermute(sent, "tm", swap)
-
-    late, _ = lax.optimization_barrier((column, raw))
-    table = functools.partial(make_table, inner=inner, points=points, factor=factor)
-    known = functools.partial(fixed_table, residue=16, inner=inner, points=points, factor=factor)
-    residue = 2 * late + pick
-    made = [table(residue, transposed=False), table(residue, transposed=True), table(2 * late + 1 - pick, transposed=False)]
-    raw, made = lax.optimization_barrier((raw, made))
     picked_tables = made[0] + known(transposed=False) + made[1] + known(transposed=True)
     other_tables = made[2]
 

time: 276 us -> 281 us (1.018)
  blocking collectives: 197 us -> 165 us
  waiting for transfers between devices: 1.11 us -> 30.7 us
  starting transfers between devices: 5.09 us -> 12.6 us
    all_to_all x1 -> x0, blocking collectives: 36.5 us -> none  [on_device(): lax.all_to_all(grad_out.reshape(SHARDS, sliver, channels), 'tm', 0, 0, ti...]
    all_to_all x0 -> x1, waiting for transfers between devices: none -> 25.4 us  [on_device(): lax.all_to_all(grad_out.reshape(SHARDS, sliver, channels), 'tm', 0, 0, ti...]
    all_to_all x0 -> x1, starting transfers between devices: none -> 7.97 us  [on_device(): lax.all_to_all(grad_out.reshape(SHARDS, sliver, channels), 'tm', 0, 0, ti...]
    ppermute x1, waiting for transfers between devices: 0.01 us -> 3.31 us  [on_device(): swapped = lax.ppermute(sent, 'tm', swap)]
  transfers between devices with their start and end apart: 4 -> 5, of which waited for: 1 -> 3; matrix products, arithmetic and copies ran while one was open for 2% -> 2% of each run, Pallas kernels for 15% -> 15%
where the time goes in v6:
time: 281 us; the launch traced here: 280 us
  blocking collectives  165 us (59%)
  Pallas kernels  47.2 us (17%)
  waiting for transfers between devices  30.7 us (11%)
  between operations  14.1 us (5%)
  starting transfers between devices  12.6 us (4%)
  other arithmetic  5.38 us (2%)
  local copies, waits for them, and re-layouts  5.37 us (2%)
    all_to_all x1, blocking collectives, on_device(): z_first = lax.all_to_all(first_part, 'tm', 0, 0, tiled=True)  78.2 us
    all_to_all x1, blocking collectives, on_device(): landed = lax.all_to_all(inverted, 'tm', 0, 0, tiled=True)  55.4 us
    all_to_all x1, blocking collectives, on_device(): back = lax.all_to_all(combined, 'tm', 0, 0, tiled=True)  30.9 us
    all_to_all x1, waiting for transfers between devices, on_device(): lax.all_to_all(grad_out.reshape(SHARDS, sliver, channels), 'tm', 0, 0, ti...  25.4 us
    pallas_call x1, Pallas kernels, on_device(): pl.pallas_call(spectrum_kernel, grid_spec=pltpu.PrefetchScalarGridSpec(nu...  19.8 us
    pallas_call x2, Pallas kernels, second(): pl.pallas_call(other_kernel, grid_spec=pltpu.PrefetchScalarGridSpec(num_s...  13.1 us
    pallas_call x2, Pallas kernels, expand(): pl.pallas_call(functools.partial(expand_kernel, picked), grid=(picked + o...  9.09 us
    all_to_all x1, starting transfers between devices, on_device(): lax.all_to_all(grad_out.reshape(SHARDS, sliver, channels), 'tm', 0, 0, ti...  7.97 us
  transfers between devices with their start and end apart: 5, of which 3 were waited for; matrix products, arithmetic and copies ran while one was open for 2% of the time, Pallas kernels for 15%

profile of v6, /device:TPU:0, one launch (start us, length us, event | category | flops | bytes accessed | tf_op | source)
XLA Modules:
  0.0 280.0 jit_solution(10793645077615782366)
XLA Ops:
  7.2 0.0 copy-start.3
  7.2 8.0 %all-to-all-start = ((f32[16,64,512]{2,1,0:T(8,128)}), f32[16,64,512]{2,1,0:T(8,128)S(1)}, u32[]{:S(2)}, u32[]{:S(2)}) async-start(f32[16,64,512]{2,1,0:T(8,128)} %bitcast.8), calls=%async_computation | async-start | bytes 4194304 | tf_op jit(solution)/shard_map/all_to_all | solution.py:356
  15.2 0.0 all-gather.2.cloned.1.call-start
  15.2 0.0 copy-done.3
  15.2 0.1 sine_multiply_fusion
  15.3 1.1 dynamic-slice_bitcast_fusion
  16.5 0.3 rev.3
  16.7 4.6 %fusion.5 = (bf16[4,256,256]{2,1,0:T(8,128)(2,1)}, bf16[4,256,256]{2,1,0:T(8,128)(2,1)}, bf16[4,256,256]{2,1,0:T(8,128)(2,1)}, bf16[4,256,256]{2,1,0:T(8,128)(2,...) fusion(f32[4,256,256]{2,1,0:T(8,128)} %constant.108.clone, ...), kind=kLoop, calls=%fused_computation.17 | loop fusion | flops 11010048 | bytes 10502144 | tf_op jit(solution)/shard_map/convert_element_type | solution.py:297
  21.4 25.4 %all-to-all-done.x_ref = f32[16,64,512]{2,1,0:T(8,128)S(1)} async-done(((f32[16,64,512]{2,1,0:T(8,128)}), f32[16,64,512]{2,1,0:T(8,128)S(1)}, u32[]{:S(2)}, u32[]{:S(2)}) %all-to-all-start) | async-done | bytes 2097184 | tf_op jit(solution)/shard_map/all_to_all | solution.py:356
  46.8 0.0 copy-start
  46.8 0.8 collective-permute-start
  47.7 0.5 copy-done
  48.1 2.6 expand_rest.1
  50.8 6.4 %expand.1 = f32[16,6,2,4,16,128]{5,4,3,2,1,0:T(8,128)} custom-call(f32[16,64,512]{2,1,0:T(8,128)} %copy-done), custom_call_target="tpu_custom_call" | custom-call | flops 1048576 | bytes 1048576 | tf_op jit(solution)/shard_map/expand/pallas_call | solution.py:370
  57.2 3.3 %collective-permute-done = f32[2,128,512]{2,1,0:T(8,128)S(1)} collective-permute-done((f32[2,128,512]{2,1,0:T(8,128)S(1)}, f32[2,128,512]{2,1,0:T(8,128)S(1)}, u32[]{:S(2)}, u32[]{:S(2)}) %collective-permute-start) | collective-permute-done | bytes 524320 | tf_op jit(solution)/shard_map/ppermute | solution.py:363
  60.5 0.8 copy-done.2
  61.3 0.0 all-gather.2.cloned.1.call-update
  61.4 78.2 %all_to_all.25.z_ref = f32[16,6,2,4,16,128]{5,4,3,2,1,0:T(8,128)} all-to-all(f32[16,6,2,4,16,128]{5,4,3,2,1,0:T(8,128)} %expand.1), channel_id=1, replica_groups=mesh['dp'=8,'tm'=16] {'tm'}, dimensions={0} | all-to-all | bytes 12582912 | tf_op jit(solution)/shard_map/all_to_all | solution.py:388
  139.6 3.7 %all-to-all-start.2 = ((f32[16,2,2,4,16,128]{5,4,3,2,1,0:T(8,128)}), f32[16,2,2,4,16,128]{5,4,3,2,1,0:T(8,128)S(1)}, u32[]{:S(2)}, u32[]{:S(2)}) async-start(f32[16,2,2,4,16,128]{5,4,3,2,1,0:T(8,128)} %expand_rest.1), calls=%async_computation.2 | async-start | bytes 4194304 | tf_op jit(solution)/shard_map/all_to_all | solution.py:390
  143.3 0.0 reduce-scatter.2.cloned.1.call-start
  143.4 0.7 pad_add_fusion.pick_ref
  144.0 0.0 all-gather.2.cloned.1.call-done.refs_18_
  144.0 19.8 %spectrum.1 = (f32[2,2,1,1024,512]{4,3,2,1,0:T(8,128)}, f32[16,4,2,4,16,128]{5,4,3,2,1,0:T(8,128)}) custom-call(s32[2]{0:T(128)} %pad_add_fusion.pick_ref, f32[16,6,2,4,16,128]{5,4,3,2,1,0:T(8,128)} %all_to_all.25.z_ref, bf16[4,256,256]{2,1,0:T(8,128)(2,1)} %get-tuple-element.49.refs_0_, bf16[4,256,256]{2,1,0:T(8,128)(2,1)} %get-tuple-element.50.refs_1_, ...), custom_call_target="tpu_custom_call" | custom-call | flops 10000000000 | bytes 25165824 | tf_op jit(solution)/shard_map/spectrum/pallas_call | solution.py:404
  163.9 6.6 %other.1.refs_5_ = f32[2,2,1,1024,512]{4,3,2,1,0:T(8,128)} custom-call(s32[2]{0:T(128)} %pad_add_fusion.pick_ref, f32[16,6,2,4,16,128]{5,4,3,2,1,0:T(8,128)} %all_to_all.25.z_ref, bf16[4,256,256]{2,1,0:T(8,128)(2,1)} %get-tuple-element.45.refs_0_, bf16[4,256,256]{2,1,0:T(8,128)(2,1)} %get-tuple-element.46.refs_1_, ...), custom_call_target="tpu_custom_call", output_to_operand_aliasing={{}: (7, {})} | custom-call | flops 4000000000 | bytes 6291456 | tf_op jit(solution)/shard_map/other/pallas_call | solution.py:430
  170.4 1.9 all-to-all-done.2.z_ref
  172.4 1.4 copy-done.1
  173.7 6.6 %other_rest.1 = f32[2,2,1,1024,512]{4,3,2,1,0:T(8,128)} custom-call(s32[2]{0:T(128)} %pad_add_fusion.pick_ref, f32[16,2,2,4,16,128]{5,4,3,2,1,0:T(8,128)} %copy-done.1, bf16[4,256,256]{2,1,0:T(8,128)(2,1)} %get-tuple-element.45.refs_0_, bf16[4,256,256]{2,1,0:T(8,128)(2,1)} %get-tuple-element.46.refs_1_, ...), custom_call_target="tpu_custom_call", output_to_operand_aliasing={{}: (7, {})} | custom-call | flops 4000000000 | bytes 6291456 | tf_op jit(solution)/shard_map/other_rest/pallas_call | solution.py:430
  180.3 0.0 reduce-scatter.2.cloned.1.call-update
  180.3 55.4 %all_to_all.26.u_ref = f32[16,4,2,4,16,128]{5,4,3,2,1,0:T(8,128)} all-to-all(f32[16,4,2,4,16,128]{5,4,3,2,1,0:T(8,128)} %get-tuple-element.64), channel_id=1, replica_groups=mesh['dp'=8,'tm'=16] {'tm'}, dimensions={0} | all-to-all | bytes 8388608 | tf_op jit(solution)/shard_map/all_to_all | solution.py:459
  235.8 5.2 %combine.1 = f32[16,64,512]{2,1,0:T(8,128)} custom-call(f32[16,4,2,4,16,128]{5,4,3,2,1,0:T(8,128)} %all_to_all.26.u_ref, f32[16,64,512]{2,1,0:T(8,128)} %copy-done, f32[1,512]{1,0:T(1,128)} %bitcast.9), custom_call_target="tpu_custom_call" | custom-call | flops 13107200 | bytes 8388608 | tf_op jit(solution)/shard_map/combine/pallas_call | solution.py:460
  240.9 30.9 %all_to_all.27 = f32[16,64,512]{2,1,0:T(8,128)S(1)} all-to-all(f32[16,64,512]{2,1,0:T(8,128)} %combine.1), channel_id=1, replica_groups=mesh['dp'=8,'tm'=16] {'tm'}, dimensions={0} | all-to-all | bytes 4194304 | tf_op jit(solution)/shard_map/all_to_all | solution.py:475
  271.8 1.3 copy.28
  (3 shorter events, 0.0 us)
Async XLA Ops:
  7.2 8.1 %copy-start.3 = (s32[4,256]{1,0:T(4,128)S(1)}, s32[4,256]{1,0:T(4,128)}, u32[]{:S(2)}) copy-start(s32[4,256]{1,0:T(4,128)} %constant.107.clone) | copy-start | bytes 12292
  7.2 39.6 %all-to-all-start = ((f32[16,64,512]{2,1,0:T(8,128)}), f32[16,64,512]{2,1,0:T(8,128)S(1)}, u32[]{:S(2)}, u32[]{:S(2)}) async-start(f32[16,64,512]{2,1,0:T(8,128)} %bitcast.8), calls=%async_computation | async-start | bytes 4194304 | tf_op jit(solution)/shard_map/all_to_all | solution.py:356
  15.2 128.9 %all-gather.2.cloned.1.call-start = ((), (), s32[]{:S(2)}) async-start(), calls=%async_computation.6 | async-start | bytes 4718592 | tf_op jit(solution)/shard_map/all_gather | solution.py:387
  46.8 1.3 copy-start
  46.8 13.7 %collective-permute-start = (f32[2,128,512]{2,1,0:T(8,128)S(1)}, f32[2,128,512]{2,1,0:T(8,128)S(1)}, u32[]{:S(2)}, u32[]{:S(2)}) collective-permute-start(f32[2,128,512]{2,1,0:T(8,128)S(1)} %rev.3), channel_id=1, source_target_pairs={{0,15},{1,14},{2,13},{3,12},{4,11},{5,10},{6,9},{7,8},{8,0},{9,7},... | collective-permute-start | bytes 1572872 | tf_op jit(solution)/shard_map/ppermute | solution.py:363
  60.5 0.8 copy-start.2
  139.6 32.8 %all-to-all-start.2 = ((f32[16,2,2,4,16,128]{5,4,3,2,1,0:T(8,128)}), f32[16,2,2,4,16,128]{5,4,3,2,1,0:T(8,128)S(1)}, u32[]{:S(2)}, u32[]{:S(2)}) async-start(f32[16,2,2,4,16,128]{5,4,3,2,1,0:T(8,128)} %expand_rest.1), calls=%async_computation.2 | async-start | bytes 4194304 | tf_op jit(solution)/shard_map/all_to_all | solution.py:390
  143.3 128.5 %reduce-scatter.2.cloned.1.call-start = ((), (), s32[]{:S(2)}) async-start(), calls=%async_computation.7 | async-start | bytes 9437184 | tf_op jit(solution)/shard_map/reduce_scatter | solution.py:458
  172.4 1.4 copy-start.1
Sparse Core Ops, SparseCore 0:
  61.5 31.5 all-gather.1
  180.5 50.3 reduce-scatter.1

commit v7 on v5

--- a/solution.py
+++ b/solution.py
@@ -340,13 +340,14 @@
     blocks = channels // LANES
     early = blocks // 2
 
+    lead = (column < 8).astype(jnp.int32)
+    grad_out, picks, pick, lead, stream = lax.optimization_barrier((grad_out, picks, pick, lead, stream))
+    raw = lax.all_to_all(grad_out.reshape(SHARDS, sliver, channels), "tm", 0, 0, tiled=True)
+    raw, lead, stream = lax.optimization_barrier((raw, lead, stream))
     part = length // groups
     filt = filter_spectrum[:, :, 0]
-    give = lax.dynamic_index_in_dim(filt, (column < 8).astype(jnp.int32), 1, False)
+    give = lax.dynamic_index_in_dim(filt, lead, 1, False)
     sent = lax.rev(lax.dynamic_slice_in_dim(give, (groups - 1 - stream) * part, part, 1), (1,))
-    grad_out, sent, picks, pick = lax.optimization_barrier((grad_out, sent, picks, pick))
-    raw = lax.all_to_all(grad_out.reshape(SHARDS, sliver, channels), "tm", 0, 0, tiled=True)
-    raw, sent = lax.optimization_barrier((raw, sent))
     swap = [(a, 15 - a) for a in range(8)] + [(8, 0)] + [(a, 16 - a) for a in range(9, 16)]
     swapped = lax.ppermute(sent, "tm", swap)
 

time: 276 us -> 275 us (level)
  no operation moved by 1% of the time
where the time goes in v7:
time: 275 us; the launch traced here: 274 us
  blocking collectives  196 us (71%)
  Pallas kernels  47.3 us (17%)
  between operations  14.1 us (5%)
  starting transfers between devices  5.21 us (2%)
  other arithmetic  4.94 us (2%)
  local copies, waits for them, and re-layouts  4.84 us (2%)
    all_to_all x1, blocking collectives, on_device(): z_first = lax.all_to_all(first_part, 'tm', 0, 0, tiled=True)  78 us
    all_to_all x1, blocking collectives, on_device(): landed = lax.all_to_all(inverted, 'tm', 0, 0, tiled=True)  53.1 us
    all_to_all x1, blocking collectives, on_device(): lax.all_to_all(grad_out.reshape(SHARDS, sliver, channels), 'tm', 0, 0, ti...  36.5 us
    all_to_all x1, blocking collectives, on_device(): back = lax.all_to_all(combined, 'tm', 0, 0, tiled=True)  28.8 us
    pallas_call x1, Pallas kernels, on_device(): pl.pallas_call(spectrum_kernel, grid_spec=pltpu.PrefetchScalarGridSpec(nu...  19.9 us
    pallas_call x2, Pallas kernels, second(): pl.pallas_call(other_kernel, grid_spec=pltpu.PrefetchScalarGridSpec(num_s...  13.1 us
    pallas_call x2, Pallas kernels, expand(): pl.pallas_call(functools.partial(expand_kernel, picked), grid=(picked + o...  9.08 us
  transfers between devices with their start and end apart: 4, of which 1 were waited for; matrix products, arithmetic and copies ran while one was open for 2% of the time, Pallas kernels for 15%

profile of v7, /device:TPU:0, one launch (start us, length us, event | category | flops | bytes accessed | tf_op | source)
XLA Modules:
  0.0 273.9 jit_solution(10387416955317317413)
XLA Ops:
  7.2 0.0 copy-start.4
  7.2 0.0 copy-start.1
  7.2 0.0 copy-start.2
  7.2 0.0 all-gather.2.cloned.1.call-start
  7.3 0.6 pad_add_fusion.pick_ref
  7.8 36.5 %all_to_all.25.x_ref = f32[16,64,512]{2,1,0:T(8,128)} all-to-all(f32[16,64,512]{2,1,0:T(8,128)} %bitcast.8), channel_id=1, replica_groups=mesh['dp'=8,'tm'=16] {'tm'}, dimensions={0} | all-to-all | bytes 4194304 | tf_op jit(solution)/shard_map/all_to_all | solution.py:345
  44.3 1.1 dynamic-slice_bitcast_fusion
  45.4 0.3 rev.3
  45.7 1.2 collective-permute-start
  46.9 0.0 copy-done.4
  46.9 0.1 sine_multiply_fusion
  47.0 0.0 copy-done.1
  47.0 4.3 %fusion.5 = (bf16[4,256,256]{2,1,0:T(8,128)(2,1)}, bf16[4,256,256]{2,1,0:T(8,128)(2,1)}, bf16[4,256,256]{2,1,0:T(8,128)(2,1)}, bf16[4,256,256]{2,1,0:T(8,128)(2,...) fusion(f32[4,256,256]{2,1,0:T(8,128)} %constant.108.clone, ...), kind=kLoop, calls=%fused_computation.17 | loop fusion | flops 11010048 | bytes 10502144 | tf_op jit(solution)/shard_map/convert_element_type | solution.py:288
  51.3 2.6 expand_rest.1
  54.0 6.4 %expand.1 = f32[16,6,2,4,16,128]{5,4,3,2,1,0:T(8,128)} custom-call(f32[16,64,512]{2,1,0:T(8,128)} %all_to_all.25.x_ref), custom_call_target="tpu_custom_call" | custom-call | flops 1048576 | bytes 1048576 | tf_op jit(solution)/shard_map/expand/pallas_call | solution.py:366
  60.4 0.0 collective-permute-done
  60.4 0.8 copy-done.3
  61.2 0.0 all-gather.2.cloned.1.call-update
  61.2 78.0 %all_to_all.26.z_ref = f32[16,6,2,4,16,128]{5,4,3,2,1,0:T(8,128)} all-to-all(f32[16,6,2,4,16,128]{5,4,3,2,1,0:T(8,128)} %expand.1), channel_id=1, replica_groups=mesh['dp'=8,'tm'=16] {'tm'}, dimensions={0} | all-to-all | bytes 12582912 | tf_op jit(solution)/shard_map/all_to_all | solution.py:384
  139.2 3.9 %all-to-all-start.2 = ((f32[16,2,2,4,16,128]{5,4,3,2,1,0:T(8,128)}), f32[16,2,2,4,16,128]{5,4,3,2,1,0:T(8,128)S(1)}, u32[]{:S(2)}, u32[]{:S(2)}) async-start(f32[16,2,2,4,16,128]{5,4,3,2,1,0:T(8,128)} %expand_rest.1), calls=%async_computation.2 | async-start | bytes 4194304 | tf_op jit(solution)/shard_map/all_to_all | solution.py:386
  143.1 0.0 reduce-scatter.2.cloned.1.call-start
  143.2 0.0 all-gather.2.cloned.1.call-done.refs_18_
  143.2 19.9 %spectrum.1 = (f32[2,2,1,1024,512]{4,3,2,1,0:T(8,128)}, f32[16,4,2,4,16,128]{5,4,3,2,1,0:T(8,128)}) custom-call(s32[2]{0:T(128)} %pad_add_fusion.pick_ref, f32[16,6,2,4,16,128]{5,4,3,2,1,0:T(8,128)} %all_to_all.26.z_ref, bf16[4,256,256]{2,1,0:T(8,128)(2,1)} %get-tuple-element.65.refs_0_, bf16[4,256,256]{2,1,0:T(8,128)(2,1)} %get-tuple-element.66.refs_1_, ...), custom_call_target="tpu_custom_call" | custom-call | flops 10000000000 | bytes 25165824 | tf_op jit(solution)/shard_map/spectrum/pallas_call | solution.py:400
  163.1 6.6 %other.1.refs_5_ = f32[2,2,1,1024,512]{4,3,2,1,0:T(8,128)} custom-call(s32[2]{0:T(128)} %pad_add_fusion.pick_ref, f32[16,6,2,4,16,128]{5,4,3,2,1,0:T(8,128)} %all_to_all.26.z_ref, bf16[4,256,256]{2,1,0:T(8,128)(2,1)} %get-tuple-element.61.refs_0_, bf16[4,256,256]{2,1,0:T(8,128)(2,1)} %get-tuple-element.62.refs_1_, ...), custom_call_target="tpu_custom_call", output_to_operand_aliasing={{}: (7, {})} | custom-call | flops 4000000000 | bytes 6291456 | tf_op jit(solution)/shard_map/other/pallas_call | solution.py:426
  169.7 1.1 all-to-all-done.2.z_ref
  170.8 1.3 copy-done
  172.1 6.6 %other_rest.1 = f32[2,2,1,1024,512]{4,3,2,1,0:T(8,128)} custom-call(s32[2]{0:T(128)} %pad_add_fusion.pick_ref, f32[16,2,2,4,16,128]{5,4,3,2,1,0:T(8,128)} %copy-done, bf16[4,256,256]{2,1,0:T(8,128)(2,1)} %get-tuple-element.61.refs_0_, bf16[4,256,256]{2,1,0:T(8,128)(2,1)} %get-tuple-element.62.refs_1_, ...), custom_call_target="tpu_custom_call", output_to_operand_aliasing={{}: (7, {})} | custom-call | flops 4000000000 | bytes 6291456 | tf_op jit(solution)/shard_map/other_rest/pallas_call | solution.py:426
  178.7 0.0 reduce-scatter.2.cloned.1.call-update
  178.7 53.1 %all_to_all.27.u_ref = f32[16,4,2,4,16,128]{5,4,3,2,1,0:T(8,128)} all-to-all(f32[16,4,2,4,16,128]{5,4,3,2,1,0:T(8,128)} %get-tuple-element.80), channel_id=1, replica_groups=mesh['dp'=8,'tm'=16] {'tm'}, dimensions={0} | all-to-all | bytes 8388608 | tf_op jit(solution)/shard_map/all_to_all | solution.py:455
  231.8 5.2 %combine.1 = f32[16,64,512]{2,1,0:T(8,128)} custom-call(f32[16,4,2,4,16,128]{5,4,3,2,1,0:T(8,128)} %all_to_all.27.u_ref, f32[16,64,512]{2,1,0:T(8,128)} %all_to_all.25.x_ref, f32[1,512]{1,0:T(1,128)} %bitcast.9), custom_call_target="tpu_custom_call" | custom-call | flops 13107200 | bytes 8388608 | tf_op jit(solution)/shard_map/combine/pallas_call | solution.py:456
  237.0 28.8 %all_to_all.28 = f32[16,64,512]{2,1,0:T(8,128)S(1)} all-to-all(f32[16,64,512]{2,1,0:T(8,128)} %combine.1), channel_id=1, replica_groups=mesh['dp'=8,'tm'=16] {'tm'}, dimensions={0} | all-to-all | bytes 4194304 | tf_op jit(solution)/shard_map/all_to_all | solution.py:471
  265.8 1.3 copy.28
  (4 shorter events, 0.0 us)
Async XLA Ops:
  7.2 39.7 %copy-start.4 = (s32[4,256]{1,0:T(4,128)S(1)}, s32[4,256]{1,0:T(4,128)}, u32[]{:S(2)}) copy-start(s32[4,256]{1,0:T(4,128)} %constant.107.clone) | copy-start | bytes 12292
  7.2 39.8 %copy-start.1 = (f32[4,256,256]{2,1,0:T(8,128)S(1)}, f32[4,256,256]{2,1,0:T(8,128)}, u32[]{:S(2)}) copy-start(f32[4,256,256]{2,1,0:T(8,128)} %constant.111.clone) | copy-start | bytes 3145732
  7.2 39.8 %copy-start.2 = (f32[4,256,256]{2,1,0:T(8,128)S(1)}, f32[4,256,256]{2,1,0:T(8,128)}, u32[]{:S(2)}) copy-start(f32[4,256,256]{2,1,0:T(8,128)} %constant.110.clone) | copy-start | bytes 3145732
  7.2 136.0 %all-gather.2.cloned.1.call-start = ((), (), s32[]{:S(2)}) async-start(), calls=%async_computation.6 | async-start | bytes 4718592 | tf_op jit(solution)/shard_map/all_gather | solution.py:383
  45.7 14.7 %collective-permute-start = (f32[2,128,512]{2,1,0:T(8,128)S(1)}, f32[2,128,512]{2,1,0:T(8,128)S(1)}, u32[]{:S(2)}, u32[]{:S(2)}) collective-permute-start(f32[2,128,512]{2,1,0:T(8,128)S(1)} %rev.3), channel_id=1, source_target_pairs={{0,15},{1,14},{2,13},{3,12},{4,11},{5,10},{6,9},{7,8},{8,0},{9,7},... | collective-permute-start | bytes 1572872 | tf_op jit(solution)/shard_map/ppermute | solution.py:352
  60.4 0.8 copy-start.3
  139.2 31.5 %all-to-all-start.2 = ((f32[16,2,2,4,16,128]{5,4,3,2,1,0:T(8,128)}), f32[16,2,2,4,16,128]{5,4,3,2,1,0:T(8,128)S(1)}, u32[]{:S(2)}, u32[]{:S(2)}) async-start(f32[16,2,2,4,16,128]{5,4,3,2,1,0:T(8,128)} %expand_rest.1), calls=%async_computation.2 | async-start | bytes 4194304 | tf_op jit(solution)/shard_map/all_to_all | solution.py:386
  143.1 122.6 %reduce-scatter.2.cloned.1.call-start = ((), (), s32[]{:S(2)}) async-start(), calls=%async_computation.7 | async-start | bytes 9437184 | tf_op jit(solution)/shard_map/reduce_scatter | solution.py:454
  170.8 1.3 copy-start
Sparse Core Ops, SparseCore 0:
  61.3 32.1 all-gather.1
  178.8 50.9 reduce-scatter.1

commit v8 on v7

--- a/solution.py
+++ b/solution.py
@@ -355,10 +355,9 @@
     table = functools.partial(make_table, inner=inner, points=points, factor=factor)
     known = functools.partial(fixed_table, residue=16, inner=inner, points=points, factor=factor)
     residue = 2 * late + pick
-    made = [table(residue, transposed=False), table(residue, transposed=True), table(2 * late + 1 - pick, transposed=False)]
+    made = [table(residue, transposed=False), table(residue, transposed=True)]
     raw, made = lax.optimization_barrier((raw, made))
     picked_tables = made[0] + known(transposed=False) + made[1] + known(transposed=True)
-    other_tables = made[2]
 
     z_tail = (2, RADIX, rows, LANES)
 
@@ -384,6 +383,8 @@
     z_first = lax.all_to_all(first_part, "tm", 0, 0, tiled=True)
     z_first, rest = lax.optimization_barrier((z_first, rest))
     z_rest = lax.all_to_all(rest, "tm", 0, 0, tiled=True)
+    later, _ = lax.optimization_barrier((column, z_first))
+    other_tables = table(2 * later + 1 - pick, transposed=False)
 
     def fixed(values):
         return pl.BlockSpec(values.shape, lambda c, s: (0,) * values.ndim, pipeline_mode=pl.Buffered(1))

time: 275 us -> 276 us (level)
    convert_element_type x1 -> x2, other arithmetic: 4.3 us -> 6.45 us  [split_table(): return [high.astype(jnp.bfloat16), (values - high).astype(jnp.bfloat16)]]
  transfers between devices with their start and end apart: 4 -> 4, of which waited for: 1 -> 0; matrix products, arithmetic and copies ran while one was open for 2% -> 2% of each run, Pallas kernels for 15% -> 15%
where the time goes in v8:
time: 276 us; the launch traced here: 275 us
  blocking collectives  196 us (71%)
  Pallas kernels  47.3 us (17%)
  between operations  14.1 us (5%)
  other arithmetic  7.22 us (3%)
  starting transfers between devices  5.21 us (2%)
  local copies, waits for them, and re-layouts  4.84 us (2%)
    all_to_all x1, blocking collectives, on_device(): z_first = lax.all_to_all(first_part, 'tm', 0, 0, tiled=True)  78 us
    all_to_all x1, blocking collectives, on_device(): landed = lax.all_to_all(inverted, 'tm', 0, 0, tiled=True)  53.3 us
    all_to_all x1, blocking collectives, on_device(): lax.all_to_all(grad_out.reshape(SHARDS, sliver, channels), 'tm', 0, 0, ti...  36.5 us
    all_to_all x1, blocking collectives, on_device(): back = lax.all_to_all(combined, 'tm', 0, 0, tiled=True)  28.7 us
    pallas_call x1, Pallas kernels, on_device(): pl.pallas_call(spectrum_kernel, grid_spec=pltpu.PrefetchScalarGridSpec(nu...  19.9 us
    pallas_call x2, Pallas kernels, second(): pl.pallas_call(other_kernel, grid_spec=pltpu.PrefetchScalarGridSpec(num_s...  13.1 us
    pallas_call x2, Pallas kernels, expand(): pl.pallas_call(functools.partial(expand_kernel, picked), grid=(picked + o...  9.07 us
    convert_element_type x2, other arithmetic, split_table(): return [high.astype(jnp.bfloat16), (values - high).astype(jnp.bfloat16)]  6.45 us
  transfers between devices with their start and end apart: 4, of which 0 were waited for; matrix products, arithmetic and copies ran while one was open for 2% of the time, Pallas kernels for 15%

profile of v8, /device:TPU:0, one launch (start us, length us, event | category | flops | bytes accessed | tf_op | source)
XLA Modules:
  0.0 275.2 jit_solution(12176904161345671529)
XLA Ops:
  7.2 0.0 copy-start.4
  7.2 0.0 copy-start.1
  7.2 0.0 copy-start.2
  7.2 0.0 all-gather.2.cloned.1.call-start
  7.3 0.7 pad_add_fusion.pick_ref
  7.9 36.5 %all_to_all.25.x_ref = f32[16,64,512]{2,1,0:T(8,128)} all-to-all(f32[16,64,512]{2,1,0:T(8,128)} %bitcast.8), channel_id=1, replica_groups=mesh['dp'=8,'tm'=16] {'tm'}, dimensions={0} | all-to-all | bytes 4194304 | tf_op jit(solution)/shard_map/all_to_all | solution.py:345
  44.4 1.1 dynamic-slice_bitcast_fusion
  45.5 0.3 rev.3
  45.8 1.2 collective-permute-start
  47.0 0.0 copy-done.4
  47.0 0.1 sine_multiply_fusion.1
  47.1 3.5 %fusion.3 = (bf16[4,256,256]{2,1,0:T(8,128)(2,1)}, bf16[4,256,256]{2,1,0:T(8,128)(2,1)}, bf16[4,256,256]{2,1,0:T(8,128)(2,1)}, bf16[4,256,256]{2,1,0:T(8,128)(2,...) fusion(f32[4,256,256]{2,1,0:T(8,128)} %constant.110.clone, ...), kind=kLoop, calls=%fused_computation.15 | loop fusion | flops 7340032 | bytes 8396800 | tf_op jit(solution)/shard_map/convert_element_type | solution.py:288
  50.6 2.6 expand_rest.1
  53.2 6.4 %expand.1 = f32[16,6,2,4,16,128]{5,4,3,2,1,0:T(8,128)} custom-call(f32[16,64,512]{2,1,0:T(8,128)} %all_to_all.25.x_ref), custom_call_target="tpu_custom_call" | custom-call | flops 1048576 | bytes 1048576 | tf_op jit(solution)/shard_map/expand/pallas_call | solution.py:365
  59.7 0.0 collective-permute-done
  59.7 0.8 copy-done.3
  60.5 0.0 all-gather.2.cloned.1.call-update
  60.5 78.0 %all_to_all.26.z_ref = f32[16,6,2,4,16,128]{5,4,3,2,1,0:T(8,128)} all-to-all(f32[16,6,2,4,16,128]{5,4,3,2,1,0:T(8,128)} %expand.1), channel_id=1, replica_groups=mesh['dp'=8,'tm'=16] {'tm'}, dimensions={0} | all-to-all | bytes 12582912 | tf_op jit(solution)/shard_map/all_to_all | solution.py:383
  138.5 3.9 %all-to-all-start.2 = ((f32[16,2,2,4,16,128]{5,4,3,2,1,0:T(8,128)}), f32[16,2,2,4,16,128]{5,4,3,2,1,0:T(8,128)S(1)}, u32[]{:S(2)}, u32[]{:S(2)}) async-start(f32[16,2,2,4,16,128]{5,4,3,2,1,0:T(8,128)} %expand_rest.1), calls=%async_computation.2 | async-start | bytes 4194304 | tf_op jit(solution)/shard_map/all_to_all | solution.py:385
  142.4 0.0 reduce-scatter.2.cloned.1.call-start
  142.5 0.1 sine_multiply_fusion
  142.5 3.0 %fusion.5 = (bf16[4,256,256]{2,1,0:T(8,128)(2,1)}, bf16[4,256,256]{2,1,0:T(8,128)(2,1)}, bf16[4,256,256]{2,1,0:T(8,128)(2,1)}, bf16[4,256,256]{2,1,0:T(8,128)(2,1)}) fusion(f32[4,256,256]{2,1,0:T(8,128)} %constant.108.clone, f32[4,256,256]{2,1,0:T(8,128)S(1)} %copy-done.1, f32[4,256]{1,0:T(4,128)S(1)} %get-tuple-element.58, f32[4,256]{1,0:T(4,128)S(1)} %get-tuple-element.57), kind=kLoop, calls=%fused_computation.17 | loop fusion | flops 3670016 | bytes 4202496 | tf_op jit(solution)/shard_map/convert_element_type | solution.py:288
  145.5 19.9 %spectrum.1 = (f32[2,2,1,1024,512]{4,3,2,1,0:T(8,128)}, f32[16,4,2,4,16,128]{5,4,3,2,1,0:T(8,128)}) custom-call(s32[2]{0:T(128)} %pad_add_fusion.pick_ref, f32[16,6,2,4,16,128]{5,4,3,2,1,0:T(8,128)} %all_to_all.26.z_ref, bf16[4,256,256]{2,1,0:T(8,128)(2,1)} %get-tuple-element.59.refs_0_, bf16[4,256,256]{2,1,0:T(8,128)(2,1)} %get-tuple-element.60.refs_1_, ...), custom_call_target="tpu_custom_call" | custom-call | flops 10000000000 | bytes 25165824 | tf_op jit(solution)/shard_map/spectrum/pallas_call | solution.py:401
  165.4 6.6 %other.1.refs_5_ = f32[2,2,1,1024,512]{4,3,2,1,0:T(8,128)} custom-call(s32[2]{0:T(128)} %pad_add_fusion.pick_ref, f32[16,6,2,4,16,128]{5,4,3,2,1,0:T(8,128)} %all_to_all.26.z_ref, bf16[4,256,256]{2,1,0:T(8,128)(2,1)} %get-tuple-element.79.refs_0_, bf16[4,256,256]{2,1,0:T(8,128)(2,1)} %get-tuple-element.77.refs_1_, ...), custom_call_target="tpu_custom_call", output_to_operand_aliasing={{}: (7, {})} | custom-call | flops 4000000000 | bytes 6291456 | tf_op jit(solution)/shard_map/other/pallas_call | solution.py:427
  171.9 0.0 all-to-all-done.2.z_ref
  171.9 1.3 copy-done
  173.3 6.6 %other_rest.1 = f32[2,2,1,1024,512]{4,3,2,1,0:T(8,128)} custom-call(s32[2]{0:T(128)} %pad_add_fusion.pick_ref, f32[16,2,2,4,16,128]{5,4,3,2,1,0:T(8,128)} %copy-done, bf16[4,256,256]{2,1,0:T(8,128)(2,1)} %get-tuple-element.79.refs_0_, bf16[4,256,256]{2,1,0:T(8,128)(2,1)} %get-tuple-element.77.refs_1_, ...), custom_call_target="tpu_custom_call", output_to_operand_aliasing={{}: (7, {})} | custom-call | flops 4000000000 | bytes 6291456 | tf_op jit(solution)/shard_map/other_rest/pallas_call | solution.py:427
  179.8 0.0 reduce-scatter.2.cloned.1.call-update
  179.9 53.3 %all_to_all.27.u_ref = f32[16,4,2,4,16,128]{5,4,3,2,1,0:T(8,128)} all-to-all(f32[16,4,2,4,16,128]{5,4,3,2,1,0:T(8,128)} %get-tuple-element.74), channel_id=1, replica_groups=mesh['dp'=8,'tm'=16] {'tm'}, dimensions={0} | all-to-all | bytes 8388608 | tf_op jit(solution)/shard_map/all_to_all | solution.py:456
  233.2 5.2 %combine.1 = f32[16,64,512]{2,1,0:T(8,128)} custom-call(f32[16,4,2,4,16,128]{5,4,3,2,1,0:T(8,128)} %all_to_all.27.u_ref, f32[16,64,512]{2,1,0:T(8,128)} %all_to_all.25.x_ref, f32[1,512]{1,0:T(1,128)} %bitcast.9), custom_call_target="tpu_custom_call" | custom-call | flops 13107200 | bytes 8388608 | tf_op jit(solution)/shard_map/combine/pallas_call | solution.py:457
  238.4 28.7 %all_to_all.28 = f32[16,64,512]{2,1,0:T(8,128)S(1)} all-to-all(f32[16,64,512]{2,1,0:T(8,128)} %combine.1), channel_id=1, replica_groups=mesh['dp'=8,'tm'=16] {'tm'}, dimensions={0} | all-to-all | bytes 4194304 | tf_op jit(solution)/shard_map/all_to_all | solution.py:472
  267.1 1.3 copy.28
  (6 shorter events, 0.0 us)
Async XLA Ops:
  7.2 39.8 %copy-start.4 = (s32[4,256]{1,0:T(4,128)S(1)}, s32[4,256]{1,0:T(4,128)}, u32[]{:S(2)}) copy-start(s32[4,256]{1,0:T(4,128)} %constant.107.clone) | copy-start | bytes 12292
  7.2 39.9 %copy-start.1 = (f32[4,256,256]{2,1,0:T(8,128)S(1)}, f32[4,256,256]{2,1,0:T(8,128)}, u32[]{:S(2)}) copy-start(f32[4,256,256]{2,1,0:T(8,128)} %constant.109.clone) | copy-start | bytes 3145732
  7.2 39.9 %copy-start.2 = (f32[4,256,256]{2,1,0:T(8,128)S(1)}, f32[4,256,256]{2,1,0:T(8,128)}, u32[]{:S(2)}) copy-start(f32[4,256,256]{2,1,0:T(8,128)} %constant.108.clone) | copy-start | bytes 3145732
  7.2 138.3 %all-gather.2.cloned.1.call-start = ((), (), s32[]{:S(2)}) async-start(), calls=%async_computation.6 | async-start | bytes 4718592 | tf_op jit(solution)/shard_map/all_gather | solution.py:382
  45.8 13.9 %collective-permute-start = (f32[2,128,512]{2,1,0:T(8,128)S(1)}, f32[2,128,512]{2,1,0:T(8,128)S(1)}, u32[]{:S(2)}, u32[]{:S(2)}) collective-permute-start(f32[2,128,512]{2,1,0:T(8,128)S(1)} %rev.3), channel_id=1, source_target_pairs={{0,15},{1,14},{2,13},{3,12},{4,11},{5,10},{6,9},{7,8},{8,0},{9,7},... | collective-permute-start | bytes 1572872 | tf_op jit(solution)/shard_map/ppermute | solution.py:352
  59.7 0.8 copy-start.3
  138.5 33.4 %all-to-all-start.2 = ((f32[16,2,2,4,16,128]{5,4,3,2,1,0:T(8,128)}), f32[16,2,2,4,16,128]{5,4,3,2,1,0:T(8,128)S(1)}, u32[]{:S(2)}, u32[]{:S(2)}) async-start(f32[16,2,2,4,16,128]{5,4,3,2,1,0:T(8,128)} %expand_rest.1), calls=%async_computation.2 | async-start | bytes 4194304 | tf_op jit(solution)/shard_map/all_to_all | solution.py:385
  142.4 124.7 %reduce-scatter.2.cloned.1.call-start = ((), (), s32[]{:S(2)}) async-start(), calls=%async_computation.7 | async-start | bytes 9437184 | tf_op jit(solution)/shard_map/reduce_scatter | solution.py:455
  171.9 1.3 copy-start
Sparse Core Ops, SparseCore 0:
  60.7 32.1 all-gather.1
  180.0 52.1 reduce-scatter.1
